TPU v7x, 32 devices: a whole 2x2x4 slice. The times are simulated.
32 devices in a mesh: hst: 4 (over x, core), dev: 8 (over z, y).
Axes of the slice: x: 2, y: 2, z: 4, core: 2. Of those that a mesh axis runs over, the one named last changes fastest.
Arguments:
- features: float32 [524288, 128], P(('hst', 'dev')), may hold values from -6 to 6
- requests: int32 [1024, 256], P(('hst', 'dev')), may hold values from 0 to 16383
- adjacent_one: int32 [135168, 15], P(('hst', 'dev')), may hold values from 0 to 8191, as said below
- adjacent_two: int32 [12288, 10], P(('hst', 'dev')), may hold values from 0 to 4223
- adjacent_three: int32 [2048, 5], P(('hst', 'dev')), may hold values from 0 to 383
- valid_one: int32 [135168, 15], P(('hst', 'dev')), may hold values from 0 to 1, as said below
- valid_two: int32 [12288, 10], P(('hst', 'dev')), may hold values from 0 to 1
- valid_three: int32 [2048, 5], P(('hst', 'dev')), may hold values from 0 to 1
- labels: int32 [2048], P(('hst', 'dev')), may hold values from 0 to 171
- labelled: int32 [2048], P(('hst', 'dev')), may hold values from 0 to 1, as said below
- weights_in: float32 [2, 128, 256], replicated, may hold values from -0.5 to 0.5
- weights_mid: float32 [2, 256, 256], replicated, may hold values from -0.375 to 0.375
- weights_out: float32 [2, 256, 172], replicated, may hold values from -0.375 to 0.375
- biases: float32 [684], replicated, may hold values from -0.6 to 0.6
- moment_one: float32 [684], replicated, may hold values from -0.0007954951 to 0.0007954951
- moment_two: float32 [684], replicated, may hold values from 6.1035155e-07 to 2.4414062e-06
- step_count: int32 [], replicated, may hold values from 2 to 20
- left_in: float32 [2, 128, 128], replicated, as said below
- left_mid: float32 [2, 256, 256], replicated, as said below
- left_out: float32 [2, 256, 256], replicated, as said below
- right_in: float32 [2, 256, 256], replicated, as said below
- right_mid: float32 [2, 256, 256], replicated, as said below
- right_out: float32 [2, 172, 172], replicated, as said below
- invleft_in: float32 [2, 128, 128], replicated, as said below
- invleft_mid: float32 [2, 256, 256], replicated, as said below
- invleft_out: float32 [2, 256, 256], replicated, as said below
- invright_in: float32 [2, 256, 256], replicated, as said below
- invright_mid: float32 [2, 256, 256], replicated, as said below
- invright_out: float32 [2, 172, 172], replicated, as said below
Outputs:
- loss: float32 [], replicated
- new_weights_in: float32 [2, 128, 256], replicated
- new_weights_mid: float32 [2, 256, 256], replicated
- new_weights_out: float32 [2, 256, 172], replicated
- copy_in: bfloat16 [2, 128, 256], replicated
- copy_mid: bfloat16 [2, 256, 256], replicated
- copy_out: bfloat16 [2, 256, 172], replicated
- new_left_in: float32 [2, 128, 128], replicated
- new_left_mid: float32 [2, 256, 256], replicated
- new_left_out: float32 [2, 256, 256], replicated
- new_right_in: float32 [2, 256, 256], replicated
- new_right_mid: float32 [2, 256, 256], replicated
- new_right_out: float32 [2, 172, 172], replicated
- new_biases: float32 [684], replicated
- new_moment_one: float32 [684], replicated
- new_moment_two: float32 [684], replicated
Inputs may be any that keep to these rules, and one draw needn't show every extreme that they name: `adjacent_one`: every one of a device's 8192 pulled slots is named by some entry of its rows. `valid_one`: valid shares differ from device to device. The first seed of every device is labelled. `left_in`: a positive multiple of the identity in each of the two matrices. `left_mid`: a positive multiple of the identity in each of the two matrices. `left_out`: a positive multiple of the identity in each of the two matrices. `right_in`: a positive multiple of the identity in each of the two matrices. `right_mid`: a positive multiple of the identity in each of the two matrices. `right_out`: a positive multiple of the identity in each of the two matrices. `invleft_in`: symmetric. `invleft_mid`: symmetric. `invleft_out`: symmetric. `invright_in`: symmetric. `invright_mid`: symmetric. `invright_out`: symmetric.
All inputs are finite; a program needn't handle non-finite values.
Results may differ from a plain program's by a relative error of at most 0.0094.
Values may be sent and summed in bfloat16 or wider, within the bound.
No kernel may reach another device: no remote copies, remote signals or barrier semaphores. Data moves between devices by JAX's collectives and lax.ppermute only.
A program may use at most 128 MiB of HBM per device.

v0:
```python
import functools

import jax
import jax.numpy as jnp
from jax import lax
from jax.experimental import pallas as pl
from jax.experimental.pallas import tpu as pltpu
from jax.sharding import PartitionSpec as P

LANES = 128
SPAN = 256
PARTS = 2
COUNTS = jnp.float8_e4m3fn
BIG = 52 << 20
AXES = ("chip", "core", "dev")
PEERS = ("chip", "dev")

smem = pl.BlockSpec(memory_space=pltpu.SMEM)
vmem = pl.BlockSpec(memory_space=pltpu.VMEM)
anywhere = pl.BlockSpec(memory_space=pltpu.HBM)


def up(value, unit):
    return -(-value // unit) * unit


def call(kernel, name, out_shape, in_specs, out_specs, scratch, cost, room):
    return pl.pallas_call(
        kernel,
        name=name,
        out_shape=out_shape,
        in_specs=in_specs,
        out_specs=out_specs,
        scratch_shapes=scratch,
        compiler_params=pltpu.CompilerParams(vmem_limit_bytes=room),
        cost_estimate=pl.CostEstimate(
            flops=0, transcendentals=0, bytes_accessed=int(cost * 3.6e6)
        ),
    )


def dot(left, right):
    return jnp.dot(left, right, preferred_element_type=jnp.float32)


def dot_rows(left, right):
    return lax.dot_general(
        left, right, (((0,), (0,)), ((), ())), preferred_element_type=jnp.float32
    )


def dot_cols(left, right):
    return lax.dot_general(
        left, right, (((1,), (1,)), ((), ())), preferred_element_type=jnp.float32
    )


def halves(value):
    high = value.astype(jnp.bfloat16)
    return high, (value - high.astype(jnp.float32)).astype(jnp.bfloat16)


def grown(value, rows, columns):
    short = columns - value.shape[1]
    if short:
        value = jnp.concatenate([value, jnp.zeros((value.shape[0], short), value.dtype)], axis=1)
    short = rows - value.shape[0]
    if short:
        value = jnp.concatenate([value, jnp.zeros((short, columns), value.dtype)], axis=0)
    return value


def clipped_counts(valid):
    return jnp.maximum(jnp.sum(valid.astype(jnp.float32), axis=1, keepdims=True), 1.0)


def copy_rows(names, base, size, source, target):
    for u in range(size):
        target[u : u + 1, :] = source[pl.ds(names[base + u], 1), :]


def cuts(per):
    return (0, per // 2), (per // 2, per)


def pick_kernel(wanted, table, out, rows, *, first, last, per):
    part = last - first

    def body(device, carry):
        for u in range(part):
            name = wanted[device * per + (first + u)]
            rows[pl.ds(device * part + u, 1), :] = table[pl.ds(name, 1), :]
        return carry

    lax.fori_loop(0, out.shape[0] // part, body, 0)
    out[...] = rows[...].astype(jnp.bfloat16)


def pick_rows(wanted, table, per, ends):
    first, last = ends
    width = table.shape[1]
    count = wanted.shape[0] // per * (last - first)
    return call(
        functools.partial(pick_kernel, first=first, last=last, per=per),
        "pick_rows",
        jax.ShapeDtypeStruct((count, width), jnp.bfloat16),
        [smem, vmem],
        vmem,
        [pltpu.VMEM((count, width), jnp.float32)],
        4.6,
        20 << 20,
    )(wanted, table)


def stood(flat, unit):
    size = flat.shape[1]
    flat = jnp.concatenate(
        [flat, jnp.full((unit - flat.shape[0], size), -1, jnp.int32)], axis=0
    ).astype(jnp.float32)
    step = min(LANES, size)
    parts = [jnp.transpose(flat[:, k : k + step]) for k in range(0, size, step)]
    return jnp.concatenate(parts, axis=0).astype(jnp.int32)


def reach_kernel(
    adjacent_three,
    valid_three,
    labelled,
    adjacent_two,
    valid_two,
    names,
    places,
    near_two,
    near_three,
    count,
    left,
    right,
    *,
    rows_all,
    per,
):
    fan_three, seeds = adjacent_three.shape
    fan_two, targets = adjacent_two.shape
    low = jnp.bfloat16
    blocks = rows_all // LANES
    deep = names.shape[0]
    line = labelled[...].reshape(1, seeds)
    column = jnp.transpose(jnp.broadcast_to(line.astype(jnp.float32), (8, seeds)))[:, 0:1]
    near = stood(jnp.where(valid_three[...] > 0, adjacent_three[...], -1), near_three.shape[1])
    near_three[...] = near
    here = jnp.where(column > 0.0, near, -1)
    place = lax.broadcasted_iota(jnp.int32, (seeds, targets), 1)
    hit = jnp.zeros((seeds, targets), jnp.float32)
    for j in range(fan_three):
        hit = hit + jnp.where(here[:, j : j + 1] == place, 1.0, 0.0)
    need = jnp.max(hit, axis=0, keepdims=True) + jnp.concatenate(
        [line.astype(jnp.float32), jnp.zeros((1, targets - seeds), jnp.float32)], axis=1
    )

    level = lax.broadcasted_iota(jnp.int32, (deep, targets), 0)
    lane = lax.broadcasted_iota(jnp.int32, (targets, LANES), 1)
    flat = jnp.where(valid_two[...] > 0, adjacent_two[...], -1)
    tall = stood(flat, near_two.shape[1])
    near_two[...] = tall
    flat = jnp.where(need > 0.0, flat, -1)
    for j in range(fan_two):
        left[0:deep, j * targets : (j + 1) * targets] = jnp.where(
            lax.shift_right_arithmetic(flat[j : j + 1, :], 7) == level, 1.0, 0.0
        ).astype(low)
        right[j * targets : (j + 1) * targets, :] = jnp.where(
            (tall[:, j : j + 1] & (LANES - 1)) == lane, 1.0, 0.0
        ).astype(low)
    used = dot(left[0:deep, 0 : fan_two * targets], right[0 : fan_two * targets, :])
    own = [need[:, k : k + LANES] for k in range(0, targets, LANES)]
    own = jnp.concatenate(
        own + [jnp.zeros((deep - len(own), LANES), jnp.float32)], axis=0
    )
    flag = jnp.where(used + own > 0.0, 1.0, 0.0)

    square_row = lax.broadcasted_iota(jnp.int32, (LANES, LANES), 0)
    square_col = lax.broadcasted_iota(jnp.int32, (LANES, LANES), 1)
    full = jnp.concatenate([flag, jnp.zeros((LANES - deep, LANES), jnp.float32)], axis=0)
    flag_low = full.astype(low)
    running = dot(flag_low, jnp.where(square_row <= square_col, 1.0, 0.0).astype(low))
    totals = dot(flag_low, jnp.ones((LANES, LANES), low)).astype(low)
    before = dot(jnp.where(square_row > square_col, 1.0, 0.0).astype(low), totals)
    order = (before + running - full).astype(jnp.int32)
    number = jnp.sum(flag).astype(jnp.int32)
    count[0] = number
    count[1] = 2 * lax.div(number + (2 * SPAN - 1), 2 * SPAN)

    high = jnp.where(full > 0.0, lax.shift_right_arithmetic(order, 7), -1)
    rest = jnp.transpose((order & (LANES - 1)).astype(jnp.float32)).astype(jnp.int32)
    step = lax.broadcasted_iota(jnp.int32, (deep, LANES), 0)
    inner = lax.broadcasted_iota(jnp.int32, (deep, LANES), 1).astype(jnp.float32)
    for b in range(blocks):
        match = jnp.where(high[b : b + 1, :] == step, 1.0, 0.0)
        lanes = slice(b * LANES, (b + 1) * LANES)
        left[0:deep, lanes] = (match * inner).astype(low)
        left[deep : 2 * deep, lanes] = (match * float(b)).astype(low)
        right[lanes, :] = jnp.where(rest[:, b : b + 1] == square_col, 1.0, 0.0).astype(low)
    found = dot(left[:, 0:rows_all], right[0:rows_all, :]).astype(jnp.int32)
    where = step * LANES + lax.broadcasted_iota(jnp.int32, (deep, LANES), 1)
    name = found[deep:] * LANES + found[0:deep]
    names[...] = jnp.where(where < number, name, rows_all)
    name = jnp.minimum(jnp.where(where < number, name, 0), rows_all - 1)
    owners = -(-rows_all // per)
    owner = lax.shift_right_logical(name, per.bit_length() - 1)
    slot = name & (per - 1)
    early, late = (last - first for first, last in cuts(per))
    places[...] = jnp.where(
        slot < early, owner * early + slot, owners * early + owner * late + slot - early
    )


def reach(adjacent_three, valid_three, labelled, adjacent_two, valid_two, rows_all, per):
    targets, fan = adjacent_two.shape
    seeds = labelled.shape[0]
    deep = up(up(rows_all, 2 * SPAN) // LANES, 16)
    area = max(fan * targets, rows_all)
    return call(
        functools.partial(reach_kernel, rows_all=rows_all, per=per),
        "reach",
        (
            jax.ShapeDtypeStruct((deep, LANES), jnp.int32),
            jax.ShapeDtypeStruct((deep, LANES), jnp.int32),
            jax.ShapeDtypeStruct((targets, 16), jnp.int32),
            jax.ShapeDtypeStruct((seeds, 8), jnp.int32),
            jax.ShapeDtypeStruct((2,), jnp.int32),
        ),
        [vmem] * 5,
        (vmem,) * 4 + (smem,),
        [
            pltpu.VMEM((2 * deep, area), jnp.bfloat16),
            pltpu.VMEM((area, LANES), jnp.bfloat16),
        ],
        3.0,
        8 << 20,
    )(adjacent_three.T, valid_three.T, labelled, adjacent_two.T, valid_two.T)


def tally_kernel(count, names, adjacent, valid, *refs, per, which):
    multiply = which == 0
    if multiply:
        source, out, table, rows, spread, marked, buffer, sems, terms, sums = refs
        width = source.shape[1]
        terms[:, 0:width] = source[...]
        terms[:, width:] = jnp.ones((source.shape[0], width), jnp.bfloat16)
    else:
        out, table, rows, spread, marked, buffer, sems = refs
    low = jnp.bfloat16
    fan, targets = adjacent.shape
    unit = spread.shape[0]
    groups = SPAN // unit
    few = 8 if multiply else groups
    used = count[1]
    high_all = buffer.shape[2] // SPAN
    first, last = cuts(per)[which]
    size = last - first

    slot = adjacent[...]
    owner = lax.shift_right_logical(slot, per.bit_length() - 1)
    inner = slot & (per - 1)
    here = (valid[...] > 0) & (inner >= first) & (inner < last)
    slot = jnp.where(here, owner * size + inner - first, -1)
    slot = jnp.concatenate([slot, jnp.full((unit - fan, targets), -1, jnp.int32)], axis=0)
    slot = slot.astype(jnp.float32)
    for b in range(0, targets, LANES):
        table[b : b + LANES, :] = jnp.transpose(slot[:, b : b + LANES]).astype(jnp.int32)
    table[targets:, :] = jnp.full((table.shape[0] - targets, unit), -1, jnp.int32)

    across = lax.broadcasted_iota(jnp.int32, (unit, SPAN), 1)
    down = lax.broadcasted_iota(jnp.int32, (unit, SPAN), 0)
    spread[...] = jnp.where(lax.div(across, unit) == down, 1.0, 0.0).astype(low)
    lane = across.astype(jnp.float32).astype(low)
    one = jnp.ones((unit, SPAN), low)
    zero = jnp.zeros((unit, SPAN), low)

    def copies(block, slot):
        where = pl.ds(pl.multiple_of(block * SPAN, SPAN), SPAN)
        result = sums if multiply else buffer
        return pltpu.make_async_copy(result.at[slot], out.at[where, :], sems.at[slot])

    def body(block, carry):
        slot = lax.rem(block, 2)

        @pl.when(block >= 2)
        def _():
            copies(block - 2, slot).wait()

        copy_rows(names, block * SPAN, SPAN, table, rows)
        high = lax.shift_right_arithmetic(rows[...], 8).astype(jnp.float32).astype(low)
        own = lax.rem(lax.broadcasted_iota(jnp.int32, (SPAN, SPAN), 0), unit) == lax.rem(
            lax.broadcasted_iota(jnp.int32, (SPAN, SPAN), 1), unit
        )
        marked[...] = jnp.where(own, dot(high, spread[...]), -1.0).astype(low)

        def single(g):
            first = pl.multiple_of(g * unit, unit)
            rest = (rows[pl.ds(first, unit), :] & (SPAN - 1)).astype(jnp.float32)
            columns = [
                jnp.where(
                    jnp.broadcast_to(rest[:, j : j + 1], (unit, SPAN)).astype(low) == lane,
                    one,
                    zero,
                )
                for j in range(unit)
            ]
            mark = marked[pl.ds(first, unit), :]
            marks = [
                jnp.where(mark == jnp.full((unit, SPAN), float(q), low), one, zero)
                for q in range(high_all)
            ]
            return dot(jnp.concatenate(marks, axis=0), jnp.concatenate(columns, axis=0))

        def group(step, inner):
            for u in range(0, few, 2):
                pair = [single(step * few + u), single(step * few + u + 1)]
                where = pl.ds(pl.multiple_of((step * few + u) * unit, 2 * unit), 2 * unit)
                for q in range(high_all):
                    tile = jnp.concatenate(
                        [item[q * unit : (q + 1) * unit] for item in pair], axis=0
                    )
                    buffer[slot, where, q * SPAN : (q + 1) * SPAN] = tile.astype(buffer.dtype)
            return inner

        lax.fori_loop(0, groups // few, group, 0)
        if multiply:
            sums[slot] = dot(buffer[slot], terms[...])
        copies(block, slot).start()
        return carry

    lax.fori_loop(0, used, body, 0)

    @pl.when(used >= 2)
    def _():
        copies(used - 2, lax.rem(used - 2, 2)).wait()

    @pl.when(used >= 1)
    def _():
        copies(used - 1, lax.rem(used - 1, 2)).wait()


def tally(count, names, adjacent, valid, padded, devices, per, which, sources):
    targets = adjacent.shape[0]
    unit = 16
    first, last = cuts(per)[which]
    wide = devices * (last - first)
    multiply = which == 0
    width = sources[0].shape[1] if multiply else 0
    scratch = [
        pltpu.VMEM((targets + 8, unit), jnp.int32),
        pltpu.VMEM((SPAN, unit), jnp.int32),
        pltpu.VMEM((unit, SPAN), jnp.bfloat16),
        pltpu.VMEM((SPAN, SPAN), jnp.bfloat16),
        pltpu.VMEM((2, SPAN, wide), jnp.bfloat16 if multiply else COUNTS),
        pltpu.SemaphoreType.DMA((2,)),
    ]
    if multiply:
        out = jax.ShapeDtypeStruct((3 * padded, 2 * width), jnp.float32)
        scratch += [
            pltpu.VMEM((wide, 2 * width), jnp.bfloat16),
            pltpu.VMEM((2, SPAN, 2 * width), jnp.float32),
        ]
    else:
        out = jax.ShapeDtypeStruct((padded, wide), COUNTS)
    return call(
        functools.partial(tally_kernel, per=per, which=which),
        "early_sums" if multiply else "tally",
        out,
        [smem, smem] + [vmem] * (2 + len(sources)),
        anywhere,
        scratch,
        14.0,
        BIG,
    )(count, names, adjacent.T, valid.T, *sources)


def link_kernel(count, names, near, out, buffer, sems, *, fan):
    targets = near.shape[0]
    tile = 32
    blocks = count[1]

    def rows(step, carry):
        first = pl.multiple_of(step * tile, tile)
        here = near[pl.ds(first, tile), :]
        spread = [jnp.broadcast_to(here[:, j : j + 1], (tile, LANES)) for j in range(fan)]
        own = first + lax.broadcasted_iota(jnp.int32, (tile, LANES), 0)

        def columns(block, inner):
            for part in range(SPAN // LANES):
                name = jnp.broadcast_to(
                    names[pl.ds(block * (SPAN // LANES) + part, 1), :], (tile, LANES)
                )
                number = jnp.zeros((tile, LANES), jnp.float32)
                for j in range(fan):
                    number = number + jnp.where(spread[j] == name, 1.0, 0.0)
                lanes = pl.ds(part * LANES, LANES)
                buffer[block, pl.ds(first, tile), lanes] = number.astype(jnp.bfloat16)
                buffer[block, pl.ds(targets + first, tile), lanes] = jnp.where(
                    own == name, 1.0, 0.0
                ).astype(jnp.bfloat16)
            return inner

        return lax.fori_loop(0, blocks, columns, carry)

    lax.fori_loop(0, targets // tile, rows, 0)

    def save(block):
        return pltpu.make_async_copy(buffer.at[block], out.at[block], sems.at[block])

    def start(block, carry):
        save(block).start()
        return carry

    def finish(block, carry):
        save(block).wait()
        return carry

    lax.fori_loop(0, blocks, start, 0)
    lax.fori_loop(0, blocks, finish, 0)


def link_matrix(count, names, near, fan, padded):
    blocks = padded // SPAN
    targets = near.shape[0]
    return call(
        functools.partial(link_kernel, fan=fan),
        "link_matrix",
        jax.ShapeDtypeStruct((2 * blocks, 2 * targets, SPAN), jnp.bfloat16),
        [smem, vmem, vmem],
        anywhere,
        [
            pltpu.VMEM((blocks, 2 * targets, SPAN), jnp.bfloat16),
            pltpu.SemaphoreType.DMA((blocks,)),
        ],
        5.0,
        BIG,
    )(count, names, near)


def step_kernel(
    info,
    count,
    places,
    partial,
    tallies,
    links,
    *refs,
    classes,
):
    sources = refs[:PARTS]
    step_body(
        info, count, places, partial, tallies, links, sources, *refs[PARTS:],
        classes=classes,
    )


def step_body(
    info,
    count,
    places,
    partial,
    tallies,
    links,
    sources,
    near_two,
    near_three,
    labels,
    labelled,
    weights_in,
    weights_mid,
    weights_out,
    biases_line,
    keep,
    send,
    slopes,
    packed,
    sums,
    weight_sums,
    mid_sums,
    out_sums,
    own_table,
    late_table,
    mixin,
    own_rows,
    joined,
    late,
    early,
    link,
    sems,
    link_sems,
    *,
    classes,
):
    blocks, both, _ = links.shape
    targets = both // 2
    hidden = weights_in.shape[2]
    seeds = labels.shape[0]
    biases = biases_line[...].reshape(1, biases_line.shape[0])
    label, marked = [
        jnp.transpose(
            jnp.broadcast_to(item[...].reshape(1, seeds).astype(jnp.float32), (8, seeds))
        )[:, 0:1]
        for item in (labels, labelled)
    ]
    wide = up(classes, LANES)
    core = info[0]
    used = count[1]
    low = jnp.bfloat16
    width = sources[0].shape[1]

    def load(pair, slot):
        rows = pl.ds(pl.multiple_of(pair * 2 * SPAN, 2 * SPAN), 2 * SPAN)
        return (
            pltpu.make_async_copy(tallies.at[rows, :], late.at[slot], sems.at[slot, 0]),
            pltpu.make_async_copy(partial.at[rows, :], early.at[slot], sems.at[slot, 1]),
        )

    def load_link(block):
        return pltpu.make_async_copy(links.at[block], link.at[block], link_sems.at[block])

    @pl.when(used > 0)
    def _():
        for copy in load(0, 0):
            copy.start()

    def start_link(block, carry):
        load_link(block).start()
        return carry

    lax.fori_loop(0, used, start_link, 0)
    late_table[:, 0:width] = sources[-1][...]
    late_table[:, width:] = jnp.ones((late_table.shape[0], width), low)
    filled = 0
    for source in sources:
        held = own_table.shape[0] * source.shape[0] // sum(item.shape[0] for item in sources)
        own_table[filled : filled + held, :] = source[0:held, :].astype(jnp.float32)
        filled += held

    w_in = weights_in[...].astype(low).reshape(2 * weights_in.shape[1], hidden)
    bias_in = biases[:, 0:hidden]
    bias_mid = biases[:, hidden : 2 * hidden]
    bias_out = jnp.concatenate(
        [
            biases[:, 2 * hidden : 2 * hidden + classes],
            jnp.full((1, wide - classes), -1e30, jnp.float32),
        ],
        axis=1,
    )

    sums[...] = jnp.zeros_like(sums)

    def forward(pair, carry):
        rows = pl.ds(pl.multiple_of(pair * 2 * SPAN, 2 * SPAN), 2 * SPAN)
        slot = lax.rem(pair, 2)
        for copy in load(pair, slot):
            copy.wait()
        load_link(2 * pair).wait()
        load_link(2 * pair + 1).wait()

        @pl.when(2 * pair + 2 < used)
        def _():
            for copy in load(pair + 1, 1 - slot):
                copy.start()

        copy_rows(places, pair * 2 * SPAN, 2 * SPAN, own_table, own_rows)
        joined[...] = dot(late[slot].astype(low), late_table[...]) + early[slot]
        mixin[rows, 0:width] = own_rows[...].astype(low)
        mixin[rows, width:] = (
            joined[:, 0:width] / jnp.maximum(joined[:, width:], 1.0)
        ).astype(low)
        z = dot(mixin[rows, :], w_in) + bias_in
        s = 1.0 / (1.0 + jnp.exp(-z))
        slopes[rows, :] = s * (1.0 + z * (1.0 - s))
        wide_link = jnp.concatenate([link[2 * pair], link[2 * pair + 1]], axis=1)
        sums[...] += dot(wide_link, (z * s).astype(low))
        return carry

    pairs = lax.div(used, 2)
    lax.fori_loop(0, pairs, forward, 0)
    total = sums[...]
    counts_two = clipped_counts(near_two[...] >= 0)
    mixed_one = (total[0:targets] / counts_two).astype(low)
    self_one = total[targets:].astype(low)
    w_mid = weights_mid[...].astype(low)
    both_one = jnp.concatenate([self_one, mixed_one], axis=1)
    z = dot(both_one, w_mid.reshape(2 * hidden, hidden)) + bias_mid
    s = 1.0 / (1.0 + jnp.exp(-z))
    slope_mid = s * (1.0 + z * (1.0 - s))
    hidden_two = (z * s).astype(low)

    here = near_three[...]
    place = lax.broadcasted_iota(jnp.int32, (seeds, targets), 1)
    number = jnp.zeros((seeds, targets), jnp.float32)
    for j in range(here.shape[1]):
        number = number + jnp.where(here[:, j : j + 1] == place, 1.0, 0.0)
    number = number.astype(low)
    counts_three = clipped_counts(here >= 0)
    mixed_two = (dot(number, hidden_two) / counts_three).astype(low)
    self_two = hidden_two[0:seeds]
    w_out = [
        jnp.concatenate(
            [weights_out[:, k, :], jnp.zeros((wide - classes, hidden), jnp.float32)], axis=0
        ).astype(low)
        for k in range(2)
    ]
    both_two = jnp.concatenate([self_two, mixed_two], axis=1)
    logits = dot_cols(both_two, jnp.concatenate(w_out, axis=1)) + bias_out
    top = jnp.max(logits, axis=1, keepdims=True)
    log_total = top + jnp.log(jnp.sum(jnp.exp(logits - top), axis=1, keepdims=True))
    onehot = jnp.where(
        label.astype(jnp.int32) == lax.broadcasted_iota(jnp.int32, (seeds, wide), 1), 1.0, 0.0
    )
    picked = jnp.sum(jnp.where(onehot > 0.0, logits, 0.0), axis=1, keepdims=True)
    loss = jnp.sum(marked * (log_total - picked), axis=0, keepdims=True)
    counted = jnp.sum(marked, axis=0, keepdims=True)
    grad_out = (marked * (jnp.exp(logits - log_total) - onehot)).astype(low)

    out_sums[...] = dot_rows(grad_out, both_two)
    bias_grad_out = jnp.sum(grad_out.astype(jnp.float32), axis=0, keepdims=True)
    to_self = dot(grad_out, w_out[0])
    spread = (dot(grad_out, w_out[1]) / counts_three).astype(low)
    sums[0:targets, :] = dot_rows(number, spread)
    sums[0:seeds, :] += to_self
    grad_mid = (sums[0:targets, :] * slope_mid).astype(low)

    mid_sums[...] = dot_rows(both_one, grad_mid)
    bias_grad_mid = jnp.sum(grad_mid.astype(jnp.float32), axis=0, keepdims=True)
    down = jnp.concatenate(
        [dot_cols(grad_mid, w_mid[1]) / counts_two, dot_cols(grad_mid, w_mid[0])], axis=0
    )
    spread = down.astype(low)

    weight_sums[...] = jnp.zeros_like(weight_sums)

    def backward(pair, bias):
        rows = pl.ds(pl.multiple_of(pair * 2 * SPAN, 2 * SPAN), 2 * SPAN)
        wide_link = jnp.concatenate([link[2 * pair], link[2 * pair + 1]], axis=1)
        grad = (dot_rows(wide_link, spread) * slopes[rows, :]).astype(low)
        weight_sums[...] += dot_rows(mixin[rows, :], grad)
        return bias + jnp.sum(grad.astype(jnp.float32), axis=0, keepdims=True)

    bias_grad_in = lax.fori_loop(0, pairs, backward, jnp.zeros((1, hidden), jnp.float32))

    row = 0
    for part in (weight_sums, mid_sums):
        for column in range(0, hidden, LANES):
            packed[row : row + part.shape[0], :] = part[:, column : column + LANES]
            row += part.shape[0]
    tall = up(classes, 16)
    for column in range(0, 2 * hidden, LANES):
        packed[row : row + tall, :] = out_sums[0:tall, column : column + LANES]
        row += tall
    packed[row:, :] = jnp.zeros((packed.shape[0] - row, LANES), jnp.float32)
    lane = lax.broadcasted_iota(jnp.int32, (1, LANES), 1)
    scalars = jnp.where(lane == 0, loss, 0.0) + jnp.where(lane == 1, counted, 0.0)
    extra = [
        item[:, column : column + LANES]
        for item in (bias_grad_in, bias_grad_mid, bias_grad_out)
        for column in range(0, hidden, LANES)
    ] + [scalars, jnp.zeros((1, LANES), jnp.float32)]
    extra = jnp.concatenate(extra, axis=0)
    high = extra.astype(low).astype(jnp.float32)
    packed[packed.shape[0] - 16 :, :] = jnp.concatenate([high, extra - high], axis=0)
    half = keep.shape[0]
    keep[...] = packed[pl.ds(pl.multiple_of(core * half, 16), half), :].astype(low)
    send[...] = packed[pl.ds(pl.multiple_of((1 - core) * half, 16), half), :].astype(low)


def run_step(info, count, places, partial, tallies, links, sources, rest, half, classes, held):
    padded = tallies.shape[0]
    blocks, both = padded // SPAN, links.shape[1]
    total, width = sources[-1].shape
    hidden = rest[4].shape[2]
    wide = up(classes, LANES)
    return call(
        functools.partial(step_kernel, classes=classes),
        "step",
        (jax.ShapeDtypeStruct((half, LANES), jnp.bfloat16),) * 2,
        [smem] * 3 + [anywhere] * 3 + [vmem] * (PARTS + 8),
        (vmem, vmem),
        [
            pltpu.VMEM((padded, hidden), jnp.float32),
            pltpu.VMEM((2 * half, LANES), jnp.float32),
            pltpu.VMEM((both, hidden), jnp.float32),
            pltpu.VMEM((2 * width, hidden), jnp.float32),
            pltpu.VMEM((2 * hidden, hidden), jnp.float32),
            pltpu.VMEM((wide, 2 * hidden), jnp.float32),
            pltpu.VMEM((held, width), jnp.float32),
            pltpu.VMEM((total, 2 * width), jnp.bfloat16),
            pltpu.VMEM((padded, 2 * width), jnp.bfloat16),
            pltpu.VMEM((2 * SPAN, width), jnp.float32),
            pltpu.VMEM((2 * SPAN, 2 * width), jnp.float32),
            pltpu.VMEM((2, 2 * SPAN, total), COUNTS),
            pltpu.VMEM((2, 2 * SPAN, 2 * width), jnp.float32),
            pltpu.VMEM((blocks, both, SPAN), jnp.bfloat16),
            pltpu.SemaphoreType.DMA((2, 2)),
            pltpu.SemaphoreType.DMA((blocks,)),
        ],
        14.0,
        BIG,
    )(info, count, places, partial, tallies, links, *sources, *rest)


def refit(total, rows):
    extra = total[rows - 16 : rows - 8] + total[rows - 8 : rows]
    high = extra.astype(jnp.bfloat16).astype(jnp.float32)
    return jnp.concatenate([high, extra - high], axis=0)


def pair_kernel(info, mine, theirs, out):
    total = mine[...].astype(jnp.float32) + theirs[...].astype(jnp.float32)
    out[...] = total.astype(jnp.bfloat16)

    @pl.when(info[0] == 1)
    def _():
        rows = total.shape[0]
        out[rows - 16 :, :] = refit(total, rows).astype(jnp.bfloat16)


def pair_sum(info, mine, theirs):
    return call(
        pair_kernel,
        "pair_sum",
        jax.ShapeDtypeStruct(mine.shape, jnp.bfloat16),
        [smem, vmem, vmem],
        vmem,
        [],
        0.6,
        6 << 20,
    )(info, mine, theirs)


def spread_kernel(info, pieces, out):
    total = pieces[0].astype(jnp.float32)
    for k in range(1, pieces.shape[0]):
        total = total + pieces[k].astype(jnp.float32)
    rows = total.shape[0]
    fitted = jnp.concatenate([total[0 : rows - 16], refit(total, rows)], axis=0)
    result = jnp.where(info[1] == 1, fitted, total).astype(jnp.bfloat16)
    for k in range(pieces.shape[0]):
        out[k] = result


def spread_sum(info, pieces):
    return call(
        spread_kernel,
        "spread_sum",
        jax.ShapeDtypeStruct(pieces.shape, jnp.bfloat16),
        [smem, vmem],
        vmem,
        [],
        0.6,
        6 << 20,
    )(info, pieces)


def update_kernel(
    info, fixes, mine, theirs, biases, moment_one, moment_two, *refs
):
    groups = [refs[5 * k : 5 * k + 5] for k in range(3)]
    loss_out = refs[15]
    outs = [refs[16 + 4 * k : 20 + 4 * k] for k in range(3)]
    bias_out, first_out, second_out = refs[28:31]
    packed = refs[31]
    low = jnp.bfloat16
    half = mine.shape[0]
    core = info[0]
    packed[pl.ds(pl.multiple_of(core * half, 16), half), :] = mine[...]
    packed[pl.ds(pl.multiple_of((1 - core) * half, 16), half), :] = theirs[...]
    last = packed.shape[0]
    extra = packed[last - 16 :, :].astype(jnp.float32)
    extra = extra[0:8] + extra[8:16]
    counted = extra[6:7, 1:2]
    inverse = 1.0 / counted
    loss_out[...] = extra[6:7, 0:1] / counted
    scale = 0.5 * inverse * inverse

    row = 0
    for group in range(3):
        master, left, right, left_root, right_root = groups[group]
        new_master, copy, new_left, new_right = outs[group]
        turned = group == 2
        depth, hidden = (master.shape[0], master.shape[2]) if turned else master.shape[1:]
        deep = up(depth, LANES)

        def take(ref, k, middle):
            return ref[:, k, :] if middle else ref[k]

        def put(ref, k, middle, value):
            if middle:
                ref[:, k, :] = value
            else:
                ref[k] = value

        grads = []
        if turned:
            tall = up(depth, 16)
            for k in range(2):
                parts = []
                for column in range(0, hidden, LANES):
                    parts.append(packed[row : row + tall, :])
                    row += tall
                grads.append(grown(jnp.concatenate(parts, axis=1), deep, hidden))
        else:
            parts = []
            for column in range(0, hidden, LANES):
                parts.append(packed[row : row + 2 * depth, :])
                row += 2 * depth
            whole = jnp.concatenate(parts, axis=1)
            grads = [whole[k * depth : (k + 1) * depth] for k in range(2)]

        for k in range(2):
            grad = grads[k]
            for old, new, size, product, middle in (
                (left, new_left, depth, dot_cols(grad, grad), turned),
                (right, new_right, hidden, dot_rows(grad, grad), False),
            ):
                corner = old[0:1, k, 0:1] if middle else old[k, 0:1, 0:1]
                eye = lax.broadcasted_iota(jnp.int32, (size, size), 0) == (
                    lax.broadcasted_iota(jnp.int32, (size, size), 1)
                )
                value = jnp.where(eye, 0.5 * corner, 0.0) + scale * product[0:size, 0:size]
                put(new, k, middle, value)
            root = jnp.concatenate(
                halves(grown(take(left_root, k, turned), deep, deep)), axis=1
            )
            middle_high, middle_rest = halves(dot(root, jnp.concatenate([grad, grad], axis=0)))
            root_high, root_rest = halves(right_root[k])
            way = dot(
                jnp.concatenate([middle_high, middle_high, middle_rest], axis=1),
                jnp.concatenate([root_high, root_rest, root_high], axis=0),
            )[0:depth]
            put(new_master, k, turned, take(master, k, turned) - inverse * way)
        copy[...] = new_master[...].astype(low)

    size = biases.shape[0]
    grad = jnp.concatenate([extra[k : k + 1, :] for k in range(6)], axis=1)[:, 0:size]
    grad = grad / counted

    def line(ref):
        return ref[...].reshape(1, size)

    first = 0.9 * line(moment_one) + 0.1 * grad
    second = 0.95 * line(moment_two) + 0.05 * grad * grad
    old = line(biases)
    fresh = old - 0.1 * (
        (first / fixes[0]) / (jnp.sqrt(second / fixes[1]) + 1e-08) + 0.01 * old
    )
    for ref, value in ((bias_out, fresh), (first_out, first), (second_out, second)):
        ref[...] = value[0]


def run_update(info, fixes, mine, theirs, vectors, groups):
    outs = [jax.ShapeDtypeStruct((1, 1), jnp.float32)]
    flat = []
    for master, left, right, left_root, right_root in groups:
        flat += [master, left, right, left_root, right_root]
        outs += [
            jax.ShapeDtypeStruct(master.shape, jnp.float32),
            jax.ShapeDtypeStruct(master.shape, jnp.bfloat16),
            jax.ShapeDtypeStruct(left_root.shape, jnp.float32),
            jax.ShapeDtypeStruct(right_root.shape, jnp.float32),
        ]
    outs += [jax.ShapeDtypeStruct(vectors[0].shape, jnp.float32)] * 3
    return call(
        update_kernel,
        "update",
        tuple(outs),
        [smem] * 2 + [vmem] * (5 + len(flat)),
        (vmem,) * len(outs),
        [pltpu.VMEM((2 * mine.shape[0], LANES), jnp.bfloat16)],
        4.0,
        16 << 20,
    )(info, fixes, mine, theirs, *vectors, *flat)


def body(
    features,
    requests,
    adjacent_one,
    adjacent_two,
    adjacent_three,
    valid_one,
    valid_two,
    valid_three,
    labels,
    labelled,
    weights_in,
    weights_mid,
    weights_out,
    biases,
    moment_one,
    moment_two,
    step_count,
    left_in,
    left_mid,
    left_out,
    right_in,
    right_mid,
    right_out,
    invleft_in,
    invleft_mid,
    invleft_out,
    invright_in,
    invright_mid,
    invright_out,
    *,
    peers,
):
    width = features.shape[1]
    devices, per = requests.shape
    targets = adjacent_one.shape[0]
    padded = up(targets, 2 * SPAN)
    classes = weights_out.shape[2]
    hidden = weights_in.shape[2]
    core = lax.axis_index("core")
    own = lax.axis_index(PEERS)

    wanted = lax.all_to_all(requests, AXES, split_axis=0, concat_axis=0, tiled=True)
    names, places, near_two, near_three, count = reach(
        adjacent_three, valid_three, labelled, adjacent_two, valid_two, targets, per
    )
    wanted, count = lax.optimization_barrier((wanted.reshape(-1), count))
    early_cut, late_cut = cuts(per)

    def trade(found):
        pulled = lax.all_to_all(
            found.reshape(devices, -1, width), AXES, split_axis=0, concat_axis=0, tiled=True
        )
        return pulled.reshape(-1, width)

    early_source = trade(pick_rows(wanted, features, per, early_cut))
    found = pick_rows(wanted, features, per, late_cut)
    links = link_matrix(count, names, near_two, adjacent_two.shape[1], padded)
    names, places = names.reshape(-1), places.reshape(-1)
    late_tally = tally(
        count, names, adjacent_one, valid_one, padded, devices, per, 1, ()
    )

    core_info = jnp.stack([core, ((core == 1) & (own == peers - 1)).astype(jnp.int32)])
    core_info = core_info.astype(jnp.int32)
    stepped = step_count.astype(jnp.float32)
    fixes = jnp.stack([1.0 - 0.9**stepped, 1.0 - 0.95**stepped])
    found, late_tally, info, fixes = lax.optimization_barrier(
        (found, late_tally, core_info, fixes)
    )
    late_source = trade(found)
    partial = tally(
        count, names, adjacent_one, valid_one, padded, devices, per, 0, (early_source,)
    )

    rows = (2 * width + 2 * weights_mid.shape[1]) * (hidden // LANES)
    rows += up(classes, 16) * (2 * hidden // LANES)
    each = up(-(-(rows + 16) // (2 * peers)), 8)
    half = each * peers
    turned_out = weights_out.transpose(2, 0, 1)
    keep, send = run_step(
        info,
        count,
        places,
        partial,
        late_tally,
        links,
        (early_source, late_source),
        (
            near_two,
            near_three,
            labels,
            labelled,
            weights_in,
            weights_mid,
            turned_out,
            biases,
        ),
        half,
        classes,
        -(-targets // per) * per,
    )
    swap = [(0, 1), (1, 0)]
    theirs = lax.ppermute(send, "core", swap)
    summed = pair_sum(info, keep, theirs).reshape(peers, each, LANES)
    pieces = lax.all_to_all(summed, PEERS, split_axis=0, concat_axis=0, tiled=True)
    shared = spread_sum(info, pieces)
    mine = lax.all_to_all(shared, PEERS, split_axis=0, concat_axis=0, tiled=True)
    mine = mine.reshape(half, LANES)
    theirs = lax.ppermute(mine, "core", swap)

    outs = run_update(
        info,
        fixes,
        mine,
        theirs,
        (biases, moment_one, moment_two),
        (
            (weights_in, left_in, right_in, invleft_in, invright_in),
            (weights_mid, left_mid, right_mid, invleft_mid, invright_mid),
            (
                turned_out,
                right_out.transpose(1, 0, 2),
                left_out,
                invright_out.transpose(1, 0, 2),
                invleft_out,
            ),
        ),
    )
    first, second, third = (outs[1 + 4 * k : 5 + 4 * k] for k in range(3))
    third = (
        third[0].transpose(1, 2, 0),
        third[1].transpose(1, 2, 0),
        third[3],
        third[2].transpose(1, 0, 2),
    )
    return (
        (outs[0].reshape(()),)
        + tuple(group[which] for which in range(4) for group in (first, second, third))
        + tuple(outs[13:16])
    )


def solution(mesh):
    chips, dev = mesh.shape["hst"] // 2, mesh.shape["dev"]
    fine = jax.sharding.Mesh(mesh.devices.reshape(chips, 2, dev), AXES)
    split = P(AXES, None)
    line = P(AXES)
    whole = P()
    mapped = jax.shard_map(
        functools.partial(body, peers=chips * dev),
        mesh=fine,
        in_specs=(split,) * 8 + (line,) * 2 + (whole,) * 19,
        out_specs=(whole,) * 16,
        check_vma=False,
    )

    def run(*args):
        with jax.sharding.use_abstract_mesh(fine.abstract_mesh):
            return mapped(*args)

    return run
```

profile of v0, /device:TPU:0, one launch (start us, length us, event | category | flops | bytes accessed | tf_op | source)
XLA Modules:
  0.0 146.9 jit_solution(519331485953002248)
XLA Ops:
  0.6 1.4 all_to_all.18
  2.0 7.3 %all-to-all-start = ((s32[32,1,256]{2,1,0:T(1,128)}), s32[32,1,256]{2,1,0:T(1,128)S(1)}, u32[]{:S(2)}, u32[]{:S(2)}) async-start(s32[32,1,256]{2,1,0:T(1,128)} %all_to_all.18), calls=%async_computation | async-start | bytes 65536 | tf_op jit(solution)/shard_map/all_to_all | solution.py:921
  9.3 0.0 copy-start.20
  9.4 0.7 copy-done.20
  10.1 0.7 copy-done.21
  10.8 0.7 copy-done.25
  11.5 0.7 copy-done.26
  12.2 0.7 copy-done.27
  12.9 2.6 %reach.1 = (s32[48,128]{1,0:T(8,128)S(1)}, s32[48,128]{1,0:T(8,128)S(1)}, s32[384,16]{1,0:T(8,128)S(1)}, s32[64,8]{1,0:T(8,128)S(1)}, s32[2]{0:T(128)S(1)}) custom-call(s32[5,64]{1,0:T(8,128)S(1)} %bitcast.46, s32[5,64]{1,0:T(8,128)S(1)} %bitcast.47, s32[64]{0:T(128)S(1)} %copy-done.27, s32[10,384]{1,0:T(8,128)S(1)} %bitcast.44, s32[10,384]{1,0:T(8,128)S(1)} %bitcast.45), custom_call_target="tpu_custom_call" | custom-call | bytes 10800000 | tf_op jit(solution)/shard_map/reach/pallas_call | solution.py:221
  15.5 1.0 all-to-all-done
  16.5 3.4 %copy-done = f32[16384,128]{1,0:T(8,128)S(1)} copy-done((f32[16384,128]{1,0:T(8,128)S(1)}, f32[16384,128]{1,0:T(8,128)}, u32[]{:S(2)}) %copy-start) | copy-done | bytes 8388632
  19.9 5.5 %pick_rows.3 = bf16[4096,128]{1,0:T(8,128)(2,1)} custom-call(s32[8192]{0:T(1024)S(1)} %bitcast.39, f32[16384,128]{1,0:T(8,128)S(1)} %copy-done), custom_call_target="tpu_custom_call" | custom-call | bytes 16559999 | tf_op jit(solution)/shard_map/pick_rows/pallas_call | solution.py:103
  25.5 4.8 %all-to-all-start.1 = ((bf16[32,128,128]{2,1,0:T(8,128)(2,1)}), bf16[32,128,128]{2,1,0:T(8,128)(2,1)S(1)}, u32[]{:S(2)}, u32[]{:S(2)}) async-start(bf16[32,128,128]{2,1,0:T(8,128)(2,1)} %bitcast.13), calls=%async_computation.1 | async-start | bytes 2097152 | tf_op jit(solution)/shard_map/all_to_all | solution.py:929
  31.0 0.1 pad_add_fusion.info
  31.1 0.1 pad_maximum_fusion.fixes
  31.2 3.4 %copy-done.1 = f32[16384,128]{1,0:T(8,128)S(1)} copy-done((f32[16384,128]{1,0:T(8,128)S(1)}, f32[16384,128]{1,0:T(8,128)}, u32[]{:S(2)}) %copy-start.1) | copy-done | bytes 8388632
  34.6 5.5 %pick_rows.2 = bf16[4096,128]{1,0:T(8,128)(2,1)} custom-call(s32[8192]{0:T(1024)S(1)} %bitcast.40, f32[16384,128]{1,0:T(8,128)S(1)} %copy-done.1), custom_call_target="tpu_custom_call" | custom-call | bytes 16559999 | tf_op jit(solution)/shard_map/pick_rows/pallas_call | solution.py:103
  40.1 4.5 %tally.1.tallies = f8e4m3fn[4608,4096]{1,0:T(32,128)(4,1)} custom-call(s32[2]{0:T(128)S(1)} %get-tuple-element.47.count, s32[6144]{0:T(1024)S(1)} %bitcast.41, s32[15,4224]{1,0:T(8,128)S(1)} %bitcast.33, s32[15,4224]{1,0:T(8,128)S(1)} %bitcast.35), custom_call_target="tpu_custom_call" | custom-call | bytes 50400000 | tf_op jit(solution)/shard_map/tally/pallas_call | solution.py:367
  44.6 13.3 %all-to-all-done.1 = bf16[32,128,128]{2,1,0:T(8,128)(2,1)S(1)} async-done(((bf16[32,128,128]{2,1,0:T(8,128)(2,1)}), bf16[32,128,128]{2,1,0:T(8,128)(2,1)S(1)}, u32[]{:S(2)}, u32[]{:S(2)}) %all-to-all-start.1) | async-done | bytes 1048608 | tf_op jit(solution)/shard_map/all_to_all | solution.py:929
  57.9 3.4 %all-to-all-start.2 = ((bf16[32,128,128]{2,1,0:T(8,128)(2,1)}), bf16[32,128,128]{2,1,0:T(8,128)(2,1)}, u32[]{:S(2)}, u32[]{:S(2)}) async-start(bf16[32,128,128]{2,1,0:T(8,128)(2,1)} %bitcast.15), calls=%async_computation.2 | async-start | bytes 2097152 | tf_op jit(solution)/shard_map/all_to_all | solution.py:929
  61.3 0.0 copy-start.3
  61.3 0.0 copy-start.4
  61.3 0.0 copy-start.7
  61.3 0.0 copy-start.22
  61.3 0.0 copy-start.28
  61.3 0.0 copy-start.29
  61.3 4.0 %link_matrix.1.links = bf16[36,768,256]{2,1,0:T(8,128)(2,1)} custom-call(s32[2]{0:T(128)S(1)} %get-tuple-element.47.count, s32[48,128]{1,0:T(8,128)S(1)} %get-tuple-element.48.names, s32[384,16]{1,0:T(8,128)S(1)} %get-tuple-element.53.near.refs_2_), custom_call_target="tpu_custom_call" | custom-call | bytes 18000000 | tf_op jit(solution)/shard_map/link_matrix/pallas_call | solution.py:427
  65.4 6.8 %early_sums.1.partial = f32[13824,256]{1,0:T(8,128)} custom-call(s32[2]{0:T(128)S(1)} %get-tuple-element.47.count, s32[6144]{0:T(1024)S(1)} %bitcast.42, s32[15,4224]{1,0:T(8,128)S(1)} %bitcast.34, s32[15,4224]{1,0:T(8,128)S(1)} %bitcast.36, bf16[4096,128]{1,0:T(8,128)(2,1)S(1)} %bitcast.26), custom_call_target="tpu_custom_call" | custom-call | bytes 50400000 | tf_op jit(solution)/shard_map/early_sums/pallas_call | solution.py:367
  72.3 16.6 %all-to-all-done.2 = bf16[32,128,128]{2,1,0:T(8,128)(2,1)} async-done(((bf16[32,128,128]{2,1,0:T(8,128)(2,1)}), bf16[32,128,128]{2,1,0:T(8,128)(2,1)}, u32[]{:S(2)}, u32[]{:S(2)}) %all-to-all-start.2) | async-done | bytes 1048608 | tf_op jit(solution)/shard_map/all_to_all | solution.py:929
  88.9 0.0 copy-start.8
  88.9 0.0 copy-start.9
  88.9 0.0 copy-start.10
  88.9 0.0 copy-start.11
  88.9 0.0 copy-start.12
  88.9 0.0 copy-start.13
  89.0 0.0 copy-start.15
  89.0 0.0 copy-start.16
  89.0 0.0 copy-start.18
  89.0 0.0 copy-start.19
  89.1 9.0 %step.1 = (bf16[1152,128]{1,0:T(8,128)(2,1)S(1)}, bf16[1152,128]{1,0:T(8,128)(2,1)S(1)}) custom-call(s32[2]{0:T(128)S(1)} %pad_add_fusion.info, s32[2]{0:T(128)S(1)} %get-tuple-element.47.count, s32[6144]{0:T(1024)S(1)} %bitcast.43, f32[13824,256]{1,0:T(8,128)} %early_sums.1.partial, f8e4m3fn[4608,4096]{1,0:T(32,128)(4,1)} %tally.1.tallies, ...), custom_call_target="tpu_custom_call" | custom-call | bytes 50400000 | tf_op jit(solution)/shard_map/step/pallas_call | solution.py:677
  98.0 0.1 collective-permute-start
  98.1 1.6 %collective-permute-done.theirs = bf16[1152,128]{1,0:T(8,128)(2,1)S(1)} collective-permute-done((bf16[1152,128]{1,0:T(8,128)(2,1)S(1)}, bf16[1152,128]{1,0:T(8,128)(2,1)S(1)}, u32[]{:S(2)}, u32[]{:S(2)}) %collective-permute-start) | collective-permute-done | bytes 294944 | tf_op jit(solution)/shard_map/ppermute | solution.py:982
  99.7 0.6 pair_sum.1
  100.3 26.9 %all_to_all.29.pieces = bf16[16,72,128]{2,1,0:T(8,128)(2,1)S(1)} all-to-all(bf16[16,72,128]{2,1,0:T(8,128)(2,1)S(1)} %bitcast.32), channel_id=1, replica_groups=mesh['chip'=2,'core'=2,'dev'=8] {'chip','dev'}, dimensions={0} | all-to-all | bytes 589824 | tf_op jit(solution)/shard_map/all_to_all | solution.py:984
  127.2 0.6 spread_sum.1
  127.8 13.3 %all_to_all.30 = bf16[16,72,128]{2,1,0:T(8,128)(2,1)S(1)} all-to-all(bf16[16,72,128]{2,1,0:T(8,128)(2,1)S(1)} %spread_sum.1), channel_id=1, replica_groups=mesh['chip'=2,'core'=2,'dev'=8] {'chip','dev'}, dimensions={0} | all-to-all | bytes 589824 | tf_op jit(solution)/shard_map/all_to_all | solution.py:986
  141.1 1.6 %collective-permute-done.1.theirs = bf16[1152,128]{1,0:T(8,128)(2,1)S(1)} collective-permute-done((bf16[1152,128]{1,0:T(8,128)(2,1)S(1)}, bf16[1152,128]{1,0:T(8,128)(2,1)S(1)}, u32[]{:S(2)}, u32[]{:S(2)}) %collective-permute-start.1) | collective-permute-done | bytes 294944 | tf_op jit(solution)/shard_map/ppermute | solution.py:988
  142.8 3.9 %update.1 = (f32[1,1]{1,0:T(1,128)}, f32[2,128,256]{2,1,0:T(8,128)}, bf16[2,128,256]{2,1,0:T(8,128)(2,1)}, f32[2,128,128]{2,1,0:T(8,128)}, f32[2,256,256]{2,1,0:...) custom-call(s32[2]{0:T(128)S(1)} %pad_add_fusion.info, ...), custom_call_target="tpu_custom_call" | custom-call | bytes 14400000 | tf_op jit(solution)/shard_map/update/pallas_call | solution.py:867
  (37 shorter events, 0.1 us)
Async XLA Ops:
  2.0 14.5 %all-to-all-start = ((s32[32,1,256]{2,1,0:T(1,128)}), s32[32,1,256]{2,1,0:T(1,128)S(1)}, u32[]{:S(2)}, u32[]{:S(2)}) async-start(s32[32,1,256]{2,1,0:T(1,128)} %all_to_all.18), calls=%async_computation | async-start | bytes 65536 | tf_op jit(solution)/shard_map/all_to_all | solution.py:921
  9.3 0.7 copy-start.20
  10.1 0.7 copy-start.21
  10.8 0.7 copy-start.25
  11.5 0.7 copy-start.26
  12.2 0.7 copy-start.27
  16.5 3.4 %copy-start = (f32[16384,128]{1,0:T(8,128)S(1)}, f32[16384,128]{1,0:T(8,128)}, u32[]{:S(2)}) copy-start(f32[16384,128]{1,0:T(8,128)} %table.3) | copy-start | bytes 25165828
  19.9 20.2 %copy-start.5 = (s32[4224,15]{0,1:T(8,128)S(1)}, s32[4224,15]{0,1:T(8,128)}, u32[]{:S(2)}) copy-start(s32[4224,15]{0,1:T(8,128)} %param.31) | copy-start | bytes 760324
  19.9 20.2 %copy-start.6 = (s32[4224,15]{0,1:T(8,128)S(1)}, s32[4224,15]{0,1:T(8,128)}, u32[]{:S(2)}) copy-start(s32[4224,15]{0,1:T(8,128)} %param.34) | copy-start | bytes 760324
  25.5 32.4 %all-to-all-start.1 = ((bf16[32,128,128]{2,1,0:T(8,128)(2,1)}), bf16[32,128,128]{2,1,0:T(8,128)(2,1)S(1)}, u32[]{:S(2)}, u32[]{:S(2)}) async-start(bf16[32,128,128]{2,1,0:T(8,128)(2,1)} %bitcast.13), calls=%async_computation.1 | async-start | bytes 2097152 | tf_op jit(solution)/shard_map/all_to_all | solution.py:929
  31.2 3.4 %copy-start.1 = (f32[16384,128]{1,0:T(8,128)S(1)}, f32[16384,128]{1,0:T(8,128)}, u32[]{:S(2)}) copy-start(f32[16384,128]{1,0:T(8,128)} %table.3) | copy-start | bytes 25165828
  57.9 14.4 %copy-start.2 = (bf16[32,128,128]{2,1,0:T(8,128)(2,1)}, bf16[32,128,128]{2,1,0:T(8,128)(2,1)S(1)}, u32[]{:S(2)}) copy-start(bf16[32,128,128]{2,1,0:T(8,128)(2,1)S(1)} %all-to-all-done.1) | copy-start | bytes 3145732
  57.9 31.0 %all-to-all-start.2 = ((bf16[32,128,128]{2,1,0:T(8,128)(2,1)}), bf16[32,128,128]{2,1,0:T(8,128)(2,1)}, u32[]{:S(2)}, u32[]{:S(2)}) async-start(bf16[32,128,128]{2,1,0:T(8,128)(2,1)} %bitcast.15), calls=%async_computation.2 | async-start | bytes 2097152 | tf_op jit(solution)/shard_map/all_to_all | solution.py:929
  61.3 27.6 %copy-start.3 = (f32[2,256,256]{2,1,0:T(8,128)S(1)}, f32[2,256,256]{2,1,0:T(8,128)}, u32[]{:S(2)}) copy-start(f32[2,256,256]{2,1,0:T(8,128)} %refs_5_.3) | copy-start | bytes 1572868
  61.3 27.6 %copy-start.4 = (f32[2,256,172]{1,0,2:T(2,128)S(1)}, f32[2,256,172]{1,0,2:T(2,128)}, u32[]{:S(2)}) copy-start(f32[2,256,172]{1,0,2:T(2,128)} %param.41) | copy-start | bytes 1056772
  61.3 27.5 %copy-start.7 = (f32[2,128,256]{2,1,0:T(8,128)S(1)}, f32[2,128,256]{2,1,0:T(8,128)}, u32[]{:S(2)}) copy-start(f32[2,128,256]{2,1,0:T(8,128)} %refs_0_.1) | copy-start | bytes 786436
  61.3 27.5 %copy-start.22 = (f32[684]{0:T(1024)S(1)}, f32[684]{0:T(1024)}, u32[]{:S(2)}) copy-start(f32[684]{0:T(1024)} %biases.1) | copy-start | bytes 8212
  61.3 27.5 %copy-start.28 = (s32[64]{0:T(128)S(1)}, s32[64]{0:T(128)}, u32[]{:S(2)}) copy-start(s32[64]{0:T(128)} %refs_5_.2) | copy-start | bytes 772
  61.3 27.5 %copy-start.29 = (s32[64]{0:T(128)S(1)}, s32[64]{0:T(128)}, u32[]{:S(2)}) copy-start(s32[64]{0:T(128)} %refs_4_.2) | copy-start | bytes 772
  88.9 53.8 %copy-start.8 = (f32[2,256,256]{2,1,0:T(8,128)S(1)}, f32[2,256,256]{2,1,0:T(8,128)}, u32[]{:S(2)}) copy-start(f32[2,256,256]{2,1,0:T(8,128)} %refs_2_.1) | copy-start | bytes 1572868
  88.9 53.8 %copy-start.9 = (f32[2,256,256]{2,1,0:T(8,128)S(1)}, f32[2,256,256]{2,1,0:T(8,128)}, u32[]{:S(2)}) copy-start(f32[2,256,256]{2,1,0:T(8,128)} %refs_4_.3) | copy-start | bytes 1572868
  88.9 53.8 %copy-start.10 = (f32[2,256,256]{2,1,0:T(8,128)S(1)}, f32[2,256,256]{2,1,0:T(8,128)}, u32[]{:S(2)}) copy-start(f32[2,256,256]{2,1,0:T(8,128)} %refs_6_.3) | copy-start | bytes 1572868
  88.9 53.8 %copy-start.11 = (f32[2,256,256]{2,1,0:T(8,128)S(1)}, f32[2,256,256]{2,1,0:T(8,128)}, u32[]{:S(2)}) copy-start(f32[2,256,256]{2,1,0:T(8,128)} %refs_7_.3) | copy-start | bytes 1572868
  88.9 53.8 %copy-start.12 = (f32[2,256,256]{2,1,0:T(8,128)S(1)}, f32[2,256,256]{2,1,0:T(8,128)}, u32[]{:S(2)}) copy-start(f32[2,256,256]{2,1,0:T(8,128)} %refs_8_.1) | copy-start | bytes 1572868
  88.9 53.8 %copy-start.13 = (f32[2,256,256]{2,1,0:T(8,128)S(1)}, f32[2,256,256]{2,1,0:T(8,128)}, u32[]{:S(2)}) copy-start(f32[2,256,256]{2,1,0:T(8,128)} %refs_9_.3) | copy-start | bytes 1572868
  89.0 53.8 %copy-start.14 = (f32[2,256,256]{2,1,0:T(8,128)S(1)}, f32[2,256,256]{2,1,0:T(8,128)}, u32[]{:S(2)}) copy-start(f32[2,256,256]{2,1,0:T(8,128)} %refs_12_.1) | copy-start | bytes 1572868
  89.0 53.8 %copy-start.15 = (f32[2,256,256]{2,1,0:T(8,128)S(1)}, f32[2,256,256]{2,1,0:T(8,128)}, u32[]{:S(2)}) copy-start(f32[2,256,256]{2,1,0:T(8,128)} %refs_14_.1) | copy-start | bytes 1572868
  89.0 53.8 %copy-start.16 = (f32[2,172,172]{2,0,1:T(2,128)S(1)}, f32[2,172,172]{2,0,1:T(2,128)}, u32[]{:S(2)}) copy-start(f32[2,172,172]{2,0,1:T(2,128)} %param.51) | copy-start | bytes 710020
  89.0 53.8 %copy-start.17 = (f32[2,172,172]{2,0,1:T(2,128)S(1)}, f32[2,172,172]{2,0,1:T(2,128)}, u32[]{:S(2)}) copy-start(f32[2,172,172]{2,0,1:T(2,128)} %param.57) | copy-start | bytes 710020
  89.0 53.8 %copy-start.18 = (f32[2,128,128]{2,1,0:T(8,128)S(1)}, f32[2,128,128]{2,1,0:T(8,128)}, u32[]{:S(2)}) copy-start(f32[2,128,128]{2,1,0:T(8,128)} %refs_1_.1) | copy-start | bytes 393220
  89.0 53.8 %copy-start.19 = (f32[2,128,128]{2,1,0:T(8,128)S(1)}, f32[2,128,128]{2,1,0:T(8,128)}, u32[]{:S(2)}) copy-start(f32[2,128,128]{2,1,0:T(8,128)} %refs_3_.1) | copy-start | bytes 393220
  89.0 53.7 %copy-start.23 = (f32[684]{0:T(1024)S(1)}, f32[684]{0:T(1024)}, u32[]{:S(2)}) copy-start(f32[684]{0:T(1024)} %moment_one.1) | copy-start | bytes 8212
  89.0 53.7 %copy-start.24 = (f32[684]{0:T(1024)S(1)}, f32[684]{0:T(1024)}, u32[]{:S(2)}) copy-start(f32[684]{0:T(1024)} %moment_two.1) | copy-start | bytes 8212
  98.0 1.6 %collective-permute-start = (bf16[1152,128]{1,0:T(8,128)(2,1)S(1)}, bf16[1152,128]{1,0:T(8,128)(2,1)S(1)}, u32[]{:S(2)}, u32[]{:S(2)}) collective-permute-start(bf16[1152,128]{1,0:T(8,128)(2,1)S(1)} %get-tuple-element.57), channel_id=1, source_target_pairs={{0,8},{8,0},{1,9},{9,1},{2,10},{10,2},{3,11},{11,3},{4,12},{12,4},... | collective-permute-start | bytes 884744 | tf_op jit(solution)/shard_map/ppermute | solution.py:982
  141.1 1.6 %collective-permute-start.1 = (bf16[1152,128]{1,0:T(8,128)(2,1)S(1)}, bf16[1152,128]{1,0:T(8,128)(2,1)S(1)}, u32[]{:S(2)}, u32[]{:S(2)}) collective-permute-start(bf16[1152,128]{1,0:T(8,128)(2,1)S(1)} %bitcast.30), channel_id=1, source_target_pairs={{0,8},{8,0},{1,9},{9,1},{2,10},{10,2},{3,11},{11,3},{4,12},{12,4},... | collective-permute-start | bytes 884744 | tf_op jit(solution)/shard_map/ppermute | solution.py:988
where the time goes:
time: 144 us; the launch traced here: 147 us
  Pallas kernels  43.2 us (30%)
  blocking collectives  40.2 us (28%)
  waiting for transfers between devices  34 us (24%)
  starting transfers between devices  15.6 us (11%)
  local copies, waits for them, and re-layouts  11.8 us (8%)
  between operations  1.94 us (1%)
    all_to_all x2, waiting for transfers between devices, trade(): lax.all_to_all(found.reshape(devices, -1, width), AXES, split_axis=0, con...  29.8 us
    all_to_all x1, blocking collectives, body(): lax.all_to_all(summed, PEERS, split_axis=0, concat_axis=0, tiled=True)  26.9 us
    all_to_all x1, blocking collectives, body(): lax.all_to_all(shared, PEERS, split_axis=0, concat_axis=0, tiled=True)  13.3 us
    pallas_call x2, Pallas kernels, tally(): call(functools.partial(tally_kernel, per=per, which=which), 'early_sums'...  11.3 us
    pallas_call x2, Pallas kernels, pick_rows(): call(functools.partial(pick_kernel, first=first, last=last, per=per), 'pi...  11.1 us
    unnamed x60, local copies, waits for them, and re-layouts  10.4 us
    pallas_call x1, Pallas kernels, run_step(): call(functools.partial(step_kernel, classes=classes), 'step', (jax.ShapeD...  8.98 us
    all_to_all x2, starting transfers between devices, trade(): lax.all_to_all(found.reshape(devices, -1, width), AXES, split_axis=0, con...  8.2 us
  transfers between devices with their start and end apart: 5, of which 5 were waited for; matrix products, arithmetic and copies ran while one was open for 0% of the time, Pallas kernels for 16%

commit v1 on v0

--- a/solution.py
+++ b/solution.py
@@ -380,6 +380,14 @@
     targets = near.shape[0]
     tile = 32
     blocks = count[1]
+    all_blocks = buffer.shape[0] - 2
+    across = SPAN // LANES
+
+    def line(block, part):
+        return jnp.broadcast_to(names[pl.ds(block * across + part, 1), :], (tile, LANES))
+
+    def save(block):
+        return pltpu.make_async_copy(buffer.at[block], out.at[block], sems.at[block])
 
     def rows(step, carry):
         first = pl.multiple_of(step * tile, tile)
@@ -388,26 +396,25 @@
         own = first + lax.broadcasted_iota(jnp.int32, (tile, LANES), 0)
 
         def columns(block, inner):
-            for part in range(SPAN // LANES):
-                name = jnp.broadcast_to(
-                    names[pl.ds(block * (SPAN // LANES) + part, 1), :], (tile, LANES)
-                )
+            for part in range(across):
+                name = line(block, part)
                 number = jnp.zeros((tile, LANES), jnp.float32)
                 for j in range(fan):
                     number = number + jnp.where(spread[j] == name, 1.0, 0.0)
                 lanes = pl.ds(part * LANES, LANES)
                 buffer[block, pl.ds(first, tile), lanes] = number.astype(jnp.bfloat16)
-                buffer[block, pl.ds(targets + first, tile), lanes] = jnp.where(
-                    own == name, 1.0, 0.0
+            return inner
+
+        lax.fori_loop(0, blocks, columns, 0)
+        for block in range(2):
+            for part in range(across):
+                lanes = slice(part * LANES, (part + 1) * LANES)
+                buffer[all_blocks + block, pl.ds(first, tile), lanes] = jnp.where(
+                    own == line(block, part), 1.0, 0.0
                 ).astype(jnp.bfloat16)
-            return inner
-
-        return lax.fori_loop(0, blocks, columns, carry)
+        return carry
 
     lax.fori_loop(0, targets // tile, rows, 0)
-
-    def save(block):
-        return pltpu.make_async_copy(buffer.at[block], out.at[block], sems.at[block])
 
     def start(block, carry):
         save(block).start()
@@ -417,8 +424,10 @@
         save(block).wait()
         return carry
 
-    lax.fori_loop(0, blocks, start, 0)
-    lax.fori_loop(0, blocks, finish, 0)
+    for ends in ((0, blocks), (all_blocks, all_blocks + 2)):
+        lax.fori_loop(*ends, start, 0)
+    for ends in ((0, blocks), (all_blocks, all_blocks + 2)):
+        lax.fori_loop(*ends, finish, 0)
 
 
 def link_matrix(count, names, near, fan, padded):
@@ -427,12 +436,12 @@
     return call(
         functools.partial(link_kernel, fan=fan),
         "link_matrix",
-        jax.ShapeDtypeStruct((2 * blocks, 2 * targets, SPAN), jnp.bfloat16),
+        jax.ShapeDtypeStruct((4 * blocks, targets, SPAN), jnp.bfloat16),
         [smem, vmem, vmem],
         anywhere,
         [
-            pltpu.VMEM((blocks, 2 * targets, SPAN), jnp.bfloat16),
-            pltpu.SemaphoreType.DMA((blocks,)),
+            pltpu.VMEM((blocks + 2, targets, SPAN), jnp.bfloat16),
+            pltpu.SemaphoreType.DMA((blocks + 2,)),
         ],
         5.0,
         BIG,
@@ -487,14 +496,15 @@
     joined,
     late,
     early,
+    hid,
+    down_low,
     link,
     sems,
     link_sems,
     *,
     classes,
 ):
-    blocks, both, _ = links.shape
-    targets = both // 2
+    targets = links.shape[1]
     hidden = weights_in.shape[2]
     seeds = labels.shape[0]
     biases = biases_line[...].reshape(1, biases_line.shape[0])
@@ -530,6 +540,9 @@
         return carry
 
     lax.fori_loop(0, used, start_link, 0)
+    own_link = link.shape[0] - 2
+    for block in range(2):
+        load_link(own_link + block).start()
     late_table[:, 0:width] = sources[-1][...]
     late_table[:, width:] = jnp.ones((late_table.shape[0], width), low)
     filled = 0
@@ -551,6 +564,9 @@
 
     sums[...] = jnp.zeros_like(sums)
 
+    def paired(block):
+        return jnp.concatenate([link[block], link[block + 1]], axis=1)
+
     def forward(pair, carry):
         rows = pl.ds(pl.multiple_of(pair * 2 * SPAN, 2 * SPAN), 2 * SPAN)
         slot = lax.rem(pair, 2)
@@ -573,8 +589,15 @@
         z = dot(mixin[rows, :], w_in) + bias_in
         s = 1.0 / (1.0 + jnp.exp(-z))
         slopes[rows, :] = s * (1.0 + z * (1.0 - s))
-        wide_link = jnp.concatenate([link[2 * pair], link[2 * pair + 1]], axis=1)
-        sums[...] += dot(wide_link, (z * s).astype(low))
+        hid[...] = (z * s).astype(low)
+        sums[0:targets, :] += dot(paired(2 * pair), hid[...])
+
+        @pl.when(pair == 0)
+        def _():
+            for block in range(2):
+                load_link(own_link + block).wait()
+            sums[targets:, :] = dot(paired(own_link), hid[...])
+
         return carry
 
     pairs = lax.div(used, 2)
@@ -630,14 +653,19 @@
     down = jnp.concatenate(
         [dot_cols(grad_mid, w_mid[1]) / counts_two, dot_cols(grad_mid, w_mid[0])], axis=0
     )
-    spread = down.astype(low)
+    down_low[...] = down.astype(low)
 
     weight_sums[...] = jnp.zeros_like(weight_sums)
 
     def backward(pair, bias):
         rows = pl.ds(pl.multiple_of(pair * 2 * SPAN, 2 * SPAN), 2 * SPAN)
-        wide_link = jnp.concatenate([link[2 * pair], link[2 * pair + 1]], axis=1)
-        grad = (dot_rows(wide_link, spread) * slopes[rows, :]).astype(low)
+        joined[...] = dot_rows(paired(2 * pair), down_low[0:targets, :])
+
+        @pl.when(pair == 0)
+        def _():
+            joined[...] += dot_rows(paired(own_link), down_low[targets:, :])
+
+        grad = (joined[...] * slopes[rows, :]).astype(low)
         weight_sums[...] += dot_rows(mixin[rows, :], grad)
         return bias + jnp.sum(grad.astype(jnp.float32), axis=0, keepdims=True)
 
@@ -670,7 +698,7 @@
 
 def run_step(info, count, places, partial, tallies, links, sources, rest, half, classes, held):
     padded = tallies.shape[0]
-    blocks, both = padded // SPAN, links.shape[1]
+    blocks, targets = padded // SPAN, links.shape[1]
     total, width = sources[-1].shape
     hidden = rest[4].shape[2]
     wide = up(classes, LANES)
@@ -683,7 +711,7 @@
         [
             pltpu.VMEM((padded, hidden), jnp.float32),
             pltpu.VMEM((2 * half, LANES), jnp.float32),
-            pltpu.VMEM((both, hidden), jnp.float32),
+            pltpu.VMEM((2 * targets, hidden), jnp.float32),
             pltpu.VMEM((2 * width, hidden), jnp.float32),
             pltpu.VMEM((2 * hidden, hidden), jnp.float32),
             pltpu.VMEM((wide, 2 * hidden), jnp.float32),
@@ -694,9 +722,11 @@
             pltpu.VMEM((2 * SPAN, 2 * width), jnp.float32),
             pltpu.VMEM((2, 2 * SPAN, total), COUNTS),
             pltpu.VMEM((2, 2 * SPAN, 2 * width), jnp.float32),
-            pltpu.VMEM((blocks, both, SPAN), jnp.bfloat16),
+            pltpu.VMEM((2 * SPAN, hidden), jnp.bfloat16),
+            pltpu.VMEM((2 * targets, hidden), jnp.bfloat16),
+            pltpu.VMEM((blocks + 2, targets, SPAN), jnp.bfloat16),
             pltpu.SemaphoreType.DMA((2, 2)),
-            pltpu.SemaphoreType.DMA((blocks,)),
+            pltpu.SemaphoreType.DMA((blocks + 2,)),
         ],
         14.0,
         BIG,
@@ -943,8 +973,8 @@
     core_info = core_info.astype(jnp.int32)
     stepped = step_count.astype(jnp.float32)
     fixes = jnp.stack([1.0 - 0.9**stepped, 1.0 - 0.95**stepped])
-    found, late_tally, info, fixes = lax.optimization_barrier(
-        (found, late_tally, core_info, fixes)
+    found, late_tally, links, info, fixes = lax.optimization_barrier(
+        (found, late_tally, links, core_info, fixes)
     )
     late_source = trade(found)
     partial = tally(

time: 144 us -> 145 us (level); the launches traced: 147 us -> 144 us
  blocking collectives: 40.2 us -> 34.6 us
  starting transfers between devices: 15.6 us -> 17.9 us
    all_to_all x1, blocking collectives: 26.9 us -> 21.3 us  [body(): lax.all_to_all(summed, PEERS, split_axis=0, concat_axis=0, tiled=True)]
    all_to_all x2, starting transfers between devices: 8.2 us -> 10.6 us  [trade(): lax.all_to_all(found.reshape(devices, -1, width), AXES, split_axis=0, con...]
where the time goes in v1:
time: 145 us; the launch traced here: 144 us
  Pallas kernels  43.7 us (30%)
  blocking collectives  34.6 us (24%)
  waiting for transfers between devices  33.9 us (23%)
  starting transfers between devices  17.9 us (12%)
  local copies, waits for them, and re-layouts  11.8 us (8%)
  between operations  1.95 us (1%)
    all_to_all x2, waiting for transfers between devices, trade(): lax.all_to_all(found.reshape(devices, -1, width), AXES, split_axis=0, con...  29.8 us
    all_to_all x1, blocking collectives, body(): lax.all_to_all(summed, PEERS, split_axis=0, concat_axis=0, tiled=True)  21.3 us
    all_to_all x1, blocking collectives, body(): lax.all_to_all(shared, PEERS, split_axis=0, concat_axis=0, tiled=True)  13.3 us
    pallas_call x2, Pallas kernels, tally(): call(functools.partial(tally_kernel, per=per, which=which), 'early_sums'...  11.3 us
    pallas_call x2, Pallas kernels, pick_rows(): call(functools.partial(pick_kernel, first=first, last=last, per=per), 'pi...  11.1 us
    all_to_all x2, starting transfers between devices, trade(): lax.all_to_all(found.reshape(devices, -1, width), AXES, split_axis=0, con...  10.6 us
    unnamed x60, local copies, waits for them, and re-layouts  10.4 us
    pallas_call x1, Pallas kernels, run_step(): call(functools.partial(step_kernel, classes=classes), 'step', (jax.ShapeD...  9.33 us
  transfers between devices with their start and end apart: 5, of which 5 were waited for; matrix products, arithmetic and copies ran while one was open for 0% of the time, Pallas kernels for 16%

profile of v1, /device:TPU:0, one launch (start us, length us, event | category | flops | bytes accessed | tf_op | source)
XLA Modules:
  0.0 144.0 jit_solution(9736217387883691739)
XLA Ops:
  0.6 1.4 all_to_all.18
  2.0 7.3 %all-to-all-start = ((s32[32,1,256]{2,1,0:T(1,128)}), s32[32,1,256]{2,1,0:T(1,128)S(1)}, u32[]{:S(2)}, u32[]{:S(2)}) async-start(s32[32,1,256]{2,1,0:T(1,128)} %all_to_all.18), calls=%async_computation | async-start | bytes 65536 | tf_op jit(solution)/shard_map/all_to_all | solution.py:951
  9.3 0.0 copy-start.20
  9.4 0.7 copy-done.20
  10.1 0.7 copy-done.21
  10.8 0.7 copy-done.25
  11.5 0.7 copy-done.26
  12.2 0.7 copy-done.27
  12.9 2.6 %reach.1 = (s32[48,128]{1,0:T(8,128)S(1)}, s32[48,128]{1,0:T(8,128)S(1)}, s32[384,16]{1,0:T(8,128)S(1)}, s32[64,8]{1,0:T(8,128)S(1)}, s32[2]{0:T(128)S(1)}) custom-call(s32[5,64]{1,0:T(8,128)S(1)} %bitcast.46, s32[5,64]{1,0:T(8,128)S(1)} %bitcast.47, s32[64]{0:T(128)S(1)} %copy-done.27, s32[10,384]{1,0:T(8,128)S(1)} %bitcast.44, s32[10,384]{1,0:T(8,128)S(1)} %bitcast.45), custom_call_target="tpu_custom_call" | custom-call | bytes 10800000 | tf_op jit(solution)/shard_map/reach/pallas_call | solution.py:221
  15.5 1.0 all-to-all-done
  16.5 3.4 %copy-done = f32[16384,128]{1,0:T(8,128)S(1)} copy-done((f32[16384,128]{1,0:T(8,128)S(1)}, f32[16384,128]{1,0:T(8,128)}, u32[]{:S(2)}) %copy-start) | copy-done | bytes 8388632
  19.9 5.6 %pick_rows.3 = bf16[4096,128]{1,0:T(8,128)(2,1)} custom-call(s32[8192]{0:T(1024)S(1)} %bitcast.39, f32[16384,128]{1,0:T(8,128)S(1)} %copy-done), custom_call_target="tpu_custom_call" | custom-call | bytes 16559999 | tf_op jit(solution)/shard_map/pick_rows/pallas_call | solution.py:103
  25.5 4.8 %all-to-all-start.1 = ((bf16[32,128,128]{2,1,0:T(8,128)(2,1)}), bf16[32,128,128]{2,1,0:T(8,128)(2,1)S(1)}, u32[]{:S(2)}, u32[]{:S(2)}) async-start(bf16[32,128,128]{2,1,0:T(8,128)(2,1)} %bitcast.13), calls=%async_computation.1 | async-start | bytes 2097152 | tf_op jit(solution)/shard_map/all_to_all | solution.py:959
  31.1 0.1 pad_add_fusion.info
  31.1 0.1 pad_maximum_fusion.fixes
  31.2 3.4 %copy-done.1 = f32[16384,128]{1,0:T(8,128)S(1)} copy-done((f32[16384,128]{1,0:T(8,128)S(1)}, f32[16384,128]{1,0:T(8,128)}, u32[]{:S(2)}) %copy-start.1) | copy-done | bytes 8388632
  34.6 5.5 %pick_rows.2 = bf16[4096,128]{1,0:T(8,128)(2,1)} custom-call(s32[8192]{0:T(1024)S(1)} %bitcast.40, f32[16384,128]{1,0:T(8,128)S(1)} %copy-done.1), custom_call_target="tpu_custom_call" | custom-call | bytes 16559999 | tf_op jit(solution)/shard_map/pick_rows/pallas_call | solution.py:103
  40.1 4.1 %link_matrix.1.links = bf16[72,384,256]{2,1,0:T(8,128)(2,1)} custom-call(s32[2]{0:T(128)S(1)} %get-tuple-element.48.count, s32[48,128]{1,0:T(8,128)S(1)} %get-tuple-element.49.names, s32[384,16]{1,0:T(8,128)S(1)} %get-tuple-element.50.near.refs_2_), custom_call_target="tpu_custom_call" | custom-call | bytes 18000000 | tf_op jit(solution)/shard_map/link_matrix/pallas_call | solution.py:436
  44.3 0.0 copy-start.3
  44.3 0.0 copy-start.4
  44.3 0.0 copy-start.7
  44.3 0.0 copy-start.22
  44.3 0.0 copy-start.28
  44.3 0.0 copy-start.29
  44.4 4.5 %tally.1.tallies = f8e4m3fn[4608,4096]{1,0:T(32,128)(4,1)} custom-call(s32[2]{0:T(128)S(1)} %get-tuple-element.48.count, s32[6144]{0:T(1024)S(1)} %bitcast.41, s32[15,4224]{1,0:T(8,128)S(1)} %bitcast.33, s32[15,4224]{1,0:T(8,128)S(1)} %bitcast.35), custom_call_target="tpu_custom_call" | custom-call | bytes 50400000 | tf_op jit(solution)/shard_map/tally/pallas_call | solution.py:367
  48.9 9.0 %all-to-all-done.1 = bf16[32,128,128]{2,1,0:T(8,128)(2,1)S(1)} async-done(((bf16[32,128,128]{2,1,0:T(8,128)(2,1)}), bf16[32,128,128]{2,1,0:T(8,128)(2,1)S(1)}, u32[]{:S(2)}, u32[]{:S(2)}) %all-to-all-start.1) | async-done | bytes 1048608 | tf_op jit(solution)/shard_map/all_to_all | solution.py:959
  57.9 5.7 %all-to-all-start.2 = ((bf16[32,128,128]{2,1,0:T(8,128)(2,1)}), bf16[32,128,128]{2,1,0:T(8,128)(2,1)}, u32[]{:S(2)}, u32[]{:S(2)}) async-start(bf16[32,128,128]{2,1,0:T(8,128)(2,1)} %bitcast.15), calls=%async_computation.2 | async-start | bytes 2097152 | tf_op jit(solution)/shard_map/all_to_all | solution.py:959
  63.7 6.8 %early_sums.1.partial = f32[13824,256]{1,0:T(8,128)} custom-call(s32[2]{0:T(128)S(1)} %get-tuple-element.48.count, s32[6144]{0:T(1024)S(1)} %bitcast.42, s32[15,4224]{1,0:T(8,128)S(1)} %bitcast.34, s32[15,4224]{1,0:T(8,128)S(1)} %bitcast.36, bf16[4096,128]{1,0:T(8,128)(2,1)S(1)} %bitcast.26), custom_call_target="tpu_custom_call" | custom-call | bytes 50400000 | tf_op jit(solution)/shard_map/early_sums/pallas_call | solution.py:367
  70.5 20.7 %all-to-all-done.2 = bf16[32,128,128]{2,1,0:T(8,128)(2,1)} async-done(((bf16[32,128,128]{2,1,0:T(8,128)(2,1)}), bf16[32,128,128]{2,1,0:T(8,128)(2,1)}, u32[]{:S(2)}, u32[]{:S(2)}) %all-to-all-start.2) | async-done | bytes 1048608 | tf_op jit(solution)/shard_map/all_to_all | solution.py:959
  91.3 0.0 copy-start.8
  91.3 0.0 copy-start.9
  91.3 0.0 copy-start.10
  91.3 0.0 copy-start.11
  91.3 0.0 copy-start.12
  91.3 0.0 copy-start.13
  91.4 0.0 copy-start.16
  91.4 0.0 copy-start.17
  91.4 0.0 copy-start.23
  91.4 0.0 copy-start.24
  91.4 9.3 %step.1 = (bf16[1152,128]{1,0:T(8,128)(2,1)S(1)}, bf16[1152,128]{1,0:T(8,128)(2,1)S(1)}) custom-call(s32[2]{0:T(128)S(1)} %pad_add_fusion.info, s32[2]{0:T(128)S(1)} %get-tuple-element.48.count, s32[6144]{0:T(1024)S(1)} %bitcast.43, f32[13824,256]{1,0:T(8,128)} %early_sums.1.partial, f8e4m3fn[4608,4096]{1,0:T(32,128)(4,1)} %tally.1.tallies, ...), custom_call_target="tpu_custom_call" | custom-call | bytes 50400000 | tf_op jit(solution)/shard_map/step/pallas_call | solution.py:705
  100.8 0.1 collective-permute-start
  100.9 1.6 %collective-permute-done.theirs = bf16[1152,128]{1,0:T(8,128)(2,1)S(1)} collective-permute-done((bf16[1152,128]{1,0:T(8,128)(2,1)S(1)}, bf16[1152,128]{1,0:T(8,128)(2,1)S(1)}, u32[]{:S(2)}, u32[]{:S(2)}) %collective-permute-start) | collective-permute-done | bytes 294944 | tf_op jit(solution)/shard_map/ppermute | solution.py:1012
  102.4 0.6 pair_sum.1
  103.1 21.3 %all_to_all.29.pieces = bf16[16,72,128]{2,1,0:T(8,128)(2,1)S(1)} all-to-all(bf16[16,72,128]{2,1,0:T(8,128)(2,1)S(1)} %bitcast.32), channel_id=1, replica_groups=mesh['chip'=2,'core'=2,'dev'=8] {'chip','dev'}, dimensions={0} | all-to-all | bytes 589824 | tf_op jit(solution)/shard_map/all_to_all | solution.py:1014
  124.3 0.6 spread_sum.1
  124.9 13.3 %all_to_all.30 = bf16[16,72,128]{2,1,0:T(8,128)(2,1)S(1)} all-to-all(bf16[16,72,128]{2,1,0:T(8,128)(2,1)S(1)} %spread_sum.1), channel_id=1, replica_groups=mesh['chip'=2,'core'=2,'dev'=8] {'chip','dev'}, dimensions={0} | all-to-all | bytes 589824 | tf_op jit(solution)/shard_map/all_to_all | solution.py:1016
  138.2 1.6 %collective-permute-done.1.theirs = bf16[1152,128]{1,0:T(8,128)(2,1)S(1)} collective-permute-done((bf16[1152,128]{1,0:T(8,128)(2,1)S(1)}, bf16[1152,128]{1,0:T(8,128)(2,1)S(1)}, u32[]{:S(2)}, u32[]{:S(2)}) %collective-permute-start.1) | collective-permute-done | bytes 294944 | tf_op jit(solution)/shard_map/ppermute | solution.py:1018
  139.9 3.9 %update.1 = (f32[1,1]{1,0:T(1,128)}, f32[2,128,256]{2,1,0:T(8,128)}, bf16[2,128,256]{2,1,0:T(8,128)(2,1)}, f32[2,128,128]{2,1,0:T(8,128)}, f32[2,256,256]{2,1,0:...) custom-call(s32[2]{0:T(128)S(1)} %pad_add_fusion.info, ...), custom_call_target="tpu_custom_call" | custom-call | bytes 14400000 | tf_op jit(solution)/shard_map/update/pallas_call | solution.py:897
  (37 shorter events, 0.1 us)
Async XLA Ops:
  2.0 14.5 %all-to-all-start = ((s32[32,1,256]{2,1,0:T(1,128)}), s32[32,1,256]{2,1,0:T(1,128)S(1)}, u32[]{:S(2)}, u32[]{:S(2)}) async-start(s32[32,1,256]{2,1,0:T(1,128)} %all_to_all.18), calls=%async_computation | async-start | bytes 65536 | tf_op jit(solution)/shard_map/all_to_all | solution.py:951
  9.3 0.7 copy-start.20
  10.1 0.7 copy-start.21
  10.8 0.7 copy-start.25
  11.5 0.7 copy-start.26
  12.2 0.7 copy-start.27
  16.5 3.4 %copy-start = (f32[16384,128]{1,0:T(8,128)S(1)}, f32[16384,128]{1,0:T(8,128)}, u32[]{:S(2)}) copy-start(f32[16384,128]{1,0:T(8,128)} %table.3) | copy-start | bytes 25165828
  25.5 18.8 %copy-start.5 = (s32[4224,15]{0,1:T(8,128)S(1)}, s32[4224,15]{0,1:T(8,128)}, u32[]{:S(2)}) copy-start(s32[4224,15]{0,1:T(8,128)} %param.31) | copy-start | bytes 760324
  25.5 18.8 %copy-start.6 = (s32[4224,15]{0,1:T(8,128)S(1)}, s32[4224,15]{0,1:T(8,128)}, u32[]{:S(2)}) copy-start(s32[4224,15]{0,1:T(8,128)} %param.34) | copy-start | bytes 760324
  25.5 32.4 %all-to-all-start.1 = ((bf16[32,128,128]{2,1,0:T(8,128)(2,1)}), bf16[32,128,128]{2,1,0:T(8,128)(2,1)S(1)}, u32[]{:S(2)}, u32[]{:S(2)}) async-start(bf16[32,128,128]{2,1,0:T(8,128)(2,1)} %bitcast.13), calls=%async_computation.1 | async-start | bytes 2097152 | tf_op jit(solution)/shard_map/all_to_all | solution.py:959
  31.2 3.4 %copy-start.1 = (f32[16384,128]{1,0:T(8,128)S(1)}, f32[16384,128]{1,0:T(8,128)}, u32[]{:S(2)}) copy-start(f32[16384,128]{1,0:T(8,128)} %table.3) | copy-start | bytes 25165828
  44.3 46.9 %copy-start.3 = (f32[2,256,256]{2,1,0:T(8,128)S(1)}, f32[2,256,256]{2,1,0:T(8,128)}, u32[]{:S(2)}) copy-start(f32[2,256,256]{2,1,0:T(8,128)} %refs_5_.3) | copy-start | bytes 1572868
  44.3 46.9 %copy-start.4 = (f32[2,256,172]{1,0,2:T(2,128)S(1)}, f32[2,256,172]{1,0,2:T(2,128)}, u32[]{:S(2)}) copy-start(f32[2,256,172]{1,0,2:T(2,128)} %param.41) | copy-start | bytes 1056772
  44.3 46.9 %copy-start.7 = (f32[2,128,256]{2,1,0:T(8,128)S(1)}, f32[2,128,256]{2,1,0:T(8,128)}, u32[]{:S(2)}) copy-start(f32[2,128,256]{2,1,0:T(8,128)} %refs_0_.1) | copy-start | bytes 786436
  44.3 46.9 %copy-start.22 = (f32[684]{0:T(1024)S(1)}, f32[684]{0:T(1024)}, u32[]{:S(2)}) copy-start(f32[684]{0:T(1024)} %biases.1) | copy-start | bytes 8212
  44.3 46.9 %copy-start.28 = (s32[64]{0:T(128)S(1)}, s32[64]{0:T(128)}, u32[]{:S(2)}) copy-start(s32[64]{0:T(128)} %refs_5_.2) | copy-start | bytes 772
  44.3 46.9 %copy-start.29 = (s32[64]{0:T(128)S(1)}, s32[64]{0:T(128)}, u32[]{:S(2)}) copy-start(s32[64]{0:T(128)} %refs_4_.2) | copy-start | bytes 772
  57.9 33.3 %copy-start.2 = (bf16[32,128,128]{2,1,0:T(8,128)(2,1)}, bf16[32,128,128]{2,1,0:T(8,128)(2,1)S(1)}, u32[]{:S(2)}) copy-start(bf16[32,128,128]{2,1,0:T(8,128)(2,1)S(1)} %all-to-all-done.1) | copy-start | bytes 3145732
  57.9 33.3 %all-to-all-start.2 = ((bf16[32,128,128]{2,1,0:T(8,128)(2,1)}), bf16[32,128,128]{2,1,0:T(8,128)(2,1)}, u32[]{:S(2)}, u32[]{:S(2)}) async-start(bf16[32,128,128]{2,1,0:T(8,128)(2,1)} %bitcast.15), calls=%async_computation.2 | async-start | bytes 2097152 | tf_op jit(solution)/shard_map/all_to_all | solution.py:959
  91.3 48.5 %copy-start.8 = (f32[2,256,256]{2,1,0:T(8,128)S(1)}, f32[2,256,256]{2,1,0:T(8,128)}, u32[]{:S(2)}) copy-start(f32[2,256,256]{2,1,0:T(8,128)} %refs_2_.1) | copy-start | bytes 1572868
  91.3 48.5 %copy-start.9 = (f32[2,256,256]{2,1,0:T(8,128)S(1)}, f32[2,256,256]{2,1,0:T(8,128)}, u32[]{:S(2)}) copy-start(f32[2,256,256]{2,1,0:T(8,128)} %refs_4_.3) | copy-start | bytes 1572868
  91.3 48.5 %copy-start.10 = (f32[2,256,256]{2,1,0:T(8,128)S(1)}, f32[2,256,256]{2,1,0:T(8,128)}, u32[]{:S(2)}) copy-start(f32[2,256,256]{2,1,0:T(8,128)} %refs_6_.3) | copy-start | bytes 1572868
  91.3 48.5 %copy-start.11 = (f32[2,256,256]{2,1,0:T(8,128)S(1)}, f32[2,256,256]{2,1,0:T(8,128)}, u32[]{:S(2)}) copy-start(f32[2,256,256]{2,1,0:T(8,128)} %refs_7_.3) | copy-start | bytes 1572868
  91.3 48.5 %copy-start.12 = (f32[2,256,256]{2,1,0:T(8,128)S(1)}, f32[2,256,256]{2,1,0:T(8,128)}, u32[]{:S(2)}) copy-start(f32[2,256,256]{2,1,0:T(8,128)} %refs_8_.1) | copy-start | bytes 1572868
  91.3 48.5 %copy-start.13 = (f32[2,256,256]{2,1,0:T(8,128)S(1)}, f32[2,256,256]{2,1,0:T(8,128)}, u32[]{:S(2)}) copy-start(f32[2,256,256]{2,1,0:T(8,128)} %refs_9_.3) | copy-start | bytes 1572868
  91.3 48.5 %copy-start.14 = (f32[2,256,256]{2,1,0:T(8,128)S(1)}, f32[2,256,256]{2,1,0:T(8,128)}, u32[]{:S(2)}) copy-start(f32[2,256,256]{2,1,0:T(8,128)} %refs_12_.1) | copy-start | bytes 1572868
  91.4 48.5 %copy-start.15 = (f32[2,256,256]{2,1,0:T(8,128)S(1)}, f32[2,256,256]{2,1,0:T(8,128)}, u32[]{:S(2)}) copy-start(f32[2,256,256]{2,1,0:T(8,128)} %refs_14_.1) | copy-start | bytes 1572868
  91.4 48.5 %copy-start.16 = (f32[2,172,172]{2,0,1:T(2,128)S(1)}, f32[2,172,172]{2,0,1:T(2,128)}, u32[]{:S(2)}) copy-start(f32[2,172,172]{2,0,1:T(2,128)} %param.51) | copy-start | bytes 710020
  91.4 48.5 %copy-start.17 = (f32[2,172,172]{2,0,1:T(2,128)S(1)}, f32[2,172,172]{2,0,1:T(2,128)}, u32[]{:S(2)}) copy-start(f32[2,172,172]{2,0,1:T(2,128)} %param.57) | copy-start | bytes 710020
  91.4 48.5 %copy-start.18 = (f32[2,128,128]{2,1,0:T(8,128)S(1)}, f32[2,128,128]{2,1,0:T(8,128)}, u32[]{:S(2)}) copy-start(f32[2,128,128]{2,1,0:T(8,128)} %refs_1_.1) | copy-start | bytes 393220
  91.4 48.5 %copy-start.19 = (f32[2,128,128]{2,1,0:T(8,128)S(1)}, f32[2,128,128]{2,1,0:T(8,128)}, u32[]{:S(2)}) copy-start(f32[2,128,128]{2,1,0:T(8,128)} %refs_3_.1) | copy-start | bytes 393220
  91.4 48.5 %copy-start.23 = (f32[684]{0:T(1024)S(1)}, f32[684]{0:T(1024)}, u32[]{:S(2)}) copy-start(f32[684]{0:T(1024)} %moment_one.1) | copy-start | bytes 8212
  91.4 48.5 %copy-start.24 = (f32[684]{0:T(1024)S(1)}, f32[684]{0:T(1024)}, u32[]{:S(2)}) copy-start(f32[684]{0:T(1024)} %moment_two.1) | copy-start | bytes 8212
  100.8 1.6 %collective-permute-start = (bf16[1152,128]{1,0:T(8,128)(2,1)S(1)}, bf16[1152,128]{1,0:T(8,128)(2,1)S(1)}, u32[]{:S(2)}, u32[]{:S(2)}) collective-permute-start(bf16[1152,128]{1,0:T(8,128)(2,1)S(1)} %get-tuple-element.59), channel_id=1, source_target_pairs={{0,8},{8,0},{1,9},{9,1},{2,10},{10,2},{3,11},{11,3},{4,12},{12,4},... | collective-permute-start | bytes 884744 | tf_op jit(solution)/shard_map/ppermute | solution.py:1012
  138.2 1.6 %collective-permute-start.1 = (bf16[1152,128]{1,0:T(8,128)(2,1)S(1)}, bf16[1152,128]{1,0:T(8,128)(2,1)S(1)}, u32[]{:S(2)}, u32[]{:S(2)}) collective-permute-start(bf16[1152,128]{1,0:T(8,128)(2,1)S(1)} %bitcast.30), channel_id=1, source_target_pairs={{0,8},{8,0},{1,9},{9,1},{2,10},{10,2},{3,11},{11,3},{4,12},{12,4},... | collective-permute-start | bytes 884744 | tf_op jit(solution)/shard_map/ppermute | solution.py:1018

commit v2 on v1

--- a/solution.py
+++ b/solution.py
@@ -83,30 +83,46 @@
     return (0, per // 2), (per // 2, per)
 
 
-def pick_kernel(wanted, table, out, rows, *, first, last, per):
-    part = last - first
-
-    def body(device, carry):
-        for u in range(part):
-            name = wanted[device * per + (first + u)]
-            rows[pl.ds(device * part + u, 1), :] = table[pl.ds(name, 1), :]
+def pick_kernel(wanted, table, out, rows, done, sems, *, first, part, per):
+    chunk = rows.shape[0]
+    devices = chunk // part
+
+    def save(step):
+        where = pl.ds(pl.multiple_of(step * chunk, chunk), chunk)
+        return pltpu.make_async_copy(done.at[where, :], out.at[where, :], sems.at[step])
+
+    def body(step, carry):
+        for d in range(devices):
+            base = (step * devices + d) * per + first
+            for u in range(part):
+                at = d * part + u
+                rows[at : at + 1, :] = table[pl.ds(wanted[base + u], 1), :]
+        where = pl.ds(pl.multiple_of(step * chunk, chunk), chunk)
+        done[where, :] = rows[...].astype(jnp.bfloat16)
+        save(step).start()
         return carry
 
-    lax.fori_loop(0, out.shape[0] // part, body, 0)
-    out[...] = rows[...].astype(jnp.bfloat16)
+    lax.fori_loop(0, out.shape[0] // chunk, body, 0)
+    for step in range(out.shape[0] // chunk):
+        save(step).wait()
 
 
 def pick_rows(wanted, table, per, ends):
     first, last = ends
     width = table.shape[1]
     count = wanted.shape[0] // per * (last - first)
+    chunk = 512
     return call(
-        functools.partial(pick_kernel, first=first, last=last, per=per),
+        functools.partial(pick_kernel, first=first, part=last - first, per=per),
         "pick_rows",
         jax.ShapeDtypeStruct((count, width), jnp.bfloat16),
         [smem, vmem],
-        vmem,
-        [pltpu.VMEM((count, width), jnp.float32)],
+        anywhere,
+        [
+            pltpu.VMEM((chunk, width), jnp.float32),
+            pltpu.VMEM((count, width), jnp.bfloat16),
+            pltpu.SemaphoreType.DMA((count // chunk,)),
+        ],
         4.6,
         20 << 20,
     )(wanted, table)
@@ -187,7 +203,7 @@
     order = (before + running - full).astype(jnp.int32)
     number = jnp.sum(flag).astype(jnp.int32)
     count[0] = number
-    count[1] = 2 * lax.div(number + (2 * SPAN - 1), 2 * SPAN)
+    count[1] = lax.div(number + (SPAN - 1), SPAN)
 
     high = jnp.where(full > 0.0, lax.shift_right_arithmetic(order, 7), -1)
     rest = jnp.transpose((order & (LANES - 1)).astype(jnp.float32)).astype(jnp.int32)
@@ -498,6 +514,7 @@
     early,
     hid,
     down_low,
+    bias_sums,
     link,
     sems,
     link_sems,
@@ -520,20 +537,29 @@
     low = jnp.bfloat16
     width = sources[0].shape[1]
 
-    def load(pair, slot):
-        rows = pl.ds(pl.multiple_of(pair * 2 * SPAN, 2 * SPAN), 2 * SPAN)
+    def load(pair, slot, size):
+        rows = pl.ds(pl.multiple_of(pair * 2 * SPAN, 2 * SPAN), size)
+        here = pl.ds(0, size)
         return (
-            pltpu.make_async_copy(tallies.at[rows, :], late.at[slot], sems.at[slot, 0]),
-            pltpu.make_async_copy(partial.at[rows, :], early.at[slot], sems.at[slot, 1]),
+            pltpu.make_async_copy(tallies.at[rows, :], late.at[slot, here, :], sems.at[slot, 0]),
+            pltpu.make_async_copy(partial.at[rows, :], early.at[slot, here, :], sems.at[slot, 1]),
         )
+
+    def start_load(pair, slot):
+        @pl.when(2 * pair + 1 < used)
+        def _():
+            for copy in load(pair, slot, 2 * SPAN):
+                copy.start()
+
+        @pl.when(2 * pair + 1 == used)
+        def _():
+            for copy in load(pair, slot, SPAN):
+                copy.start()
 
     def load_link(block):
         return pltpu.make_async_copy(links.at[block], link.at[block], link_sems.at[block])
 
-    @pl.when(used > 0)
-    def _():
-        for copy in load(0, 0):
-            copy.start()
+    start_load(0, 0)
 
     def start_link(block, carry):
         load_link(block).start()
@@ -564,44 +590,56 @@
 
     sums[...] = jnp.zeros_like(sums)
 
-    def paired(block):
+    def paired(block, size):
+        if size == SPAN:
+            return link[block]
         return jnp.concatenate([link[block], link[block + 1]], axis=1)
 
-    def forward(pair, carry):
-        rows = pl.ds(pl.multiple_of(pair * 2 * SPAN, 2 * SPAN), 2 * SPAN)
+    def forward(pair, size):
+        base = pair * 2 * SPAN
+        rows = pl.ds(pl.multiple_of(base, 2 * SPAN), size)
         slot = lax.rem(pair, 2)
-        for copy in load(pair, slot):
+        for copy in load(pair, slot, size):
             copy.wait()
-        load_link(2 * pair).wait()
-        load_link(2 * pair + 1).wait()
-
-        @pl.when(2 * pair + 2 < used)
-        def _():
-            for copy in load(pair + 1, 1 - slot):
-                copy.start()
-
-        copy_rows(places, pair * 2 * SPAN, 2 * SPAN, own_table, own_rows)
-        joined[...] = dot(late[slot].astype(low), late_table[...]) + early[slot]
-        mixin[rows, 0:width] = own_rows[...].astype(low)
+        for step in range(size // SPAN):
+            load_link(2 * pair + step).wait()
+        start_load(pair + 1, 1 - slot)
+        for part in range(0, size, SPAN):
+            for u in range(part, part + SPAN):
+                own_rows[u : u + 1, :] = own_table[pl.ds(places[base + u], 1), :]
+            here = slice(part, part + SPAN)
+            joined[here, :] = dot(late[slot, here, :].astype(low), late_table[...]) + (
+                early[slot, here, :]
+            )
+        mixin[rows, 0:width] = own_rows[0:size, :].astype(low)
         mixin[rows, width:] = (
-            joined[:, 0:width] / jnp.maximum(joined[:, width:], 1.0)
+            joined[0:size, 0:width] / jnp.maximum(joined[0:size, width:], 1.0)
         ).astype(low)
         z = dot(mixin[rows, :], w_in) + bias_in
         s = 1.0 / (1.0 + jnp.exp(-z))
         slopes[rows, :] = s * (1.0 + z * (1.0 - s))
-        hid[...] = (z * s).astype(low)
-        sums[0:targets, :] += dot(paired(2 * pair), hid[...])
+        hid[0:size, :] = (z * s).astype(low)
+        sums[0:targets, :] += dot(paired(2 * pair, size), hid[0:size, :])
 
         @pl.when(pair == 0)
         def _():
             for block in range(2):
                 load_link(own_link + block).wait()
-            sums[targets:, :] = dot(paired(own_link), hid[...])
-
+            sums[targets:, :] = dot(paired(own_link, size), hid[0:size, :])
+
+    pairs = lax.div(used, 2)
+    odd = lax.rem(used, 2) == 1
+
+    def forward_pair(pair, carry):
+        forward(pair, 2 * SPAN)
         return carry
 
-    pairs = lax.div(used, 2)
-    lax.fori_loop(0, pairs, forward, 0)
+    lax.fori_loop(0, pairs, forward_pair, 0)
+
+    @pl.when(odd)
+    def _():
+        forward(pairs, SPAN)
+
     total = sums[...]
     counts_two = clipped_counts(near_two[...] >= 0)
     mixed_one = (total[0:targets] / counts_two).astype(low)
@@ -657,20 +695,31 @@
 
     weight_sums[...] = jnp.zeros_like(weight_sums)
 
-    def backward(pair, bias):
-        rows = pl.ds(pl.multiple_of(pair * 2 * SPAN, 2 * SPAN), 2 * SPAN)
-        joined[...] = dot_rows(paired(2 * pair), down_low[0:targets, :])
+    bias_sums[...] = jnp.zeros_like(bias_sums)
+
+    def backward(pair, size):
+        rows = pl.ds(pl.multiple_of(pair * 2 * SPAN, 2 * SPAN), size)
+        joined[0:size, :] = dot_rows(paired(2 * pair, size), down_low[0:targets, :])
 
         @pl.when(pair == 0)
         def _():
-            joined[...] += dot_rows(paired(own_link), down_low[targets:, :])
-
-        grad = (joined[...] * slopes[rows, :]).astype(low)
+            joined[0:size, :] += dot_rows(paired(own_link, size), down_low[targets:, :])
+
+        grad = (joined[0:size, :] * slopes[rows, :]).astype(low)
         weight_sums[...] += dot_rows(mixin[rows, :], grad)
-        return bias + jnp.sum(grad.astype(jnp.float32), axis=0, keepdims=True)
-
-    bias_grad_in = lax.fori_loop(0, pairs, backward, jnp.zeros((1, hidden), jnp.float32))
-
+        bias_sums[0:1, :] += jnp.sum(grad.astype(jnp.float32), axis=0, keepdims=True)
+
+    def backward_pair(pair, carry):
+        backward(pair, 2 * SPAN)
+        return carry
+
+    lax.fori_loop(0, pairs, backward_pair, 0)
+
+    @pl.when(odd)
+    def _():
+        backward(pairs, SPAN)
+
+    bias_grad_in = bias_sums[0:1, :]
     row = 0
     for part in (weight_sums, mid_sums):
         for column in range(0, hidden, LANES):
@@ -724,6 +773,7 @@
             pltpu.VMEM((2, 2 * SPAN, 2 * width), jnp.float32),
             pltpu.VMEM((2 * SPAN, hidden), jnp.bfloat16),
             pltpu.VMEM((2 * targets, hidden), jnp.bfloat16),
+            pltpu.VMEM((8, hidden), jnp.float32),
             pltpu.VMEM((blocks + 2, targets, SPAN), jnp.bfloat16),
             pltpu.SemaphoreType.DMA((2, 2)),
             pltpu.SemaphoreType.DMA((blocks + 2,)),
@@ -791,9 +841,15 @@
 ):
     groups = [refs[5 * k : 5 * k + 5] for k in range(3)]
     loss_out = refs[15]
-    outs = [refs[16 + 4 * k : 20 + 4 * k] for k in range(3)]
+    finals = refs[16:28]
     bias_out, first_out, second_out = refs[28:31]
-    packed = refs[31]
+    packed, sems = refs[31:33]
+    held = refs[33:45]
+    outs = [held[4 * k : 4 * k + 4] for k in range(3)]
+    copies = [
+        pltpu.make_async_copy(source, final, sems.at[k])
+        for k, (source, final) in enumerate(zip(held, finals))
+    ]
     low = jnp.bfloat16
     half = mine.shape[0]
     core = info[0]
@@ -807,8 +863,16 @@
     loss_out[...] = extra[6:7, 0:1] / counted
     scale = 0.5 * inverse * inverse
 
-    row = 0
+    starts, row = [], 0
     for group in range(3):
+        master = groups[group][0]
+        starts.append(row)
+        if group == 2:
+            row += up(master.shape[0], 16) * 2 * (master.shape[2] // LANES)
+        else:
+            row += 2 * master.shape[1] * (master.shape[2] // LANES)
+    for group in (1, 2, 0):
+        row = starts[group]
         master, left, right, left_root, right_root = groups[group]
         new_master, copy, new_left, new_right = outs[group]
         turned = group == 2
@@ -864,6 +928,8 @@
             )[0:depth]
             put(new_master, k, turned, take(master, k, turned) - inverse * way)
         copy[...] = new_master[...].astype(low)
+        for which in range(4):
+            copies[4 * group + which].start()
 
     size = biases.shape[0]
     grad = jnp.concatenate([extra[k : k + 1, :] for k in range(6)], axis=1)[:, 0:size]
@@ -880,6 +946,8 @@
     )
     for ref, value in ((bias_out, fresh), (first_out, first), (second_out, second)):
         ref[...] = value[0]
+    for copy in copies:
+        copy.wait()
 
 
 def run_update(info, fixes, mine, theirs, vectors, groups):
@@ -899,8 +967,12 @@
         "update",
         tuple(outs),
         [smem] * 2 + [vmem] * (5 + len(flat)),
-        (vmem,) * len(outs),
-        [pltpu.VMEM((2 * mine.shape[0], LANES), jnp.bfloat16)],
+        (vmem,) + (anywhere,) * 12 + (vmem,) * 3,
+        [
+            pltpu.VMEM((2 * mine.shape[0], LANES), jnp.bfloat16),
+            pltpu.SemaphoreType.DMA((12,)),
+        ]
+        + [pltpu.VMEM(item.shape, item.dtype) for item in outs[1:13]],
         4.0,
         16 << 20,
     )(info, fixes, mine, theirs, *vectors, *flat)

time: 145 us -> 142 us (0.979)
  Pallas kernels: 43.7 us -> 38.8 us
  waiting for transfers between devices: 33.9 us -> 37.6 us
    all_to_all x2, waiting for transfers between devices: 29.8 us -> 33.8 us  [trade(): lax.all_to_all(found.reshape(devices, -1, width), AXES, split_axis=0, con...]
    pallas_call x2, Pallas kernels: 11.3 us -> 8.23 us  [tally(): call(functools.partial(tally_kernel, per=per, which=which), 'early_sums'...]
    all_to_all x2, starting transfers between devices: 10.6 us -> 8.21 us  [trade(): lax.all_to_all(found.reshape(devices, -1, width), AXES, split_axis=0, con...]
    pallas_call x1, Pallas kernels: 9.33 us -> 7.81 us  [run_step(): call(functools.partial(step_kernel, classes=classes), 'step', (jax.ShapeD...]
  transfers between devices with their start and end apart: 5 -> 5, of which waited for: 5 -> 5; matrix products, arithmetic and copies ran while one was open for 0% -> 0% of each run, Pallas kernels for 16% -> 14%
where the time goes in v2:
time: 142 us
  Pallas kernels  38.8 us (27%)
  waiting for transfers between devices  37.6 us (26%)
  blocking collectives  35 us (25%)
  starting transfers between devices  16.7 us (12%)
  local copies, waits for them, and re-layouts  11.8 us (8%)
  between operations  1.98 us (1%)
    all_to_all x2, waiting for transfers between devices, trade(): lax.all_to_all(found.reshape(devices, -1, width), AXES, split_axis=0, con...  33.8 us
    all_to_all x1, blocking collectives, body(): lax.all_to_all(summed, PEERS, split_axis=0, concat_axis=0, tiled=True)  21.7 us
    all_to_all x1, blocking collectives, body(): lax.all_to_all(shared, PEERS, split_axis=0, concat_axis=0, tiled=True)  13.3 us
    unnamed x60, local copies, waits for them, and re-layouts  10.4 us
    pallas_call x2, Pallas kernels, pick_rows(): call(functools.partial(pick_kernel, first=first, part=last - first, per=p...  10.3 us
    pallas_call x2, Pallas kernels, tally(): call(functools.partial(tally_kernel, per=per, which=which), 'early_sums'...  8.23 us
    all_to_all x2, starting transfers between devices, trade(): lax.all_to_all(found.reshape(devices, -1, width), AXES, split_axis=0, con...  8.21 us
    pallas_call x1, Pallas kernels, run_step(): call(functools.partial(step_kernel, classes=classes), 'step', (jax.ShapeD...  7.81 us
  transfers between devices with their start and end apart: 5, of which 5 were waited for; matrix products, arithmetic and copies ran while one was open for 0% of the time, Pallas kernels for 14%

profile of v2, /device:TPU:0, one launch (start us, length us, event | category | flops | bytes accessed | tf_op | source)
XLA Modules:
  0.0 142.1 jit_solution(13503798475284322411)
XLA Ops:
  0.6 1.4 all_to_all.18
  2.0 7.3 %all-to-all-start = ((s32[32,1,256]{2,1,0:T(1,128)}), s32[32,1,256]{2,1,0:T(1,128)S(1)}, u32[]{:S(2)}, u32[]{:S(2)}) async-start(s32[32,1,256]{2,1,0:T(1,128)} %all_to_all.18), calls=%async_computation | async-start | bytes 65536 | tf_op jit(solution)/shard_map/all_to_all | solution.py:1023
  9.3 0.0 copy-start.20
  9.4 0.7 copy-done.20
  10.1 0.7 copy-done.21
  10.8 0.7 copy-done.25
  11.5 0.7 copy-done.26
  12.2 0.7 copy-done.27
  12.9 2.6 %reach.1 = (s32[48,128]{1,0:T(8,128)S(1)}, s32[48,128]{1,0:T(8,128)S(1)}, s32[384,16]{1,0:T(8,128)S(1)}, s32[64,8]{1,0:T(8,128)S(1)}, s32[2]{0:T(128)S(1)}) custom-call(s32[5,64]{1,0:T(8,128)S(1)} %bitcast.46, s32[5,64]{1,0:T(8,128)S(1)} %bitcast.47, s32[64]{0:T(128)S(1)} %copy-done.27, s32[10,384]{1,0:T(8,128)S(1)} %bitcast.44, s32[10,384]{1,0:T(8,128)S(1)} %bitcast.45), custom_call_target="tpu_custom_call" | custom-call | bytes 10800000 | tf_op jit(solution)/shard_map/reach/pallas_call | solution.py:237
  15.5 1.0 all-to-all-done
  16.5 3.4 %copy-done = f32[16384,128]{1,0:T(8,128)S(1)} copy-done((f32[16384,128]{1,0:T(8,128)S(1)}, f32[16384,128]{1,0:T(8,128)}, u32[]{:S(2)}) %copy-start) | copy-done | bytes 8388632
  19.9 5.2 %pick_rows.3 = bf16[4096,128]{1,0:T(8,128)(2,1)} custom-call(s32[8192]{0:T(1024)S(1)} %bitcast.39, f32[16384,128]{1,0:T(8,128)S(1)} %copy-done), custom_call_target="tpu_custom_call" | custom-call | bytes 16559999 | tf_op jit(solution)/shard_map/pick_rows/pallas_call | solution.py:115
  25.1 0.0 copy-start.5
  25.1 0.0 copy-start.6
  25.1 4.8 %all-to-all-start.1 = ((bf16[32,128,128]{2,1,0:T(8,128)(2,1)}), bf16[32,128,128]{2,1,0:T(8,128)(2,1)S(1)}, u32[]{:S(2)}, u32[]{:S(2)}) async-start(bf16[32,128,128]{2,1,0:T(8,128)(2,1)} %bitcast.13), calls=%async_computation.1 | async-start | bytes 2097152 | tf_op jit(solution)/shard_map/all_to_all | solution.py:1031
  30.7 0.1 pad_add_fusion.info
  30.8 0.1 pad_maximum_fusion.fixes
  30.8 3.4 %copy-done.1 = f32[16384,128]{1,0:T(8,128)S(1)} copy-done((f32[16384,128]{1,0:T(8,128)S(1)}, f32[16384,128]{1,0:T(8,128)}, u32[]{:S(2)}) %copy-start.1) | copy-done | bytes 8388632
  34.2 5.1 %pick_rows.2 = bf16[4096,128]{1,0:T(8,128)(2,1)} custom-call(s32[8192]{0:T(1024)S(1)} %bitcast.40, f32[16384,128]{1,0:T(8,128)S(1)} %copy-done.1), custom_call_target="tpu_custom_call" | custom-call | bytes 16559999 | tf_op jit(solution)/shard_map/pick_rows/pallas_call | solution.py:115
  39.4 3.6 %link_matrix.1.links = bf16[72,384,256]{2,1,0:T(8,128)(2,1)} custom-call(s32[2]{0:T(128)S(1)} %get-tuple-element.48.count, s32[48,128]{1,0:T(8,128)S(1)} %get-tuple-element.49.names, s32[384,16]{1,0:T(8,128)S(1)} %get-tuple-element.50.near.refs_2_), custom_call_target="tpu_custom_call" | custom-call | bytes 18000000 | tf_op jit(solution)/shard_map/link_matrix/pallas_call | solution.py:452
  43.0 0.0 copy-start.3
  43.0 0.0 copy-start.4
  43.0 0.0 copy-start.7
  43.0 0.0 copy-start.22
  43.0 0.0 copy-start.28
  43.0 0.0 copy-start.29
  43.1 3.5 %tally.1.tallies = f8e4m3fn[4608,4096]{1,0:T(32,128)(4,1)} custom-call(s32[2]{0:T(128)S(1)} %get-tuple-element.48.count, s32[6144]{0:T(1024)S(1)} %bitcast.41, s32[15,4224]{1,0:T(8,128)S(1)} %bitcast.33, s32[15,4224]{1,0:T(8,128)S(1)} %bitcast.35), custom_call_target="tpu_custom_call" | custom-call | bytes 50400000 | tf_op jit(solution)/shard_map/tally/pallas_call | solution.py:383
  46.6 10.9 %all-to-all-done.1 = bf16[32,128,128]{2,1,0:T(8,128)(2,1)S(1)} async-done(((bf16[32,128,128]{2,1,0:T(8,128)(2,1)}), bf16[32,128,128]{2,1,0:T(8,128)(2,1)S(1)}, u32[]{:S(2)}, u32[]{:S(2)}) %all-to-all-start.1) | async-done | bytes 1048608 | tf_op jit(solution)/shard_map/all_to_all | solution.py:1031
  57.5 3.4 %all-to-all-start.2 = ((bf16[32,128,128]{2,1,0:T(8,128)(2,1)}), bf16[32,128,128]{2,1,0:T(8,128)(2,1)}, u32[]{:S(2)}, u32[]{:S(2)}) async-start(bf16[32,128,128]{2,1,0:T(8,128)(2,1)} %bitcast.15), calls=%async_computation.2 | async-start | bytes 2097152 | tf_op jit(solution)/shard_map/all_to_all | solution.py:1031
  60.9 4.7 %early_sums.1.partial = f32[13824,256]{1,0:T(8,128)} custom-call(s32[2]{0:T(128)S(1)} %get-tuple-element.48.count, s32[6144]{0:T(1024)S(1)} %bitcast.42, s32[15,4224]{1,0:T(8,128)S(1)} %bitcast.34, s32[15,4224]{1,0:T(8,128)S(1)} %bitcast.36, bf16[4096,128]{1,0:T(8,128)(2,1)S(1)} %bitcast.26), custom_call_target="tpu_custom_call" | custom-call | bytes 50400000 | tf_op jit(solution)/shard_map/early_sums/pallas_call | solution.py:383
  65.6 22.9 %all-to-all-done.2 = bf16[32,128,128]{2,1,0:T(8,128)(2,1)} async-done(((bf16[32,128,128]{2,1,0:T(8,128)(2,1)}), bf16[32,128,128]{2,1,0:T(8,128)(2,1)}, u32[]{:S(2)}, u32[]{:S(2)}) %all-to-all-start.2) | async-done | bytes 1048608 | tf_op jit(solution)/shard_map/all_to_all | solution.py:1031
  88.5 0.0 copy-start.8
  88.6 0.0 copy-start.9
  88.6 0.0 copy-start.11
  88.6 0.0 copy-start.12
  88.6 0.0 copy-start.15
  88.6 0.0 copy-start.16
  88.7 0.0 copy-start.19
  88.7 0.0 copy-start.23
  88.7 7.8 %step.1 = (bf16[1152,128]{1,0:T(8,128)(2,1)S(1)}, bf16[1152,128]{1,0:T(8,128)(2,1)S(1)}) custom-call(s32[2]{0:T(128)S(1)} %pad_add_fusion.info, s32[2]{0:T(128)S(1)} %get-tuple-element.48.count, s32[6144]{0:T(1024)S(1)} %bitcast.43, f32[13824,256]{1,0:T(8,128)} %early_sums.1.partial, f8e4m3fn[4608,4096]{1,0:T(32,128)(4,1)} %tally.1.tallies, ...), custom_call_target="tpu_custom_call" | custom-call | bytes 50400000 | tf_op jit(solution)/shard_map/step/pallas_call | solution.py:754
  96.5 1.2 collective-permute-start
  97.7 1.2 collective-permute-done.theirs
  98.9 0.6 pair_sum.1
  99.6 21.7 %all_to_all.29.pieces = bf16[16,72,128]{2,1,0:T(8,128)(2,1)S(1)} all-to-all(bf16[16,72,128]{2,1,0:T(8,128)(2,1)S(1)} %bitcast.32), channel_id=1, replica_groups=mesh['chip'=2,'core'=2,'dev'=8] {'chip','dev'}, dimensions={0} | all-to-all | bytes 589824 | tf_op jit(solution)/shard_map/all_to_all | solution.py:1086
  121.3 0.6 spread_sum.1
  121.9 13.3 %all_to_all.30 = bf16[16,72,128]{2,1,0:T(8,128)(2,1)S(1)} all-to-all(bf16[16,72,128]{2,1,0:T(8,128)(2,1)S(1)} %spread_sum.1), channel_id=1, replica_groups=mesh['chip'=2,'core'=2,'dev'=8] {'chip','dev'}, dimensions={0} | all-to-all | bytes 589824 | tf_op jit(solution)/shard_map/all_to_all | solution.py:1088
  135.2 1.6 %collective-permute-done.1.theirs = bf16[1152,128]{1,0:T(8,128)(2,1)S(1)} collective-permute-done((bf16[1152,128]{1,0:T(8,128)(2,1)S(1)}, bf16[1152,128]{1,0:T(8,128)(2,1)S(1)}, u32[]{:S(2)}, u32[]{:S(2)}) %collective-permute-start.1) | collective-permute-done | bytes 294944 | tf_op jit(solution)/shard_map/ppermute | solution.py:1090
  136.9 5.0 %update.1 = (f32[1,1]{1,0:T(1,128)}, f32[2,128,256]{2,1,0:T(8,128)}, bf16[2,128,256]{2,1,0:T(8,128)(2,1)}, f32[2,128,128]{2,1,0:T(8,128)}, f32[2,256,256]{2,1,0:...) custom-call(s32[2]{0:T(128)S(1)} %pad_add_fusion.info, ...), custom_call_target="tpu_custom_call" | custom-call | bytes 14400000 | tf_op jit(solution)/shard_map/update/pallas_call | solution.py:965
  (37 shorter events, 0.1 us)
Async XLA Ops:
  2.0 14.5 %all-to-all-start = ((s32[32,1,256]{2,1,0:T(1,128)}), s32[32,1,256]{2,1,0:T(1,128)S(1)}, u32[]{:S(2)}, u32[]{:S(2)}) async-start(s32[32,1,256]{2,1,0:T(1,128)} %all_to_all.18), calls=%async_computation | async-start | bytes 65536 | tf_op jit(solution)/shard_map/all_to_all | solution.py:1023
  9.3 0.7 copy-start.20
  10.1 0.7 copy-start.21
  10.8 0.7 copy-start.25
  11.5 0.7 copy-start.26
  12.2 0.7 copy-start.27
  16.5 3.4 %copy-start = (f32[16384,128]{1,0:T(8,128)S(1)}, f32[16384,128]{1,0:T(8,128)}, u32[]{:S(2)}) copy-start(f32[16384,128]{1,0:T(8,128)} %table.3) | copy-start | bytes 25165828
  25.1 17.9 %copy-start.5 = (s32[4224,15]{0,1:T(8,128)S(1)}, s32[4224,15]{0,1:T(8,128)}, u32[]{:S(2)}) copy-start(s32[4224,15]{0,1:T(8,128)} %param.31) | copy-start | bytes 760324
  25.1 17.9 %copy-start.6 = (s32[4224,15]{0,1:T(8,128)S(1)}, s32[4224,15]{0,1:T(8,128)}, u32[]{:S(2)}) copy-start(s32[4224,15]{0,1:T(8,128)} %param.34) | copy-start | bytes 760324
  25.1 32.4 %all-to-all-start.1 = ((bf16[32,128,128]{2,1,0:T(8,128)(2,1)}), bf16[32,128,128]{2,1,0:T(8,128)(2,1)S(1)}, u32[]{:S(2)}, u32[]{:S(2)}) async-start(bf16[32,128,128]{2,1,0:T(8,128)(2,1)} %bitcast.13), calls=%async_computation.1 | async-start | bytes 2097152 | tf_op jit(solution)/shard_map/all_to_all | solution.py:1031
  30.8 3.4 %copy-start.1 = (f32[16384,128]{1,0:T(8,128)S(1)}, f32[16384,128]{1,0:T(8,128)}, u32[]{:S(2)}) copy-start(f32[16384,128]{1,0:T(8,128)} %table.3) | copy-start | bytes 25165828
  43.0 45.5 %copy-start.3 = (f32[2,256,256]{2,1,0:T(8,128)S(1)}, f32[2,256,256]{2,1,0:T(8,128)}, u32[]{:S(2)}) copy-start(f32[2,256,256]{2,1,0:T(8,128)} %refs_5_.3) | copy-start | bytes 1572868
  43.0 45.5 %copy-start.4 = (f32[2,256,172]{1,0,2:T(2,128)S(1)}, f32[2,256,172]{1,0,2:T(2,128)}, u32[]{:S(2)}) copy-start(f32[2,256,172]{1,0,2:T(2,128)} %param.41) | copy-start | bytes 1056772
  43.0 45.5 %copy-start.7 = (f32[2,128,256]{2,1,0:T(8,128)S(1)}, f32[2,128,256]{2,1,0:T(8,128)}, u32[]{:S(2)}) copy-start(f32[2,128,256]{2,1,0:T(8,128)} %refs_0_.1) | copy-start | bytes 786436
  43.0 45.5 %copy-start.22 = (f32[684]{0:T(1024)S(1)}, f32[684]{0:T(1024)}, u32[]{:S(2)}) copy-start(f32[684]{0:T(1024)} %biases.1) | copy-start | bytes 8212
  43.0 45.5 %copy-start.28 = (s32[64]{0:T(128)S(1)}, s32[64]{0:T(128)}, u32[]{:S(2)}) copy-start(s32[64]{0:T(128)} %refs_5_.2) | copy-start | bytes 772
  43.0 45.5 %copy-start.29 = (s32[64]{0:T(128)S(1)}, s32[64]{0:T(128)}, u32[]{:S(2)}) copy-start(s32[64]{0:T(128)} %refs_4_.2) | copy-start | bytes 772
  57.5 31.0 %copy-start.2 = (bf16[32,128,128]{2,1,0:T(8,128)(2,1)}, bf16[32,128,128]{2,1,0:T(8,128)(2,1)S(1)}, u32[]{:S(2)}) copy-start(bf16[32,128,128]{2,1,0:T(8,128)(2,1)S(1)} %all-to-all-done.1) | copy-start | bytes 3145732
  57.5 31.0 %all-to-all-start.2 = ((bf16[32,128,128]{2,1,0:T(8,128)(2,1)}), bf16[32,128,128]{2,1,0:T(8,128)(2,1)}, u32[]{:S(2)}, u32[]{:S(2)}) async-start(bf16[32,128,128]{2,1,0:T(8,128)(2,1)} %bitcast.15), calls=%async_computation.2 | async-start | bytes 2097152 | tf_op jit(solution)/shard_map/all_to_all | solution.py:1031
  88.5 48.3 %copy-start.8 = (f32[2,256,256]{2,1,0:T(8,128)S(1)}, f32[2,256,256]{2,1,0:T(8,128)}, u32[]{:S(2)}) copy-start(f32[2,256,256]{2,1,0:T(8,128)} %refs_2_.1) | copy-start | bytes 1572868
  88.6 48.2 %copy-start.9 = (f32[2,256,256]{2,1,0:T(8,128)S(1)}, f32[2,256,256]{2,1,0:T(8,128)}, u32[]{:S(2)}) copy-start(f32[2,256,256]{2,1,0:T(8,128)} %refs_4_.3) | copy-start | bytes 1572868
  88.6 48.2 %copy-start.10 = (f32[2,256,256]{2,1,0:T(8,128)S(1)}, f32[2,256,256]{2,1,0:T(8,128)}, u32[]{:S(2)}) copy-start(f32[2,256,256]{2,1,0:T(8,128)} %refs_6_.3) | copy-start | bytes 1572868
  88.6 48.2 %copy-start.11 = (f32[2,256,256]{2,1,0:T(8,128)S(1)}, f32[2,256,256]{2,1,0:T(8,128)}, u32[]{:S(2)}) copy-start(f32[2,256,256]{2,1,0:T(8,128)} %refs_7_.3) | copy-start | bytes 1572868
  88.6 48.2 %copy-start.12 = (f32[2,256,256]{2,1,0:T(8,128)S(1)}, f32[2,256,256]{2,1,0:T(8,128)}, u32[]{:S(2)}) copy-start(f32[2,256,256]{2,1,0:T(8,128)} %refs_8_.1) | copy-start | bytes 1572868
  88.6 48.2 %copy-start.13 = (f32[2,256,256]{2,1,0:T(8,128)S(1)}, f32[2,256,256]{2,1,0:T(8,128)}, u32[]{:S(2)}) copy-start(f32[2,256,256]{2,1,0:T(8,128)} %refs_9_.3) | copy-start | bytes 1572868
  88.6 48.2 %copy-start.14 = (f32[2,256,256]{2,1,0:T(8,128)S(1)}, f32[2,256,256]{2,1,0:T(8,128)}, u32[]{:S(2)}) copy-start(f32[2,256,256]{2,1,0:T(8,128)} %refs_12_.1) | copy-start | bytes 1572868
  88.6 48.2 %copy-start.15 = (f32[2,256,256]{2,1,0:T(8,128)S(1)}, f32[2,256,256]{2,1,0:T(8,128)}, u32[]{:S(2)}) copy-start(f32[2,256,256]{2,1,0:T(8,128)} %refs_14_.1) | copy-start | bytes 1572868
  88.6 48.2 %copy-start.16 = (f32[2,172,172]{2,0,1:T(2,128)S(1)}, f32[2,172,172]{2,0,1:T(2,128)}, u32[]{:S(2)}) copy-start(f32[2,172,172]{2,0,1:T(2,128)} %param.51) | copy-start | bytes 710020
  88.7 48.2 %copy-start.17 = (f32[2,172,172]{2,0,1:T(2,128)S(1)}, f32[2,172,172]{2,0,1:T(2,128)}, u32[]{:S(2)}) copy-start(f32[2,172,172]{2,0,1:T(2,128)} %param.57) | copy-start | bytes 710020
  88.7 48.2 %copy-start.18 = (f32[2,128,128]{2,1,0:T(8,128)S(1)}, f32[2,128,128]{2,1,0:T(8,128)}, u32[]{:S(2)}) copy-start(f32[2,128,128]{2,1,0:T(8,128)} %refs_1_.1) | copy-start | bytes 393220
  88.7 48.2 %copy-start.19 = (f32[2,128,128]{2,1,0:T(8,128)S(1)}, f32[2,128,128]{2,1,0:T(8,128)}, u32[]{:S(2)}) copy-start(f32[2,128,128]{2,1,0:T(8,128)} %refs_3_.1) | copy-start | bytes 393220
  88.7 48.2 %copy-start.23 = (f32[684]{0:T(1024)S(1)}, f32[684]{0:T(1024)}, u32[]{:S(2)}) copy-start(f32[684]{0:T(1024)} %moment_one.1) | copy-start | bytes 8212
  88.7 48.2 %copy-start.24 = (f32[684]{0:T(1024)S(1)}, f32[684]{0:T(1024)}, u32[]{:S(2)}) copy-start(f32[684]{0:T(1024)} %moment_two.1) | copy-start | bytes 8212
  96.5 2.4 %collective-permute-start = (bf16[1152,128]{1,0:T(8,128)(2,1)S(1)}, bf16[1152,128]{1,0:T(8,128)(2,1)S(1)}, u32[]{:S(2)}, u32[]{:S(2)}) collective-permute-start(bf16[1152,128]{1,0:T(8,128)(2,1)S(1)} %get-tuple-element.59), channel_id=1, source_target_pairs={{0,8},{8,0},{1,9},{9,1},{2,10},{10,2},{3,11},{11,3},{4,12},{12,4},... | collective-permute-start | bytes 884744 | tf_op jit(solution)/shard_map/ppermute | solution.py:1084
  135.2 1.6 %collective-permute-start.1 = (bf16[1152,128]{1,0:T(8,128)(2,1)S(1)}, bf16[1152,128]{1,0:T(8,128)(2,1)S(1)}, u32[]{:S(2)}, u32[]{:S(2)}) collective-permute-start(bf16[1152,128]{1,0:T(8,128)(2,1)S(1)} %bitcast.30), channel_id=1, source_target_pairs={{0,8},{8,0},{1,9},{9,1},{2,10},{10,2},{3,11},{11,3},{4,12},{12,4},... | collective-permute-start | bytes 884744 | tf_op jit(solution)/shard_map/ppermute | solution.py:1090

commit v3 on v2

--- a/solution.py
+++ b/solution.py
@@ -131,8 +131,9 @@
 def stood(flat, unit):
     size = flat.shape[1]
     flat = jnp.concatenate(
-        [flat, jnp.full((unit - flat.shape[0], size), -1, jnp.int32)], axis=0
-    ).astype(jnp.float32)
+        [flat.astype(jnp.float32), jnp.full((unit - flat.shape[0], size), -1.0, jnp.float32)],
+        axis=0,
+    )
     step = min(LANES, size)
     parts = [jnp.transpose(flat[:, k : k + step]) for k in range(0, size, step)]
     return jnp.concatenate(parts, axis=0).astype(jnp.int32)
@@ -279,8 +280,9 @@
     inner = slot & (per - 1)
     here = (valid[...] > 0) & (inner >= first) & (inner < last)
     slot = jnp.where(here, owner * size + inner - first, -1)
-    slot = jnp.concatenate([slot, jnp.full((unit - fan, targets), -1, jnp.int32)], axis=0)
-    slot = slot.astype(jnp.float32)
+    slot = jnp.concatenate(
+        [slot.astype(jnp.float32), jnp.full((unit - fan, targets), -1.0, jnp.float32)], axis=0
+    )
     for b in range(0, targets, LANES):
         table[b : b + LANES, :] = jnp.transpose(slot[:, b : b + LANES]).astype(jnp.int32)
     table[targets:, :] = jnp.full((table.shape[0] - targets, unit), -1, jnp.int32)
@@ -518,6 +520,8 @@
     link,
     sems,
     link_sems,
+    early_rows,
+    own_sems,
     *,
     classes,
 ):
@@ -559,6 +563,15 @@
     def load_link(block):
         return pltpu.make_async_copy(links.at[block], link.at[block], link_sems.at[block])
 
+    held = early_rows.shape[0]
+    fetch_early = pltpu.make_async_copy(
+        sources[0].at[pl.ds(0, held), :], early_rows, own_sems.at[0]
+    )
+    fetch_late = pltpu.make_async_copy(
+        sources[1], late_table.at[:, pl.ds(0, width)], own_sems.at[1]
+    )
+    fetch_early.start()
+    fetch_late.start()
     start_load(0, 0)
 
     def start_link(block, carry):
@@ -569,13 +582,11 @@
     own_link = link.shape[0] - 2
     for block in range(2):
         load_link(own_link + block).start()
-    late_table[:, 0:width] = sources[-1][...]
     late_table[:, width:] = jnp.ones((late_table.shape[0], width), low)
-    filled = 0
-    for source in sources:
-        held = own_table.shape[0] * source.shape[0] // sum(item.shape[0] for item in sources)
-        own_table[filled : filled + held, :] = source[0:held, :].astype(jnp.float32)
-        filled += held
+    fetch_early.wait()
+    own_table[0:held, :] = early_rows[...].astype(jnp.float32)
+    fetch_late.wait()
+    own_table[held:, :] = late_table[0 : own_table.shape[0] - held, 0:width].astype(jnp.float32)
 
     w_in = weights_in[...].astype(low).reshape(2 * weights_in.shape[1], hidden)
     bias_in = biases[:, 0:hidden]
@@ -755,7 +766,7 @@
         functools.partial(step_kernel, classes=classes),
         "step",
         (jax.ShapeDtypeStruct((half, LANES), jnp.bfloat16),) * 2,
-        [smem] * 3 + [anywhere] * 3 + [vmem] * (PARTS + 8),
+        [smem] * 3 + [anywhere] * (3 + PARTS) + [vmem] * 8,
         (vmem, vmem),
         [
             pltpu.VMEM((padded, hidden), jnp.float32),
@@ -777,6 +788,8 @@
             pltpu.VMEM((blocks + 2, targets, SPAN), jnp.bfloat16),
             pltpu.SemaphoreType.DMA((2, 2)),
             pltpu.SemaphoreType.DMA((blocks + 2,)),
+            pltpu.VMEM((held * sources[0].shape[0] // (sources[0].shape[0] + total), width), jnp.bfloat16),
+            pltpu.SemaphoreType.DMA((2,)),
         ],
         14.0,
         BIG,
@@ -841,15 +854,9 @@
 ):
     groups = [refs[5 * k : 5 * k + 5] for k in range(3)]
     loss_out = refs[15]
-    finals = refs[16:28]
+    outs = [refs[16 + 4 * k : 20 + 4 * k] for k in range(3)]
     bias_out, first_out, second_out = refs[28:31]
-    packed, sems = refs[31:33]
-    held = refs[33:45]
-    outs = [held[4 * k : 4 * k + 4] for k in range(3)]
-    copies = [
-        pltpu.make_async_copy(source, final, sems.at[k])
-        for k, (source, final) in enumerate(zip(held, finals))
-    ]
+    packed = refs[31]
     low = jnp.bfloat16
     half = mine.shape[0]
     core = info[0]
@@ -863,16 +870,8 @@
     loss_out[...] = extra[6:7, 0:1] / counted
     scale = 0.5 * inverse * inverse
 
-    starts, row = [], 0
+    row = 0
     for group in range(3):
-        master = groups[group][0]
-        starts.append(row)
-        if group == 2:
-            row += up(master.shape[0], 16) * 2 * (master.shape[2] // LANES)
-        else:
-            row += 2 * master.shape[1] * (master.shape[2] // LANES)
-    for group in (1, 2, 0):
-        row = starts[group]
         master, left, right, left_root, right_root = groups[group]
         new_master, copy, new_left, new_right = outs[group]
         turned = group == 2
@@ -928,8 +927,6 @@
             )[0:depth]
             put(new_master, k, turned, take(master, k, turned) - inverse * way)
         copy[...] = new_master[...].astype(low)
-        for which in range(4):
-            copies[4 * group + which].start()
 
     size = biases.shape[0]
     grad = jnp.concatenate([extra[k : k + 1, :] for k in range(6)], axis=1)[:, 0:size]
@@ -946,8 +943,6 @@
     )
     for ref, value in ((bias_out, fresh), (first_out, first), (second_out, second)):
         ref[...] = value[0]
-    for copy in copies:
-        copy.wait()
 
 
 def run_update(info, fixes, mine, theirs, vectors, groups):
@@ -967,12 +962,8 @@
         "update",
         tuple(outs),
         [smem] * 2 + [vmem] * (5 + len(flat)),
-        (vmem,) + (anywhere,) * 12 + (vmem,) * 3,
-        [
-            pltpu.VMEM((2 * mine.shape[0], LANES), jnp.bfloat16),
-            pltpu.SemaphoreType.DMA((12,)),
-        ]
-        + [pltpu.VMEM(item.shape, item.dtype) for item in outs[1:13]],
+        (vmem,) * len(outs),
+        [pltpu.VMEM((2 * mine.shape[0], LANES), jnp.bfloat16)],
         4.0,
         16 << 20,
     )(info, fixes, mine, theirs, *vectors, *flat)

time: 142 us -> 142 us (level)
  no operation moved by 1% of the time
where the time goes in v3:
time: 142 us; the launch traced here: 141 us
  Pallas kernels  37.6 us (26%)
  waiting for transfers between devices  37.6 us (26%)
  blocking collectives  35.1 us (25%)
  starting transfers between devices  17.1 us (12%)
  local copies, waits for them, and re-layouts  11.8 us (8%)
  between operations  1.98 us (1%)
    all_to_all x2, waiting for transfers between devices, trade(): lax.all_to_all(found.reshape(devices, -1, width), AXES, split_axis=0, con...  33.8 us
    all_to_all x1, blocking collectives, body(): lax.all_to_all(summed, PEERS, split_axis=0, concat_axis=0, tiled=True)  21.8 us
    all_to_all x1, blocking collectives, body(): lax.all_to_all(shared, PEERS, split_axis=0, concat_axis=0, tiled=True)  13.3 us
    unnamed x60, local copies, waits for them, and re-layouts  10.4 us
    pallas_call x2, Pallas kernels, pick_rows(): call(functools.partial(pick_kernel, first=first, part=last - first, per=p...  10.3 us
    all_to_all x2, starting transfers between devices, trade(): lax.all_to_all(found.reshape(devices, -1, width), AXES, split_axis=0, con...  8.58 us
    pallas_call x2, Pallas kernels, tally(): call(functools.partial(tally_kernel, per=per, which=which), 'early_sums'...  8.22 us
    pallas_call x1, Pallas kernels, run_step(): call(functools.partial(step_kernel, classes=classes), 'step', (jax.ShapeD...  7.72 us
  transfers between devices with their start and end apart: 5, of which 5 were waited for; matrix products, arithmetic and copies ran while one was open for 0% of the time, Pallas kernels for 14%

profile of v3, /device:TPU:0, one launch (start us, length us, event | category | flops | bytes accessed | tf_op | source)
XLA Modules:
  0.0 141.4 jit_solution(7860199624447085363)
XLA Ops:
  0.6 1.4 all_to_all.18
  2.0 7.3 %all-to-all-start = ((s32[32,1,256]{2,1,0:T(1,128)}), s32[32,1,256]{2,1,0:T(1,128)S(1)}, u32[]{:S(2)}, u32[]{:S(2)}) async-start(s32[32,1,256]{2,1,0:T(1,128)} %all_to_all.18), calls=%async_computation | async-start | bytes 65536 | tf_op jit(solution)/shard_map/all_to_all | solution.py:1014
  9.3 0.0 copy-start.20
  9.4 0.7 copy-done.20
  10.1 0.7 copy-done.21
  10.8 0.7 copy-done.25
  11.5 0.7 copy-done.26
  12.2 0.7 copy-done.27
  12.9 2.6 %reach.1 = (s32[48,128]{1,0:T(8,128)S(1)}, s32[48,128]{1,0:T(8,128)S(1)}, s32[384,16]{1,0:T(8,128)S(1)}, s32[64,8]{1,0:T(8,128)S(1)}, s32[2]{0:T(128)S(1)}) custom-call(s32[5,64]{1,0:T(8,128)S(1)} %bitcast.46, s32[5,64]{1,0:T(8,128)S(1)} %bitcast.47, s32[64]{0:T(128)S(1)} %copy-done.27, s32[10,384]{1,0:T(8,128)S(1)} %bitcast.44, s32[10,384]{1,0:T(8,128)S(1)} %bitcast.45), custom_call_target="tpu_custom_call" | custom-call | bytes 10800000 | tf_op jit(solution)/shard_map/reach/pallas_call | solution.py:238
  15.5 1.0 all-to-all-done
  16.5 3.4 %copy-done = f32[16384,128]{1,0:T(8,128)S(1)} copy-done((f32[16384,128]{1,0:T(8,128)S(1)}, f32[16384,128]{1,0:T(8,128)}, u32[]{:S(2)}) %copy-start) | copy-done | bytes 8388632
  19.9 5.2 %pick_rows.3 = bf16[4096,128]{1,0:T(8,128)(2,1)} custom-call(s32[8192]{0:T(1024)S(1)} %bitcast.39, f32[16384,128]{1,0:T(8,128)S(1)} %copy-done), custom_call_target="tpu_custom_call" | custom-call | bytes 16559999 | tf_op jit(solution)/shard_map/pick_rows/pallas_call | solution.py:115
  25.1 0.0 copy-start.5
  25.1 0.0 copy-start.6
  25.1 4.8 %all-to-all-start.1 = ((bf16[32,128,128]{2,1,0:T(8,128)(2,1)}), bf16[32,128,128]{2,1,0:T(8,128)(2,1)S(1)}, u32[]{:S(2)}, u32[]{:S(2)}) async-start(bf16[32,128,128]{2,1,0:T(8,128)(2,1)} %bitcast.13), calls=%async_computation.1 | async-start | bytes 2097152 | tf_op jit(solution)/shard_map/all_to_all | solution.py:1022
  30.7 0.1 pad_add_fusion.info
  30.8 0.1 pad_maximum_fusion.fixes
  30.8 3.4 %copy-done.1 = f32[16384,128]{1,0:T(8,128)S(1)} copy-done((f32[16384,128]{1,0:T(8,128)S(1)}, f32[16384,128]{1,0:T(8,128)}, u32[]{:S(2)}) %copy-start.1) | copy-done | bytes 8388632
  34.2 5.1 %pick_rows.2 = bf16[4096,128]{1,0:T(8,128)(2,1)} custom-call(s32[8192]{0:T(1024)S(1)} %bitcast.40, f32[16384,128]{1,0:T(8,128)S(1)} %copy-done.1), custom_call_target="tpu_custom_call" | custom-call | bytes 16559999 | tf_op jit(solution)/shard_map/pick_rows/pallas_call | solution.py:115
  39.4 3.6 %link_matrix.1.links = bf16[72,384,256]{2,1,0:T(8,128)(2,1)} custom-call(s32[2]{0:T(128)S(1)} %get-tuple-element.48.count, s32[48,128]{1,0:T(8,128)S(1)} %get-tuple-element.49.names, s32[384,16]{1,0:T(8,128)S(1)} %get-tuple-element.50.near.refs_2_), custom_call_target="tpu_custom_call" | custom-call | bytes 18000000 | tf_op jit(solution)/shard_map/link_matrix/pallas_call | solution.py:454
  43.0 0.0 copy-start.3
  43.0 0.0 copy-start.4
  43.0 0.0 copy-start.7
  43.0 0.0 copy-start.22
  43.0 0.0 copy-start.28
  43.0 0.0 copy-start.29
  43.1 3.5 %tally.1.tallies = f8e4m3fn[4608,4096]{1,0:T(32,128)(4,1)} custom-call(s32[2]{0:T(128)S(1)} %get-tuple-element.48.count, s32[6144]{0:T(1024)S(1)} %bitcast.41, s32[15,4224]{1,0:T(8,128)S(1)} %bitcast.33, s32[15,4224]{1,0:T(8,128)S(1)} %bitcast.35), custom_call_target="tpu_custom_call" | custom-call | bytes 50400000 | tf_op jit(solution)/shard_map/tally/pallas_call | solution.py:385
  46.6 10.9 %all-to-all-done.1 = bf16[32,128,128]{2,1,0:T(8,128)(2,1)S(1)} async-done(((bf16[32,128,128]{2,1,0:T(8,128)(2,1)}), bf16[32,128,128]{2,1,0:T(8,128)(2,1)S(1)}, u32[]{:S(2)}, u32[]{:S(2)}) %all-to-all-start.1) | async-done | bytes 1048608 | tf_op jit(solution)/shard_map/all_to_all | solution.py:1022
  57.5 3.8 %all-to-all-start.2 = ((bf16[32,128,128]{2,1,0:T(8,128)(2,1)}), bf16[32,128,128]{2,1,0:T(8,128)(2,1)}, u32[]{:S(2)}, u32[]{:S(2)}) async-start(bf16[32,128,128]{2,1,0:T(8,128)(2,1)} %bitcast.15), calls=%async_computation.2 | async-start | bytes 2097152 | tf_op jit(solution)/shard_map/all_to_all | solution.py:1022
  61.3 4.7 %early_sums.1.partial = f32[13824,256]{1,0:T(8,128)} custom-call(s32[2]{0:T(128)S(1)} %get-tuple-element.48.count, s32[6144]{0:T(1024)S(1)} %bitcast.42, s32[15,4224]{1,0:T(8,128)S(1)} %bitcast.34, s32[15,4224]{1,0:T(8,128)S(1)} %bitcast.36, bf16[4096,128]{1,0:T(8,128)(2,1)S(1)} %bitcast.26), custom_call_target="tpu_custom_call" | custom-call | bytes 50400000 | tf_op jit(solution)/shard_map/early_sums/pallas_call | solution.py:385
  66.0 22.9 %all-to-all-done.2 = bf16[32,128,128]{2,1,0:T(8,128)(2,1)} async-done(((bf16[32,128,128]{2,1,0:T(8,128)(2,1)}), bf16[32,128,128]{2,1,0:T(8,128)(2,1)}, u32[]{:S(2)}, u32[]{:S(2)}) %all-to-all-start.2) | async-done | bytes 1048608 | tf_op jit(solution)/shard_map/all_to_all | solution.py:1022
  88.9 0.0 copy-start.8
  88.9 0.0 copy-start.9
  89.0 0.0 copy-start.12
  89.0 0.0 copy-start.13
  89.0 0.0 copy-start.15
  89.0 0.0 copy-start.16
  89.1 0.0 copy-start.19
  89.1 0.0 copy-start.23
  89.1 7.7 %step.1 = (bf16[1152,128]{1,0:T(8,128)(2,1)S(1)}, bf16[1152,128]{1,0:T(8,128)(2,1)S(1)}) custom-call(s32[2]{0:T(128)S(1)} %pad_add_fusion.info, s32[2]{0:T(128)S(1)} %get-tuple-element.48.count, s32[6144]{0:T(1024)S(1)} %bitcast.43, f32[13824,256]{1,0:T(8,128)} %early_sums.1.partial, f8e4m3fn[4608,4096]{1,0:T(32,128)(4,1)} %tally.1.tallies, ...), custom_call_target="tpu_custom_call" | custom-call | bytes 50400000 | tf_op jit(solution)/shard_map/step/pallas_call | solution.py:765
  96.8 1.2 collective-permute-start
  98.0 1.2 collective-permute-done.theirs
  99.3 0.6 pair_sum.1
  99.9 21.8 %all_to_all.29.pieces = bf16[16,72,128]{2,1,0:T(8,128)(2,1)S(1)} all-to-all(bf16[16,72,128]{2,1,0:T(8,128)(2,1)S(1)} %bitcast.32), channel_id=1, replica_groups=mesh['chip'=2,'core'=2,'dev'=8] {'chip','dev'}, dimensions={0} | all-to-all | bytes 589824 | tf_op jit(solution)/shard_map/all_to_all | solution.py:1077
  121.7 0.6 spread_sum.1
  122.3 13.3 %all_to_all.30 = bf16[16,72,128]{2,1,0:T(8,128)(2,1)S(1)} all-to-all(bf16[16,72,128]{2,1,0:T(8,128)(2,1)S(1)} %spread_sum.1), channel_id=1, replica_groups=mesh['chip'=2,'core'=2,'dev'=8] {'chip','dev'}, dimensions={0} | all-to-all | bytes 589824 | tf_op jit(solution)/shard_map/all_to_all | solution.py:1079
  135.6 1.6 %collective-permute-done.1.theirs = bf16[1152,128]{1,0:T(8,128)(2,1)S(1)} collective-permute-done((bf16[1152,128]{1,0:T(8,128)(2,1)S(1)}, bf16[1152,128]{1,0:T(8,128)(2,1)S(1)}, u32[]{:S(2)}, u32[]{:S(2)}) %collective-permute-start.1) | collective-permute-done | bytes 294944 | tf_op jit(solution)/shard_map/ppermute | solution.py:1081
  137.3 3.9 %update.1 = (f32[1,1]{1,0:T(1,128)}, f32[2,128,256]{2,1,0:T(8,128)}, bf16[2,128,256]{2,1,0:T(8,128)(2,1)}, f32[2,128,128]{2,1,0:T(8,128)}, f32[2,256,256]{2,1,0:...) custom-call(s32[2]{0:T(128)S(1)} %pad_add_fusion.info, ...), custom_call_target="tpu_custom_call" | custom-call | bytes 14400000 | tf_op jit(solution)/shard_map/update/pallas_call | solution.py:960
  (37 shorter events, 0.1 us)
Async XLA Ops:
  2.0 14.5 %all-to-all-start = ((s32[32,1,256]{2,1,0:T(1,128)}), s32[32,1,256]{2,1,0:T(1,128)S(1)}, u32[]{:S(2)}, u32[]{:S(2)}) async-start(s32[32,1,256]{2,1,0:T(1,128)} %all_to_all.18), calls=%async_computation | async-start | bytes 65536 | tf_op jit(solution)/shard_map/all_to_all | solution.py:1014
  9.3 0.7 copy-start.20
  10.1 0.7 copy-start.21
  10.8 0.7 copy-start.25
  11.5 0.7 copy-start.26
  12.2 0.7 copy-start.27
  16.5 3.4 %copy-start = (f32[16384,128]{1,0:T(8,128)S(1)}, f32[16384,128]{1,0:T(8,128)}, u32[]{:S(2)}) copy-start(f32[16384,128]{1,0:T(8,128)} %table.3) | copy-start | bytes 25165828
  25.1 17.9 %copy-start.5 = (s32[4224,15]{0,1:T(8,128)S(1)}, s32[4224,15]{0,1:T(8,128)}, u32[]{:S(2)}) copy-start(s32[4224,15]{0,1:T(8,128)} %param.31) | copy-start | bytes 760324
  25.1 17.9 %copy-start.6 = (s32[4224,15]{0,1:T(8,128)S(1)}, s32[4224,15]{0,1:T(8,128)}, u32[]{:S(2)}) copy-start(s32[4224,15]{0,1:T(8,128)} %param.34) | copy-start | bytes 760324
  25.1 32.4 %all-to-all-start.1 = ((bf16[32,128,128]{2,1,0:T(8,128)(2,1)}), bf16[32,128,128]{2,1,0:T(8,128)(2,1)S(1)}, u32[]{:S(2)}, u32[]{:S(2)}) async-start(bf16[32,128,128]{2,1,0:T(8,128)(2,1)} %bitcast.13), calls=%async_computation.1 | async-start | bytes 2097152 | tf_op jit(solution)/shard_map/all_to_all | solution.py:1022
  30.8 3.4 %copy-start.1 = (f32[16384,128]{1,0:T(8,128)S(1)}, f32[16384,128]{1,0:T(8,128)}, u32[]{:S(2)}) copy-start(f32[16384,128]{1,0:T(8,128)} %table.3) | copy-start | bytes 25165828
  43.0 45.9 %copy-start.3 = (f32[2,256,256]{2,1,0:T(8,128)S(1)}, f32[2,256,256]{2,1,0:T(8,128)}, u32[]{:S(2)}) copy-start(f32[2,256,256]{2,1,0:T(8,128)} %refs_5_.3) | copy-start | bytes 1572868
  43.0 45.9 %copy-start.4 = (f32[2,256,172]{1,0,2:T(2,128)S(1)}, f32[2,256,172]{1,0,2:T(2,128)}, u32[]{:S(2)}) copy-start(f32[2,256,172]{1,0,2:T(2,128)} %param.41) | copy-start | bytes 1056772
  43.0 45.9 %copy-start.7 = (f32[2,128,256]{2,1,0:T(8,128)S(1)}, f32[2,128,256]{2,1,0:T(8,128)}, u32[]{:S(2)}) copy-start(f32[2,128,256]{2,1,0:T(8,128)} %refs_0_.1) | copy-start | bytes 786436
  43.0 45.9 %copy-start.22 = (f32[684]{0:T(1024)S(1)}, f32[684]{0:T(1024)}, u32[]{:S(2)}) copy-start(f32[684]{0:T(1024)} %biases.1) | copy-start | bytes 8212
  43.0 45.9 %copy-start.28 = (s32[64]{0:T(128)S(1)}, s32[64]{0:T(128)}, u32[]{:S(2)}) copy-start(s32[64]{0:T(128)} %refs_5_.2) | copy-start | bytes 772
  43.0 45.9 %copy-start.29 = (s32[64]{0:T(128)S(1)}, s32[64]{0:T(128)}, u32[]{:S(2)}) copy-start(s32[64]{0:T(128)} %refs_4_.2) | copy-start | bytes 772
  57.5 31.3 %copy-start.2 = (bf16[32,128,128]{2,1,0:T(8,128)(2,1)}, bf16[32,128,128]{2,1,0:T(8,128)(2,1)S(1)}, u32[]{:S(2)}) copy-start(bf16[32,128,128]{2,1,0:T(8,128)(2,1)S(1)} %all-to-all-done.1) | copy-start | bytes 3145732
  57.5 31.3 %all-to-all-start.2 = ((bf16[32,128,128]{2,1,0:T(8,128)(2,1)}), bf16[32,128,128]{2,1,0:T(8,128)(2,1)}, u32[]{:S(2)}, u32[]{:S(2)}) async-start(bf16[32,128,128]{2,1,0:T(8,128)(2,1)} %bitcast.15), calls=%async_computation.2 | async-start | bytes 2097152 | tf_op jit(solution)/shard_map/all_to_all | solution.py:1022
  88.9 48.3 %copy-start.8 = (f32[2,256,256]{2,1,0:T(8,128)S(1)}, f32[2,256,256]{2,1,0:T(8,128)}, u32[]{:S(2)}) copy-start(f32[2,256,256]{2,1,0:T(8,128)} %refs_2_.1) | copy-start | bytes 1572868
  88.9 48.3 %copy-start.9 = (f32[2,256,256]{2,1,0:T(8,128)S(1)}, f32[2,256,256]{2,1,0:T(8,128)}, u32[]{:S(2)}) copy-start(f32[2,256,256]{2,1,0:T(8,128)} %refs_4_.3) | copy-start | bytes 1572868
  88.9 48.3 %copy-start.10 = (f32[2,256,256]{2,1,0:T(8,128)S(1)}, f32[2,256,256]{2,1,0:T(8,128)}, u32[]{:S(2)}) copy-start(f32[2,256,256]{2,1,0:T(8,128)} %refs_6_.3) | copy-start | bytes 1572868
  89.0 48.2 %copy-start.11 = (f32[2,256,256]{2,1,0:T(8,128)S(1)}, f32[2,256,256]{2,1,0:T(8,128)}, u32[]{:S(2)}) copy-start(f32[2,256,256]{2,1,0:T(8,128)} %refs_7_.3) | copy-start | bytes 1572868
  89.0 48.2 %copy-start.12 = (f32[2,256,256]{2,1,0:T(8,128)S(1)}, f32[2,256,256]{2,1,0:T(8,128)}, u32[]{:S(2)}) copy-start(f32[2,256,256]{2,1,0:T(8,128)} %refs_8_.1) | copy-start | bytes 1572868
  89.0 48.2 %copy-start.13 = (f32[2,256,256]{2,1,0:T(8,128)S(1)}, f32[2,256,256]{2,1,0:T(8,128)}, u32[]{:S(2)}) copy-start(f32[2,256,256]{2,1,0:T(8,128)} %refs_9_.3) | copy-start | bytes 1572868
  89.0 48.2 %copy-start.14 = (f32[2,256,256]{2,1,0:T(8,128)S(1)}, f32[2,256,256]{2,1,0:T(8,128)}, u32[]{:S(2)}) copy-start(f32[2,256,256]{2,1,0:T(8,128)} %refs_12_.1) | copy-start | bytes 1572868
  89.0 48.2 %copy-start.15 = (f32[2,256,256]{2,1,0:T(8,128)S(1)}, f32[2,256,256]{2,1,0:T(8,128)}, u32[]{:S(2)}) copy-start(f32[2,256,256]{2,1,0:T(8,128)} %refs_14_.1) | copy-start | bytes 1572868
  89.0 48.2 %copy-start.16 = (f32[2,172,172]{2,0,1:T(2,128)S(1)}, f32[2,172,172]{2,0,1:T(2,128)}, u32[]{:S(2)}) copy-start(f32[2,172,172]{2,0,1:T(2,128)} %param.51) | copy-start | bytes 710020
  89.0 48.2 %copy-start.17 = (f32[2,172,172]{2,0,1:T(2,128)S(1)}, f32[2,172,172]{2,0,1:T(2,128)}, u32[]{:S(2)}) copy-start(f32[2,172,172]{2,0,1:T(2,128)} %param.57) | copy-start | bytes 710020
  89.0 48.2 %copy-start.18 = (f32[2,128,128]{2,1,0:T(8,128)S(1)}, f32[2,128,128]{2,1,0:T(8,128)}, u32[]{:S(2)}) copy-start(f32[2,128,128]{2,1,0:T(8,128)} %refs_1_.1) | copy-start | bytes 393220
  89.1 48.2 %copy-start.19 = (f32[2,128,128]{2,1,0:T(8,128)S(1)}, f32[2,128,128]{2,1,0:T(8,128)}, u32[]{:S(2)}) copy-start(f32[2,128,128]{2,1,0:T(8,128)} %refs_3_.1) | copy-start | bytes 393220
  89.1 48.2 %copy-start.23 = (f32[684]{0:T(1024)S(1)}, f32[684]{0:T(1024)}, u32[]{:S(2)}) copy-start(f32[684]{0:T(1024)} %moment_one.1) | copy-start | bytes 8212
  89.1 48.2 %copy-start.24 = (f32[684]{0:T(1024)S(1)}, f32[684]{0:T(1024)}, u32[]{:S(2)}) copy-start(f32[684]{0:T(1024)} %moment_two.1) | copy-start | bytes 8212
  96.8 2.4 %collective-permute-start = (bf16[1152,128]{1,0:T(8,128)(2,1)S(1)}, bf16[1152,128]{1,0:T(8,128)(2,1)S(1)}, u32[]{:S(2)}, u32[]{:S(2)}) collective-permute-start(bf16[1152,128]{1,0:T(8,128)(2,1)S(1)} %get-tuple-element.59), channel_id=1, source_target_pairs={{0,8},{8,0},{1,9},{9,1},{2,10},{10,2},{3,11},{11,3},{4,12},{12,4},... | collective-permute-start | bytes 884744 | tf_op jit(solution)/shard_map/ppermute | solution.py:1075
  135.6 1.6 %collective-permute-start.1 = (bf16[1152,128]{1,0:T(8,128)(2,1)S(1)}, bf16[1152,128]{1,0:T(8,128)(2,1)S(1)}, u32[]{:S(2)}, u32[]{:S(2)}) collective-permute-start(bf16[1152,128]{1,0:T(8,128)(2,1)S(1)} %bitcast.30), channel_id=1, source_target_pairs={{0,8},{8,0},{1,9},{9,1},{2,10},{10,2},{3,11},{11,3},{4,12},{12,4},... | collective-permute-start | bytes 884744 | tf_op jit(solution)/shard_map/ppermute | solution.py:1081

commit v4 on v3

--- a/solution.py
+++ b/solution.py
@@ -83,15 +83,24 @@
     return (0, per // 2), (per // 2, per)
 
 
-def pick_kernel(wanted, table, out, rows, done, sems, *, first, part, per):
+def pick_kernel(lists, table, out, rows, done, wanted, sems, list_sems, *, first, part, per):
     chunk = rows.shape[0]
     devices = chunk // part
+    steps = out.shape[0] // chunk
+
+    def load(step):
+        where = pl.ds(pl.multiple_of(step * devices * per, devices * per), devices * per)
+        return pltpu.make_async_copy(lists.at[where], wanted.at[where], list_sems.at[step])
+
+    for step in range(steps):
+        load(step).start()
 
     def save(step):
         where = pl.ds(pl.multiple_of(step * chunk, chunk), chunk)
         return pltpu.make_async_copy(done.at[where, :], out.at[where, :], sems.at[step])
 
     def body(step, carry):
+        load(step).wait()
         for d in range(devices):
             base = (step * devices + d) * per + first
             for u in range(part):
@@ -102,8 +111,8 @@
         save(step).start()
         return carry
 
-    lax.fori_loop(0, out.shape[0] // chunk, body, 0)
-    for step in range(out.shape[0] // chunk):
+    lax.fori_loop(0, steps, body, 0)
+    for step in range(steps):
         save(step).wait()
 
 
@@ -116,11 +125,13 @@
         functools.partial(pick_kernel, first=first, part=last - first, per=per),
         "pick_rows",
         jax.ShapeDtypeStruct((count, width), jnp.bfloat16),
-        [smem, vmem],
+        [anywhere, vmem],
         anywhere,
         [
             pltpu.VMEM((chunk, width), jnp.float32),
             pltpu.VMEM((count, width), jnp.bfloat16),
+            pltpu.SMEM(wanted.shape, jnp.int32),
+            pltpu.SemaphoreType.DMA((count // chunk,)),
             pltpu.SemaphoreType.DMA((count // chunk,)),
         ],
         4.6,
@@ -521,6 +532,7 @@
     sems,
     link_sems,
     early_rows,
+    spots,
     own_sems,
     *,
     classes,
@@ -570,7 +582,9 @@
     fetch_late = pltpu.make_async_copy(
         sources[1], late_table.at[:, pl.ds(0, width)], own_sems.at[1]
     )
+    fetch_places = pltpu.make_async_copy(places, spots, own_sems.at[2])
     fetch_early.start()
+    fetch_places.start()
     fetch_late.start()
     start_load(0, 0)
 
@@ -583,6 +597,7 @@
     for block in range(2):
         load_link(own_link + block).start()
     late_table[:, width:] = jnp.ones((late_table.shape[0], width), low)
+    fetch_places.wait()
     fetch_early.wait()
     own_table[0:held, :] = early_rows[...].astype(jnp.float32)
     fetch_late.wait()
@@ -617,7 +632,7 @@
         start_load(pair + 1, 1 - slot)
         for part in range(0, size, SPAN):
             for u in range(part, part + SPAN):
-                own_rows[u : u + 1, :] = own_table[pl.ds(places[base + u], 1), :]
+                own_rows[u : u + 1, :] = own_table[pl.ds(spots[base + u], 1), :]
             here = slice(part, part + SPAN)
             joined[here, :] = dot(late[slot, here, :].astype(low), late_table[...]) + (
                 early[slot, here, :]
@@ -766,7 +781,7 @@
         functools.partial(step_kernel, classes=classes),
         "step",
         (jax.ShapeDtypeStruct((half, LANES), jnp.bfloat16),) * 2,
-        [smem] * 3 + [anywhere] * (3 + PARTS) + [vmem] * 8,
+        [smem] * 2 + [anywhere] * (4 + PARTS) + [vmem] * 8,
         (vmem, vmem),
         [
             pltpu.VMEM((padded, hidden), jnp.float32),
@@ -789,7 +804,8 @@
             pltpu.SemaphoreType.DMA((2, 2)),
             pltpu.SemaphoreType.DMA((blocks + 2,)),
             pltpu.VMEM((held * sources[0].shape[0] // (sources[0].shape[0] + total), width), jnp.bfloat16),
-            pltpu.SemaphoreType.DMA((2,)),
+            pltpu.SMEM(places.shape, jnp.int32),
+            pltpu.SemaphoreType.DMA((3,)),
         ],
         14.0,
         BIG,

time: 142 us -> 141 us (level)
  no operation moved by 1% of the time
where the time goes in v4:
time: 141 us; the launch traced here: 140 us
  waiting for transfers between devices  37.9 us (27%)
  Pallas kernels  36.5 us (26%)
  blocking collectives  35.2 us (25%)
  starting transfers between devices  16.8 us (12%)
  local copies, waits for them, and re-layouts  11.8 us (8%)
  between operations  1.98 us (1%)
    all_to_all x2, waiting for transfers between devices, trade(): lax.all_to_all(found.reshape(devices, -1, width), AXES, split_axis=0, con...  34.1 us
    all_to_all x1, blocking collectives, body(): lax.all_to_all(summed, PEERS, split_axis=0, concat_axis=0, tiled=True)  21.8 us
    all_to_all x1, blocking collectives, body(): lax.all_to_all(shared, PEERS, split_axis=0, concat_axis=0, tiled=True)  13.3 us
    unnamed x60, local copies, waits for them, and re-layouts  10.4 us
    pallas_call x2, Pallas kernels, pick_rows(): call(functools.partial(pick_kernel, first=first, part=last - first, per=p...  9.67 us
    all_to_all x2, starting transfers between devices, trade(): lax.all_to_all(found.reshape(devices, -1, width), AXES, split_axis=0, con...  8.26 us
    pallas_call x2, Pallas kernels, tally(): call(functools.partial(tally_kernel, per=per, which=which), 'early_sums'...  8.23 us
    all_to_all x1, starting transfers between devices, body(): lax.all_to_all(requests, AXES, split_axis=0, concat_axis=0, tiled=True)  7.3 us
  transfers between devices with their start and end apart: 5, of which 5 were waited for; matrix products, arithmetic and copies ran while one was open for 0% of the time, Pallas kernels for 14%

profile of v4, /device:TPU:0, one launch (start us, length us, event | category | flops | bytes accessed | tf_op | source)
XLA Modules:
  0.0 140.3 jit_solution(7729742039449080126)
XLA Ops:
  0.6 1.4 all_to_all.18
  2.0 7.3 %all-to-all-start = ((s32[32,1,256]{2,1,0:T(1,128)}), s32[32,1,256]{2,1,0:T(1,128)S(1)}, u32[]{:S(2)}, u32[]{:S(2)}) async-start(s32[32,1,256]{2,1,0:T(1,128)} %all_to_all.18), calls=%async_computation | async-start | bytes 65536 | tf_op jit(solution)/shard_map/all_to_all | solution.py:1030
  9.3 0.0 copy-start.20
  9.4 0.7 copy-done.20
  10.1 0.7 copy-done.21
  10.8 0.7 copy-done.25
  11.5 0.7 copy-done.26
  12.2 0.7 copy-done.27
  12.9 2.6 %reach.1 = (s32[48,128]{1,0:T(8,128)S(1)}, s32[48,128]{1,0:T(8,128)S(1)}, s32[384,16]{1,0:T(8,128)S(1)}, s32[64,8]{1,0:T(8,128)S(1)}, s32[2]{0:T(128)S(1)}) custom-call(s32[5,64]{1,0:T(8,128)S(1)} %bitcast.46, s32[5,64]{1,0:T(8,128)S(1)} %bitcast.47, s32[64]{0:T(128)S(1)} %copy-done.27, s32[10,384]{1,0:T(8,128)S(1)} %bitcast.44, s32[10,384]{1,0:T(8,128)S(1)} %bitcast.45), custom_call_target="tpu_custom_call" | custom-call | bytes 10800000 | tf_op jit(solution)/shard_map/reach/pallas_call | solution.py:249
  15.5 1.0 all-to-all-done
  16.5 3.4 %copy-done = f32[16384,128]{1,0:T(8,128)S(1)} copy-done((f32[16384,128]{1,0:T(8,128)S(1)}, f32[16384,128]{1,0:T(8,128)}, u32[]{:S(2)}) %copy-start) | copy-done | bytes 8388632
  19.9 4.9 %pick_rows.3 = bf16[4096,128]{1,0:T(8,128)(2,1)} custom-call(s32[8192]{0:T(1024)S(1)} %bitcast.39, f32[16384,128]{1,0:T(8,128)S(1)} %copy-done), custom_call_target="tpu_custom_call" | custom-call | bytes 16559999 | tf_op jit(solution)/shard_map/pick_rows/pallas_call | solution.py:124
  24.8 0.0 copy-start.5
  24.8 0.0 copy-start.6
  24.8 4.8 %all-to-all-start.1 = ((bf16[32,128,128]{2,1,0:T(8,128)(2,1)}), bf16[32,128,128]{2,1,0:T(8,128)(2,1)S(1)}, u32[]{:S(2)}, u32[]{:S(2)}) async-start(bf16[32,128,128]{2,1,0:T(8,128)(2,1)} %bitcast.13), calls=%async_computation.1 | async-start | bytes 2097152 | tf_op jit(solution)/shard_map/all_to_all | solution.py:1038
  30.4 0.1 pad_add_fusion.info
  30.5 0.1 pad_maximum_fusion.fixes
  30.5 3.4 %copy-done.1 = f32[16384,128]{1,0:T(8,128)S(1)} copy-done((f32[16384,128]{1,0:T(8,128)S(1)}, f32[16384,128]{1,0:T(8,128)}, u32[]{:S(2)}) %copy-start.1) | copy-done | bytes 8388632
  33.9 4.8 %pick_rows.2 = bf16[4096,128]{1,0:T(8,128)(2,1)} custom-call(s32[8192]{0:T(1024)S(1)} %bitcast.40, f32[16384,128]{1,0:T(8,128)S(1)} %copy-done.1), custom_call_target="tpu_custom_call" | custom-call | bytes 16559999 | tf_op jit(solution)/shard_map/pick_rows/pallas_call | solution.py:124
  38.7 3.6 %link_matrix.1.links = bf16[72,384,256]{2,1,0:T(8,128)(2,1)} custom-call(s32[2]{0:T(128)S(1)} %get-tuple-element.48.count, s32[48,128]{1,0:T(8,128)S(1)} %get-tuple-element.49.names, s32[384,16]{1,0:T(8,128)S(1)} %get-tuple-element.50.near.refs_2_), custom_call_target="tpu_custom_call" | custom-call | bytes 18000000 | tf_op jit(solution)/shard_map/link_matrix/pallas_call | solution.py:465
  42.3 0.0 copy-start.3
  42.4 0.0 copy-start.4
  42.4 0.0 copy-start.7
  42.4 0.0 copy-start.22
  42.4 0.0 copy-start.28
  42.4 0.0 copy-start.29
  42.4 3.5 %tally.1.tallies = f8e4m3fn[4608,4096]{1,0:T(32,128)(4,1)} custom-call(s32[2]{0:T(128)S(1)} %get-tuple-element.48.count, s32[6144]{0:T(1024)S(1)} %bitcast.41, s32[15,4224]{1,0:T(8,128)S(1)} %bitcast.33, s32[15,4224]{1,0:T(8,128)S(1)} %bitcast.35), custom_call_target="tpu_custom_call" | custom-call | bytes 50400000 | tf_op jit(solution)/shard_map/tally/pallas_call | solution.py:396
  46.0 11.3 %all-to-all-done.1 = bf16[32,128,128]{2,1,0:T(8,128)(2,1)S(1)} async-done(((bf16[32,128,128]{2,1,0:T(8,128)(2,1)}), bf16[32,128,128]{2,1,0:T(8,128)(2,1)S(1)}, u32[]{:S(2)}, u32[]{:S(2)}) %all-to-all-start.1) | async-done | bytes 1048608 | tf_op jit(solution)/shard_map/all_to_all | solution.py:1038
  57.2 3.4 %all-to-all-start.2 = ((bf16[32,128,128]{2,1,0:T(8,128)(2,1)}), bf16[32,128,128]{2,1,0:T(8,128)(2,1)}, u32[]{:S(2)}, u32[]{:S(2)}) async-start(bf16[32,128,128]{2,1,0:T(8,128)(2,1)} %bitcast.15), calls=%async_computation.2 | async-start | bytes 2097152 | tf_op jit(solution)/shard_map/all_to_all | solution.py:1038
  60.7 4.7 %early_sums.1.partial = f32[13824,256]{1,0:T(8,128)} custom-call(s32[2]{0:T(128)S(1)} %get-tuple-element.48.count, s32[6144]{0:T(1024)S(1)} %bitcast.42, s32[15,4224]{1,0:T(8,128)S(1)} %bitcast.34, s32[15,4224]{1,0:T(8,128)S(1)} %bitcast.36, bf16[4096,128]{1,0:T(8,128)(2,1)S(1)} %bitcast.26), custom_call_target="tpu_custom_call" | custom-call | bytes 50400000 | tf_op jit(solution)/shard_map/early_sums/pallas_call | solution.py:396
  65.4 22.9 %all-to-all-done.2 = bf16[32,128,128]{2,1,0:T(8,128)(2,1)} async-done(((bf16[32,128,128]{2,1,0:T(8,128)(2,1)}), bf16[32,128,128]{2,1,0:T(8,128)(2,1)}, u32[]{:S(2)}, u32[]{:S(2)}) %all-to-all-start.2) | async-done | bytes 1048608 | tf_op jit(solution)/shard_map/all_to_all | solution.py:1038
  88.3 0.0 copy-start.8
  88.3 0.0 copy-start.9
  88.3 0.0 copy-start.10
  88.3 0.0 copy-start.13
  88.4 0.0 copy-start.14
  88.4 0.0 copy-start.17
  88.4 0.0 copy-start.18
  88.4 0.0 copy-start.24
  88.4 7.2 %step.1 = (bf16[1152,128]{1,0:T(8,128)(2,1)S(1)}, bf16[1152,128]{1,0:T(8,128)(2,1)S(1)}) custom-call(s32[2]{0:T(128)S(1)} %pad_add_fusion.info, s32[2]{0:T(128)S(1)} %get-tuple-element.48.count, s32[6144]{0:T(1024)S(1)} %bitcast.43, f32[13824,256]{1,0:T(8,128)} %early_sums.1.partial, f8e4m3fn[4608,4096]{1,0:T(32,128)(4,1)} %tally.1.tallies, ...), custom_call_target="tpu_custom_call" | custom-call | bytes 50400000 | tf_op jit(solution)/shard_map/step/pallas_call | solution.py:780
  95.7 1.2 collective-permute-start
  96.9 1.2 collective-permute-done.theirs
  98.1 0.6 pair_sum.1
  98.7 21.8 %all_to_all.29.pieces = bf16[16,72,128]{2,1,0:T(8,128)(2,1)S(1)} all-to-all(bf16[16,72,128]{2,1,0:T(8,128)(2,1)S(1)} %bitcast.32), channel_id=1, replica_groups=mesh['chip'=2,'core'=2,'dev'=8] {'chip','dev'}, dimensions={0} | all-to-all | bytes 589824 | tf_op jit(solution)/shard_map/all_to_all | solution.py:1093
  120.6 0.6 spread_sum.1
  121.2 13.3 %all_to_all.30 = bf16[16,72,128]{2,1,0:T(8,128)(2,1)S(1)} all-to-all(bf16[16,72,128]{2,1,0:T(8,128)(2,1)S(1)} %spread_sum.1), channel_id=1, replica_groups=mesh['chip'=2,'core'=2,'dev'=8] {'chip','dev'}, dimensions={0} | all-to-all | bytes 589824 | tf_op jit(solution)/shard_map/all_to_all | solution.py:1095
  134.5 1.6 %collective-permute-done.1.theirs = bf16[1152,128]{1,0:T(8,128)(2,1)S(1)} collective-permute-done((bf16[1152,128]{1,0:T(8,128)(2,1)S(1)}, bf16[1152,128]{1,0:T(8,128)(2,1)S(1)}, u32[]{:S(2)}, u32[]{:S(2)}) %collective-permute-start.1) | collective-permute-done | bytes 294944 | tf_op jit(solution)/shard_map/ppermute | solution.py:1097
  136.2 3.9 %update.1 = (f32[1,1]{1,0:T(1,128)}, f32[2,128,256]{2,1,0:T(8,128)}, bf16[2,128,256]{2,1,0:T(8,128)(2,1)}, f32[2,128,128]{2,1,0:T(8,128)}, f32[2,256,256]{2,1,0:...) custom-call(s32[2]{0:T(128)S(1)} %pad_add_fusion.info, ...), custom_call_target="tpu_custom_call" | custom-call | bytes 14400000 | tf_op jit(solution)/shard_map/update/pallas_call | solution.py:976
  (37 shorter events, 0.1 us)
Async XLA Ops:
  2.0 14.5 %all-to-all-start = ((s32[32,1,256]{2,1,0:T(1,128)}), s32[32,1,256]{2,1,0:T(1,128)S(1)}, u32[]{:S(2)}, u32[]{:S(2)}) async-start(s32[32,1,256]{2,1,0:T(1,128)} %all_to_all.18), calls=%async_computation | async-start | bytes 65536 | tf_op jit(solution)/shard_map/all_to_all | solution.py:1030
  9.3 0.7 copy-start.20
  10.1 0.7 copy-start.21
  10.8 0.7 copy-start.25
  11.5 0.7 copy-start.26
  12.2 0.7 copy-start.27
  16.5 3.4 %copy-start = (f32[16384,128]{1,0:T(8,128)S(1)}, f32[16384,128]{1,0:T(8,128)}, u32[]{:S(2)}) copy-start(f32[16384,128]{1,0:T(8,128)} %table.3) | copy-start | bytes 25165828
  24.8 17.6 %copy-start.5 = (s32[4224,15]{0,1:T(8,128)S(1)}, s32[4224,15]{0,1:T(8,128)}, u32[]{:S(2)}) copy-start(s32[4224,15]{0,1:T(8,128)} %param.31) | copy-start | bytes 760324
  24.8 17.6 %copy-start.6 = (s32[4224,15]{0,1:T(8,128)S(1)}, s32[4224,15]{0,1:T(8,128)}, u32[]{:S(2)}) copy-start(s32[4224,15]{0,1:T(8,128)} %param.34) | copy-start | bytes 760324
  24.8 32.4 %all-to-all-start.1 = ((bf16[32,128,128]{2,1,0:T(8,128)(2,1)}), bf16[32,128,128]{2,1,0:T(8,128)(2,1)S(1)}, u32[]{:S(2)}, u32[]{:S(2)}) async-start(bf16[32,128,128]{2,1,0:T(8,128)(2,1)} %bitcast.13), calls=%async_computation.1 | async-start | bytes 2097152 | tf_op jit(solution)/shard_map/all_to_all | solution.py:1038
  30.5 3.4 %copy-start.1 = (f32[16384,128]{1,0:T(8,128)S(1)}, f32[16384,128]{1,0:T(8,128)}, u32[]{:S(2)}) copy-start(f32[16384,128]{1,0:T(8,128)} %table.3) | copy-start | bytes 25165828
  42.3 45.9 %copy-start.3 = (f32[2,256,256]{2,1,0:T(8,128)S(1)}, f32[2,256,256]{2,1,0:T(8,128)}, u32[]{:S(2)}) copy-start(f32[2,256,256]{2,1,0:T(8,128)} %refs_5_.3) | copy-start | bytes 1572868
  42.4 45.9 %copy-start.4 = (f32[2,256,172]{1,0,2:T(2,128)S(1)}, f32[2,256,172]{1,0,2:T(2,128)}, u32[]{:S(2)}) copy-start(f32[2,256,172]{1,0,2:T(2,128)} %param.41) | copy-start | bytes 1056772
  42.4 45.9 %copy-start.7 = (f32[2,128,256]{2,1,0:T(8,128)S(1)}, f32[2,128,256]{2,1,0:T(8,128)}, u32[]{:S(2)}) copy-start(f32[2,128,256]{2,1,0:T(8,128)} %refs_0_.1) | copy-start | bytes 786436
  42.4 45.9 %copy-start.22 = (f32[684]{0:T(1024)S(1)}, f32[684]{0:T(1024)}, u32[]{:S(2)}) copy-start(f32[684]{0:T(1024)} %biases.1) | copy-start | bytes 8212
  42.4 45.9 %copy-start.28 = (s32[64]{0:T(128)S(1)}, s32[64]{0:T(128)}, u32[]{:S(2)}) copy-start(s32[64]{0:T(128)} %refs_5_.2) | copy-start | bytes 772
  42.4 45.9 %copy-start.29 = (s32[64]{0:T(128)S(1)}, s32[64]{0:T(128)}, u32[]{:S(2)}) copy-start(s32[64]{0:T(128)} %refs_4_.2) | copy-start | bytes 772
  57.2 31.0 %copy-start.2 = (bf16[32,128,128]{2,1,0:T(8,128)(2,1)}, bf16[32,128,128]{2,1,0:T(8,128)(2,1)S(1)}, u32[]{:S(2)}) copy-start(bf16[32,128,128]{2,1,0:T(8,128)(2,1)S(1)} %all-to-all-done.1) | copy-start | bytes 3145732
  57.2 31.0 %all-to-all-start.2 = ((bf16[32,128,128]{2,1,0:T(8,128)(2,1)}), bf16[32,128,128]{2,1,0:T(8,128)(2,1)}, u32[]{:S(2)}, u32[]{:S(2)}) async-start(bf16[32,128,128]{2,1,0:T(8,128)(2,1)} %bitcast.15), calls=%async_computation.2 | async-start | bytes 2097152 | tf_op jit(solution)/shard_map/all_to_all | solution.py:1038
  88.3 47.8 %copy-start.8 = (f32[2,256,256]{2,1,0:T(8,128)S(1)}, f32[2,256,256]{2,1,0:T(8,128)}, u32[]{:S(2)}) copy-start(f32[2,256,256]{2,1,0:T(8,128)} %refs_2_.1) | copy-start | bytes 1572868
  88.3 47.8 %copy-start.9 = (f32[2,256,256]{2,1,0:T(8,128)S(1)}, f32[2,256,256]{2,1,0:T(8,128)}, u32[]{:S(2)}) copy-start(f32[2,256,256]{2,1,0:T(8,128)} %refs_4_.3) | copy-start | bytes 1572868
  88.3 47.8 %copy-start.10 = (f32[2,256,256]{2,1,0:T(8,128)S(1)}, f32[2,256,256]{2,1,0:T(8,128)}, u32[]{:S(2)}) copy-start(f32[2,256,256]{2,1,0:T(8,128)} %refs_6_.3) | copy-start | bytes 1572868
  88.3 47.8 %copy-start.11 = (f32[2,256,256]{2,1,0:T(8,128)S(1)}, f32[2,256,256]{2,1,0:T(8,128)}, u32[]{:S(2)}) copy-start(f32[2,256,256]{2,1,0:T(8,128)} %refs_7_.3) | copy-start | bytes 1572868
  88.3 47.8 %copy-start.12 = (f32[2,256,256]{2,1,0:T(8,128)S(1)}, f32[2,256,256]{2,1,0:T(8,128)}, u32[]{:S(2)}) copy-start(f32[2,256,256]{2,1,0:T(8,128)} %refs_8_.1) | copy-start | bytes 1572868
  88.3 47.8 %copy-start.13 = (f32[2,256,256]{2,1,0:T(8,128)S(1)}, f32[2,256,256]{2,1,0:T(8,128)}, u32[]{:S(2)}) copy-start(f32[2,256,256]{2,1,0:T(8,128)} %refs_9_.3) | copy-start | bytes 1572868
  88.4 47.8 %copy-start.14 = (f32[2,256,256]{2,1,0:T(8,128)S(1)}, f32[2,256,256]{2,1,0:T(8,128)}, u32[]{:S(2)}) copy-start(f32[2,256,256]{2,1,0:T(8,128)} %refs_12_.1) | copy-start | bytes 1572868
  88.4 47.8 %copy-start.15 = (f32[2,256,256]{2,1,0:T(8,128)S(1)}, f32[2,256,256]{2,1,0:T(8,128)}, u32[]{:S(2)}) copy-start(f32[2,256,256]{2,1,0:T(8,128)} %refs_14_.1) | copy-start | bytes 1572868
  88.4 47.8 %copy-start.16 = (f32[2,172,172]{2,0,1:T(2,128)S(1)}, f32[2,172,172]{2,0,1:T(2,128)}, u32[]{:S(2)}) copy-start(f32[2,172,172]{2,0,1:T(2,128)} %param.51) | copy-start | bytes 710020
  88.4 47.8 %copy-start.17 = (f32[2,172,172]{2,0,1:T(2,128)S(1)}, f32[2,172,172]{2,0,1:T(2,128)}, u32[]{:S(2)}) copy-start(f32[2,172,172]{2,0,1:T(2,128)} %param.57) | copy-start | bytes 710020
  88.4 47.8 %copy-start.18 = (f32[2,128,128]{2,1,0:T(8,128)S(1)}, f32[2,128,128]{2,1,0:T(8,128)}, u32[]{:S(2)}) copy-start(f32[2,128,128]{2,1,0:T(8,128)} %refs_1_.1) | copy-start | bytes 393220
  88.4 47.8 %copy-start.19 = (f32[2,128,128]{2,1,0:T(8,128)S(1)}, f32[2,128,128]{2,1,0:T(8,128)}, u32[]{:S(2)}) copy-start(f32[2,128,128]{2,1,0:T(8,128)} %refs_3_.1) | copy-start | bytes 393220
  88.4 47.8 %copy-start.23 = (f32[684]{0:T(1024)S(1)}, f32[684]{0:T(1024)}, u32[]{:S(2)}) copy-start(f32[684]{0:T(1024)} %moment_one.1) | copy-start | bytes 8212
  88.4 47.8 %copy-start.24 = (f32[684]{0:T(1024)S(1)}, f32[684]{0:T(1024)}, u32[]{:S(2)}) copy-start(f32[684]{0:T(1024)} %moment_two.1) | copy-start | bytes 8212
  95.7 2.4 %collective-permute-start = (bf16[1152,128]{1,0:T(8,128)(2,1)S(1)}, bf16[1152,128]{1,0:T(8,128)(2,1)S(1)}, u32[]{:S(2)}, u32[]{:S(2)}) collective-permute-start(bf16[1152,128]{1,0:T(8,128)(2,1)S(1)} %get-tuple-element.59), channel_id=1, source_target_pairs={{0,8},{8,0},{1,9},{9,1},{2,10},{10,2},{3,11},{11,3},{4,12},{12,4},... | collective-permute-start | bytes 884744 | tf_op jit(solution)/shard_map/ppermute | solution.py:1091
  134.5 1.6 %collective-permute-start.1 = (bf16[1152,128]{1,0:T(8,128)(2,1)S(1)}, bf16[1152,128]{1,0:T(8,128)(2,1)S(1)}, u32[]{:S(2)}, u32[]{:S(2)}) collective-permute-start(bf16[1152,128]{1,0:T(8,128)(2,1)S(1)} %bitcast.30), channel_id=1, source_target_pairs={{0,8},{8,0},{1,9},{9,1},{2,10},{10,2},{3,11},{11,3},{4,12},{12,4},... | collective-permute-start | bytes 884744 | tf_op jit(solution)/shard_map/ppermute | solution.py:1097

commit v5 on v4

--- a/solution.py
+++ b/solution.py
@@ -12,6 +12,7 @@
 PARTS = 2
 COUNTS = jnp.float8_e4m3fn
 BIG = 52 << 20
+ALL = (64 << 20) - (64 << 10)
 AXES = ("chip", "core", "dev")
 PEERS = ("chip", "dev")
 
@@ -83,7 +84,31 @@
     return (0, per // 2), (per // 2, per)
 
 
-def pick_kernel(lists, table, out, rows, done, wanted, sems, list_sems, *, first, part, per):
+def list_kernel(requests, out, sem):
+    copy = pltpu.make_async_copy(requests, out.at[:, 0, :], sem)
+    copy.start()
+    copy.wait()
+
+
+def as_lists(requests):
+    devices, per = requests.shape
+    return call(
+        list_kernel,
+        "as_lists",
+        jax.ShapeDtypeStruct((devices, 1, per), jnp.int32),
+        [anywhere],
+        anywhere,
+        [pltpu.SemaphoreType.DMA(())],
+        0.6,
+        ALL,
+    )(requests)
+
+
+def pick_kernel(
+    lists, source, out, rows, done, wanted, sems, list_sems, table, table_sem, *, first, part, per
+):
+    fill = pltpu.make_async_copy(source, table, table_sem)
+    fill.start()
     chunk = rows.shape[0]
     devices = chunk // part
     steps = out.shape[0] // chunk
@@ -94,6 +119,7 @@
 
     for step in range(steps):
         load(step).start()
+    fill.wait()
 
     def save(step):
         where = pl.ds(pl.multiple_of(step * chunk, chunk), chunk)
@@ -125,7 +151,7 @@
         functools.partial(pick_kernel, first=first, part=last - first, per=per),
         "pick_rows",
         jax.ShapeDtypeStruct((count, width), jnp.bfloat16),
-        [anywhere, vmem],
+        [anywhere, anywhere],
         anywhere,
         [
             pltpu.VMEM((chunk, width), jnp.float32),
@@ -133,9 +159,11 @@
             pltpu.SMEM(wanted.shape, jnp.int32),
             pltpu.SemaphoreType.DMA((count // chunk,)),
             pltpu.SemaphoreType.DMA((count // chunk,)),
+            pltpu.VMEM(table.shape, jnp.float32),
+            pltpu.SemaphoreType.DMA(()),
         ],
-        4.6,
-        20 << 20,
+        8.0,
+        ALL,
     )(wanted, table)
 
 
@@ -263,7 +291,7 @@
             pltpu.VMEM((area, LANES), jnp.bfloat16),
         ],
         3.0,
-        8 << 20,
+        ALL,
     )(adjacent_three.T, valid_three.T, labelled, adjacent_two.T, valid_two.T)
 
 
@@ -1027,7 +1055,7 @@
     core = lax.axis_index("core")
     own = lax.axis_index(PEERS)
 
-    wanted = lax.all_to_all(requests, AXES, split_axis=0, concat_axis=0, tiled=True)
+    wanted = lax.all_to_all(as_lists(requests), AXES, split_axis=0, concat_axis=0, tiled=True)
     names, places, near_two, near_three, count = reach(
         adjacent_three, valid_three, labelled, adjacent_two, valid_two, targets, per
     )

time: 141 us -> 141 us (level)
  Pallas kernels: 36.5 us -> 46 us
  local copies, waits for them, and re-layouts: 11.8 us -> 3.54 us
    unnamed x60 -> x66, local copies, waits for them, and re-layouts: 10.4 us -> 3.54 us
    pallas_call x2, Pallas kernels: 9.67 us -> 15.3 us  [pick_rows(): call(functools.partial(pick_kernel, first=first, part=last - first, per=p...]
    all_to_all x2, waiting for transfers between devices: 34.1 us -> 30.9 us  [trade(): lax.all_to_all(found.reshape(devices, -1, width), AXES, split_axis=0, con...]
    pallas_call x0 -> x1, Pallas kernels: none -> 2.11 us  [as_lists(): call(list_kernel, 'as_lists', jax.ShapeDtypeStruct((devices, 1, per), jnp...]
    all_to_all x1, waiting for transfers between devices: 1.02 us -> 2.84 us  [body(): lax.all_to_all(as_lists(requests), AXES, split_axis=0, concat_axis=0, til...]
    pallas_call x1, Pallas kernels: 2.64 us -> 4.16 us  [reach(): call(functools.partial(reach_kernel, rows_all=rows_all, per=per), 'reach'...]
  transfers between devices with their start and end apart: 5 -> 5, of which waited for: 5 -> 5; matrix products, arithmetic and copies ran while one was open for 0% -> 1% of each run, Pallas kernels for 14% -> 17%
where the time goes in v5:
time: 141 us; the launch traced here: 142 us
  Pallas kernels  46 us (33%)
  waiting for transfers between devices  36.5 us (26%)
  blocking collectives  34.1 us (24%)
  starting transfers between devices  18.2 us (13%)
  local copies, waits for them, and re-layouts  3.54 us (3%)
  between operations  2.07 us (1%)
    all_to_all x2, waiting for transfers between devices, trade(): lax.all_to_all(found.reshape(devices, -1, width), AXES, split_axis=0, con...  30.9 us
    all_to_all x1, blocking collectives, body(): lax.all_to_all(summed, PEERS, split_axis=0, concat_axis=0, tiled=True)  20.8 us
    pallas_call x2, Pallas kernels, pick_rows(): call(functools.partial(pick_kernel, first=first, part=last - first, per=p...  15.3 us
    all_to_all x1, blocking collectives, body(): lax.all_to_all(shared, PEERS, split_axis=0, concat_axis=0, tiled=True)  13.3 us
    all_to_all x2, starting transfers between devices, trade(): lax.all_to_all(found.reshape(devices, -1, width), AXES, split_axis=0, con...  9.57 us
    pallas_call x2, Pallas kernels, tally(): call(functools.partial(tally_kernel, per=per, which=which), 'early_sums'...  8.54 us
    all_to_all x1, starting transfers between devices, body(): lax.all_to_all(as_lists(requests), AXES, split_axis=0, concat_axis=0, til...  7.43 us
    pallas_call x1, Pallas kernels, run_step(): call(functools.partial(step_kernel, classes=classes), 'step', (jax.ShapeD...  7.25 us
  transfers between devices with their start and end apart: 5, of which 5 were waited for; matrix products, arithmetic and copies ran while one was open for 1% of the time, Pallas kernels for 17%

profile of v5, /device:TPU:0, one launch (start us, length us, event | category | flops | bytes accessed | tf_op | source)
XLA Modules:
  0.0 141.6 jit_solution(143511642005245240)
XLA Ops:
  0.6 2.1 %as_lists.1 = s32[32,1,256]{2,1,0:T(1,128)} custom-call(s32[32,256]{1,0:T(8,128)} %requests.1), custom_call_target="tpu_custom_call" | custom-call | bytes 2160000 | tf_op jit(solution)/shard_map/as_lists/pallas_call | solution.py:95
  2.8 7.4 %all-to-all-start = ((s32[32,1,256]{2,1,0:T(1,128)}), s32[32,1,256]{2,1,0:T(1,128)}, u32[]{:S(2)}, u32[]{:S(2)}) async-start(s32[32,1,256]{2,1,0:T(1,128)} %as_lists.1), calls=%async_computation | async-start | bytes 65536 | tf_op jit(solution)/shard_map/all_to_all | solution.py:1058
  10.2 4.2 %reach.1 = (s32[48,128]{1,0:T(8,128)}, s32[48,128]{1,0:T(8,128)}, s32[384,16]{1,0:T(8,128)}, s32[64,8]{1,0:T(8,128)}, s32[2]{0:T(128)}) custom-call(s32[5,64]{1,0:T(8,128)} %bitcast.45, s32[5,64]{1,0:T(8,128)} %bitcast.46, s32[64]{0:T(128)} %refs_5_.2, s32[10,384]{1,0:T(8,128)} %bitcast.43, s32[10,384]{1,0:T(8,128)} %bitcast.44), custom_call_target="tpu_custom_call" | custom-call | bytes 10800000 | tf_op jit(solution)/shard_map/reach/pallas_call | solution.py:277
  14.4 2.8 %all-to-all-done = s32[32,1,256]{2,1,0:T(1,128)} async-done(((s32[32,1,256]{2,1,0:T(1,128)}), s32[32,1,256]{2,1,0:T(1,128)}, u32[]{:S(2)}, u32[]{:S(2)}) %all-to-all-start) | async-done | bytes 32800 | tf_op jit(solution)/shard_map/all_to_all | solution.py:1058
  17.2 7.7 %pick_rows.3 = bf16[4096,128]{1,0:T(8,128)(2,1)} custom-call(s32[8192]{0:T(1024)} %bitcast.lists, f32[16384,128]{1,0:T(8,128)} %source.3), custom_call_target="tpu_custom_call" | custom-call | bytes 28800000 | tf_op jit(solution)/shard_map/pick_rows/pallas_call | solution.py:150
  24.9 3.4 %all-to-all-start.1 = ((bf16[32,128,128]{2,1,0:T(8,128)(2,1)}), bf16[32,128,128]{2,1,0:T(8,128)(2,1)}, u32[]{:S(2)}, u32[]{:S(2)}) async-start(bf16[32,128,128]{2,1,0:T(8,128)(2,1)} %bitcast.40), calls=%async_computation.1 | async-start | bytes 2097152 | tf_op jit(solution)/shard_map/all_to_all | solution.py:1066
  29.0 0.6 pad_add_fusion.info
  29.6 0.6 pad_maximum_fusion.fixes
  30.2 7.6 %pick_rows.2 = bf16[4096,128]{1,0:T(8,128)(2,1)} custom-call(s32[8192]{0:T(1024)} %bitcast.lists, f32[16384,128]{1,0:T(8,128)} %source.3), custom_call_target="tpu_custom_call" | custom-call | bytes 28800000 | tf_op jit(solution)/shard_map/pick_rows/pallas_call | solution.py:150
  37.8 0.0 copy-start.2
  37.8 0.0 copy-start.3
  37.8 0.0 copy-start.5
  37.8 1.0 copy-done.5
  38.8 0.7 copy-done.17
  39.6 0.7 copy-done.24
  40.2 3.6 %link_matrix.1.links = bf16[72,384,256]{2,1,0:T(8,128)(2,1)} custom-call(s32[2]{0:T(128)S(1)} %copy-done.24, s32[48,128]{1,0:T(8,128)S(1)} %copy-done.17, s32[384,16]{1,0:T(8,128)S(1)} %copy-done.5), custom_call_target="tpu_custom_call" | custom-call | bytes 18000000 | tf_op jit(solution)/shard_map/link_matrix/pallas_call | solution.py:493
  43.8 0.0 copy-start.18
  43.8 0.0 copy-start.25
  43.8 0.0 copy-start
  43.9 0.0 copy-start.1
  43.9 0.0 copy-start.4
  43.9 0.0 copy-start.6
  43.9 0.0 copy-start.21
  43.9 0.0 copy-start.26
  43.9 0.0 copy-start.29
  44.0 3.6 %tally.1.tallies = f8e4m3fn[4608,4096]{1,0:T(32,128)(4,1)} custom-call(s32[2]{0:T(128)S(1)} %copy-done.24, s32[6144]{0:T(1024)S(1)} %bitcast.37, s32[15,4224]{1,0:T(8,128)S(1)} %bitcast.31, s32[15,4224]{1,0:T(8,128)S(1)} %bitcast.33), custom_call_target="tpu_custom_call" | custom-call | bytes 50400000 | tf_op jit(solution)/shard_map/tally/pallas_call | solution.py:424
  47.5 8.3 %all-to-all-done.1 = bf16[32,128,128]{2,1,0:T(8,128)(2,1)} async-done(((bf16[32,128,128]{2,1,0:T(8,128)(2,1)}), bf16[32,128,128]{2,1,0:T(8,128)(2,1)}, u32[]{:S(2)}, u32[]{:S(2)}) %all-to-all-start.1) | async-done | bytes 1048608 | tf_op jit(solution)/shard_map/all_to_all | solution.py:1066
  55.8 6.2 %all-to-all-start.2 = ((bf16[32,128,128]{2,1,0:T(8,128)(2,1)}), bf16[32,128,128]{2,1,0:T(8,128)(2,1)S(1)}, u32[]{:S(2)}, u32[]{:S(2)}) async-start(bf16[32,128,128]{2,1,0:T(8,128)(2,1)} %bitcast.42), calls=%async_computation.2 | async-start | bytes 2097152 | tf_op jit(solution)/shard_map/all_to_all | solution.py:1066
  62.0 5.0 %early_sums.1.partial = f32[13824,256]{1,0:T(8,128)} custom-call(s32[2]{0:T(128)S(1)} %copy-done.25, s32[6144]{0:T(1024)S(1)} %bitcast.38, s32[15,4224]{1,0:T(8,128)S(1)} %bitcast.32, s32[15,4224]{1,0:T(8,128)S(1)} %bitcast.34, bf16[4096,128]{1,0:T(8,128)(2,1)} %bitcast.14.refs_0_), custom_call_target="tpu_custom_call" | custom-call | bytes 50400000 | tf_op jit(solution)/shard_map/early_sums/pallas_call | solution.py:424
  67.0 22.6 %all-to-all-done.2 = bf16[32,128,128]{2,1,0:T(8,128)(2,1)S(1)} async-done(((bf16[32,128,128]{2,1,0:T(8,128)(2,1)}), bf16[32,128,128]{2,1,0:T(8,128)(2,1)S(1)}, u32[]{:S(2)}, u32[]{:S(2)}) %all-to-all-start.2) | async-done | bytes 1048608 | tf_op jit(solution)/shard_map/all_to_all | solution.py:1066
  89.6 1.0 copy-done.32
  90.7 0.0 copy-start.7
  90.7 0.0 copy-start.8
  90.7 0.0 copy-start.11
  90.7 0.0 copy-start.12
  90.8 0.0 copy-start.14
  90.8 0.0 copy-start.15
  90.8 0.0 copy-start.20
  90.8 0.0 copy-start.27
  90.9 7.2 %step.1 = (bf16[1152,128]{1,0:T(8,128)(2,1)S(1)}, bf16[1152,128]{1,0:T(8,128)(2,1)S(1)}) custom-call(s32[2]{0:T(128)S(1)} %copy-done.26, s32[2]{0:T(128)S(1)} %copy-done.25, s32[6144]{0:T(1024)S(1)} %bitcast.39, f32[13824,256]{1,0:T(8,128)} %early_sums.1.partial, f8e4m3fn[4608,4096]{1,0:T(32,128)(4,1)} %tally.1.tallies, ...), custom_call_target="tpu_custom_call" | custom-call | bytes 50400000 | tf_op jit(solution)/shard_map/step/pallas_call | solution.py:808
  98.1 1.2 collective-permute-start
  99.3 1.2 collective-permute-done.theirs
  100.5 0.6 pair_sum.1
  101.2 20.8 %all_to_all.25.pieces = bf16[16,72,128]{2,1,0:T(8,128)(2,1)S(1)} all-to-all(bf16[16,72,128]{2,1,0:T(8,128)(2,1)S(1)} %bitcast.30), channel_id=1, replica_groups=mesh['chip'=2,'core'=2,'dev'=8] {'chip','dev'}, dimensions={0} | all-to-all | bytes 589824 | tf_op jit(solution)/shard_map/all_to_all | solution.py:1121
  122.0 0.6 spread_sum.1
  122.6 13.3 %all_to_all.26 = bf16[16,72,128]{2,1,0:T(8,128)(2,1)S(1)} all-to-all(bf16[16,72,128]{2,1,0:T(8,128)(2,1)S(1)} %spread_sum.1), channel_id=1, replica_groups=mesh['chip'=2,'core'=2,'dev'=8] {'chip','dev'}, dimensions={0} | all-to-all | bytes 589824 | tf_op jit(solution)/shard_map/all_to_all | solution.py:1123
  135.9 1.6 %collective-permute-done.1.theirs = bf16[1152,128]{1,0:T(8,128)(2,1)S(1)} collective-permute-done((bf16[1152,128]{1,0:T(8,128)(2,1)S(1)}, bf16[1152,128]{1,0:T(8,128)(2,1)S(1)}, u32[]{:S(2)}, u32[]{:S(2)}) %collective-permute-start.1) | collective-permute-done | bytes 294944 | tf_op jit(solution)/shard_map/ppermute | solution.py:1125
  137.6 3.9 %update.1 = (f32[1,1]{1,0:T(1,128)}, f32[2,128,256]{2,1,0:T(8,128)}, bf16[2,128,256]{2,1,0:T(8,128)(2,1)}, f32[2,128,128]{2,1,0:T(8,128)}, f32[2,256,256]{2,1,0:...) custom-call(s32[2]{0:T(128)S(1)} %copy-done.26, ...), custom_call_target="tpu_custom_call" | custom-call | bytes 14400000 | tf_op jit(solution)/shard_map/update/pallas_call | solution.py:1004
  (43 shorter events, 0.1 us)
Async XLA Ops:
  2.8 14.4 %all-to-all-start = ((s32[32,1,256]{2,1,0:T(1,128)}), s32[32,1,256]{2,1,0:T(1,128)}, u32[]{:S(2)}, u32[]{:S(2)}) async-start(s32[32,1,256]{2,1,0:T(1,128)} %as_lists.1), calls=%async_computation | async-start | bytes 65536 | tf_op jit(solution)/shard_map/all_to_all | solution.py:1058
  24.9 31.0 %all-to-all-start.1 = ((bf16[32,128,128]{2,1,0:T(8,128)(2,1)}), bf16[32,128,128]{2,1,0:T(8,128)(2,1)}, u32[]{:S(2)}, u32[]{:S(2)}) async-start(bf16[32,128,128]{2,1,0:T(8,128)(2,1)} %bitcast.40), calls=%async_computation.1 | async-start | bytes 2097152 | tf_op jit(solution)/shard_map/all_to_all | solution.py:1066
  37.8 6.0 %copy-start.2 = (s32[4224,15]{0,1:T(8,128)S(1)}, s32[4224,15]{0,1:T(8,128)}, u32[]{:S(2)}) copy-start(s32[4224,15]{0,1:T(8,128)} %param.31) | copy-start | bytes 760324
  37.8 6.0 %copy-start.3 = (s32[4224,15]{0,1:T(8,128)S(1)}, s32[4224,15]{0,1:T(8,128)}, u32[]{:S(2)}) copy-start(s32[4224,15]{0,1:T(8,128)} %param.34) | copy-start | bytes 760324
  37.8 1.0 copy-start.5
  38.8 0.7 copy-start.17
  39.6 0.7 copy-start.24
  43.8 18.2 %copy-start.18 = (s32[48,128]{1,0:T(8,128)S(1)}, s32[48,128]{1,0:T(8,128)}, u32[]{:S(2)}) copy-start(s32[48,128]{1,0:T(8,128)} %get-tuple-element.49.names) | copy-start | bytes 73732
  43.8 18.2 %copy-start.25 = (s32[2]{0:T(128)S(1)}, s32[2]{0:T(128)}, u32[]{:S(2)}) copy-start(s32[2]{0:T(128)} %get-tuple-element.48.count) | copy-start | bytes 28
  43.8 46.8 %copy-start = (f32[2,256,256]{2,1,0:T(8,128)S(1)}, f32[2,256,256]{2,1,0:T(8,128)}, u32[]{:S(2)}) copy-start(f32[2,256,256]{2,1,0:T(8,128)} %refs_5_.3) | copy-start | bytes 1572868
  43.9 46.8 %copy-start.1 = (f32[2,256,172]{1,0,2:T(2,128)S(1)}, f32[2,256,172]{1,0,2:T(2,128)}, u32[]{:S(2)}) copy-start(f32[2,256,172]{1,0,2:T(2,128)} %param.41) | copy-start | bytes 1056772
  43.9 46.7 %copy-start.4 = (f32[2,128,256]{2,1,0:T(8,128)S(1)}, f32[2,128,256]{2,1,0:T(8,128)}, u32[]{:S(2)}) copy-start(f32[2,128,256]{2,1,0:T(8,128)} %refs_0_.1) | copy-start | bytes 786436
  43.9 46.7 %copy-start.6 = (s32[384,16]{1,0:T(8,128)S(1)}, s32[384,16]{1,0:T(8,128)}, u32[]{:S(2)}) copy-start(s32[384,16]{1,0:T(8,128)} %get-tuple-element.50.near.refs_2_) | copy-start | bytes 73732
  43.9 46.7 %copy-start.21 = (s32[64,8]{1,0:T(8,128)S(1)}, s32[64,8]{1,0:T(8,128)}, u32[]{:S(2)}) copy-start(s32[64,8]{1,0:T(8,128)} %get-tuple-element.57.refs_3_) | copy-start | bytes 6148
  43.9 46.7 %copy-start.22 = (s32[48,128]{1,0:T(8,128)S(1)}, s32[48,128]{1,0:T(8,128)}, u32[]{:S(2)}) copy-start(s32[48,128]{1,0:T(8,128)} %get-tuple-element.53) | copy-start | bytes 73732
  43.9 46.7 %copy-start.23 = (f32[684]{0:T(1024)S(1)}, f32[684]{0:T(1024)}, u32[]{:S(2)}) copy-start(f32[684]{0:T(1024)} %biases.1) | copy-start | bytes 8212
  43.9 46.7 %copy-start.26 = (s32[2]{0:T(128)S(1)}, s32[2]{0:T(128)}, u32[]{:S(2)}) copy-start(s32[2]{0:T(128)} %pad_add_fusion.info) | copy-start | bytes 28
  43.9 46.7 %copy-start.29 = (s32[64]{0:T(128)S(1)}, s32[64]{0:T(128)}, u32[]{:S(2)}) copy-start(s32[64]{0:T(128)} %refs_5_.2) | copy-start | bytes 772
  44.0 46.7 %copy-start.30 = (s32[64]{0:T(128)S(1)}, s32[64]{0:T(128)}, u32[]{:S(2)}) copy-start(s32[64]{0:T(128)} %refs_4_.2) | copy-start | bytes 772
  55.8 33.8 %all-to-all-start.2 = ((bf16[32,128,128]{2,1,0:T(8,128)(2,1)}), bf16[32,128,128]{2,1,0:T(8,128)(2,1)S(1)}, u32[]{:S(2)}, u32[]{:S(2)}) async-start(bf16[32,128,128]{2,1,0:T(8,128)(2,1)} %bitcast.42), calls=%async_computation.2 | async-start | bytes 2097152 | tf_op jit(solution)/shard_map/all_to_all | solution.py:1066
  89.6 1.0 copy-start.32
  90.7 46.8 %copy-start.7 = (f32[2,256,256]{2,1,0:T(8,128)S(1)}, f32[2,256,256]{2,1,0:T(8,128)}, u32[]{:S(2)}) copy-start(f32[2,256,256]{2,1,0:T(8,128)} %refs_2_.1) | copy-start | bytes 1572868
  90.7 46.8 %copy-start.8 = (f32[2,256,256]{2,1,0:T(8,128)S(1)}, f32[2,256,256]{2,1,0:T(8,128)}, u32[]{:S(2)}) copy-start(f32[2,256,256]{2,1,0:T(8,128)} %refs_4_.3) | copy-start | bytes 1572868
  90.7 46.8 %copy-start.9 = (f32[2,256,256]{2,1,0:T(8,128)S(1)}, f32[2,256,256]{2,1,0:T(8,128)}, u32[]{:S(2)}) copy-start(f32[2,256,256]{2,1,0:T(8,128)} %refs_6_.3) | copy-start | bytes 1572868
  90.7 46.8 %copy-start.10 = (f32[2,256,256]{2,1,0:T(8,128)S(1)}, f32[2,256,256]{2,1,0:T(8,128)}, u32[]{:S(2)}) copy-start(f32[2,256,256]{2,1,0:T(8,128)} %refs_7_.3) | copy-start | bytes 1572868
  90.7 46.8 %copy-start.11 = (f32[2,256,256]{2,1,0:T(8,128)S(1)}, f32[2,256,256]{2,1,0:T(8,128)}, u32[]{:S(2)}) copy-start(f32[2,256,256]{2,1,0:T(8,128)} %refs_8_.1) | copy-start | bytes 1572868
  90.7 46.8 %copy-start.12 = (f32[2,256,256]{2,1,0:T(8,128)S(1)}, f32[2,256,256]{2,1,0:T(8,128)}, u32[]{:S(2)}) copy-start(f32[2,256,256]{2,1,0:T(8,128)} %refs_9_.3) | copy-start | bytes 1572868
  90.8 46.8 %copy-start.13 = (f32[2,256,256]{2,1,0:T(8,128)S(1)}, f32[2,256,256]{2,1,0:T(8,128)}, u32[]{:S(2)}) copy-start(f32[2,256,256]{2,1,0:T(8,128)} %refs_12_.1) | copy-start | bytes 1572868
  90.8 46.8 %copy-start.14 = (f32[2,256,256]{2,1,0:T(8,128)S(1)}, f32[2,256,256]{2,1,0:T(8,128)}, u32[]{:S(2)}) copy-start(f32[2,256,256]{2,1,0:T(8,128)} %refs_14_.1) | copy-start | bytes 1572868
  90.8 46.8 %copy-start.15 = (f32[2,172,172]{2,0,1:T(2,128)S(1)}, f32[2,172,172]{2,0,1:T(2,128)}, u32[]{:S(2)}) copy-start(f32[2,172,172]{2,0,1:T(2,128)} %param.51) | copy-start | bytes 710020
  90.8 46.8 %copy-start.16 = (f32[2,172,172]{2,0,1:T(2,128)S(1)}, f32[2,172,172]{2,0,1:T(2,128)}, u32[]{:S(2)}) copy-start(f32[2,172,172]{2,0,1:T(2,128)} %param.57) | copy-start | bytes 710020
  90.8 46.8 %copy-start.19 = (f32[2,128,128]{2,1,0:T(8,128)S(1)}, f32[2,128,128]{2,1,0:T(8,128)}, u32[]{:S(2)}) copy-start(f32[2,128,128]{2,1,0:T(8,128)} %refs_1_.1) | copy-start | bytes 393220
  90.8 46.8 %copy-start.20 = (f32[2,128,128]{2,1,0:T(8,128)S(1)}, f32[2,128,128]{2,1,0:T(8,128)}, u32[]{:S(2)}) copy-start(f32[2,128,128]{2,1,0:T(8,128)} %refs_3_.1) | copy-start | bytes 393220
  90.8 46.7 %copy-start.27 = (f32[684]{0:T(1024)S(1)}, f32[684]{0:T(1024)}, u32[]{:S(2)}) copy-start(f32[684]{0:T(1024)} %moment_one.1) | copy-start | bytes 8212
  90.8 46.7 %copy-start.28 = (f32[684]{0:T(1024)S(1)}, f32[684]{0:T(1024)}, u32[]{:S(2)}) copy-start(f32[684]{0:T(1024)} %moment_two.1) | copy-start | bytes 8212
  90.8 46.7 %copy-start.31 = (f32[2]{0:T(128)S(1)}, f32[2]{0:T(128)}, u32[]{:S(2)}) copy-start(f32[2]{0:T(128)} %pad_maximum_fusion.fixes) | copy-start | bytes 28
  98.1 2.4 %collective-permute-start = (bf16[1152,128]{1,0:T(8,128)(2,1)S(1)}, bf16[1152,128]{1,0:T(8,128)(2,1)S(1)}, u32[]{:S(2)}, u32[]{:S(2)}) collective-permute-start(bf16[1152,128]{1,0:T(8,128)(2,1)S(1)} %get-tuple-element.59), channel_id=1, source_target_pairs={{0,8},{8,0},{1,9},{9,1},{2,10},{10,2},{3,11},{11,3},{4,12},{12,4},... | collective-permute-start | bytes 884744 | tf_op jit(solution)/shard_map/ppermute | solution.py:1119
  135.9 1.6 %collective-permute-start.1 = (bf16[1152,128]{1,0:T(8,128)(2,1)S(1)}, bf16[1152,128]{1,0:T(8,128)(2,1)S(1)}, u32[]{:S(2)}, u32[]{:S(2)}) collective-permute-start(bf16[1152,128]{1,0:T(8,128)(2,1)S(1)} %bitcast.28), channel_id=1, source_target_pairs={{0,8},{8,0},{1,9},{9,1},{2,10},{10,2},{3,11},{11,3},{4,12},{12,4},... | collective-permute-start | bytes 884744 | tf_op jit(solution)/shard_map/ppermute | solution.py:1125

commit v6 on v4

--- a/solution.py
+++ b/solution.py
@@ -12,6 +12,7 @@
 PARTS = 2
 COUNTS = jnp.float8_e4m3fn
 BIG = 52 << 20
+MOST = 57 << 20
 AXES = ("chip", "core", "dev")
 PEERS = ("chip", "dev")
 
@@ -83,7 +84,11 @@
     return (0, per // 2), (per // 2, per)
 
 
-def pick_kernel(lists, table, out, rows, done, wanted, sems, list_sems, *, first, part, per):
+def pick_kernel(
+    lists, source, out, rows, done, wanted, sems, list_sems, table, table_sem, *, first, part, per
+):
+    fill = pltpu.make_async_copy(source, table, table_sem)
+    fill.start()
     chunk = rows.shape[0]
     devices = chunk // part
     steps = out.shape[0] // chunk
@@ -94,6 +99,7 @@
 
     for step in range(steps):
         load(step).start()
+    fill.wait()
 
     def save(step):
         where = pl.ds(pl.multiple_of(step * chunk, chunk), chunk)
@@ -125,7 +131,7 @@
         functools.partial(pick_kernel, first=first, part=last - first, per=per),
         "pick_rows",
         jax.ShapeDtypeStruct((count, width), jnp.bfloat16),
-        [anywhere, vmem],
+        [anywhere, anywhere],
         anywhere,
         [
             pltpu.VMEM((chunk, width), jnp.float32),
@@ -133,9 +139,11 @@
             pltpu.SMEM(wanted.shape, jnp.int32),
             pltpu.SemaphoreType.DMA((count // chunk,)),
             pltpu.SemaphoreType.DMA((count // chunk,)),
+            pltpu.VMEM(table.shape, jnp.float32),
+            pltpu.SemaphoreType.DMA(()),
         ],
-        4.6,
-        20 << 20,
+        8.0,
+        MOST,
     )(wanted, table)
 
 

time: 141 us -> 141 us (level)
  local copies, waits for them, and re-layouts: 11.8 us -> 5.65 us
  Pallas kernels: 36.5 us -> 42.1 us
    unnamed x60 -> x58, local copies, waits for them, and re-layouts: 10.4 us -> 4.25 us
    pallas_call x2, Pallas kernels: 9.67 us -> 15.3 us  [pick_rows(): call(functools.partial(pick_kernel, first=first, part=last - first, per=p...]
  transfers between devices with their start and end apart: 5 -> 5, of which waited for: 5 -> 5; matrix products, arithmetic and copies ran while one was open for 0% -> 0% of each run, Pallas kernels for 14% -> 16%
where the time goes in v6:
time: 141 us; the launch traced here: 140 us
  Pallas kernels  42.1 us (30%)
  waiting for transfers between devices  38.5 us (27%)
  blocking collectives  35.2 us (25%)
  starting transfers between devices  16.7 us (12%)
  local copies, waits for them, and re-layouts  5.65 us (4%)
  between operations  1.97 us (1%)
    all_to_all x2, waiting for transfers between devices, trade(): lax.all_to_all(found.reshape(devices, -1, width), AXES, split_axis=0, con...  34.7 us
    all_to_all x1, blocking collectives, body(): lax.all_to_all(summed, PEERS, split_axis=0, concat_axis=0, tiled=True)  21.9 us
    pallas_call x2, Pallas kernels, pick_rows(): call(functools.partial(pick_kernel, first=first, part=last - first, per=p...  15.3 us
    all_to_all x1, blocking collectives, body(): lax.all_to_all(shared, PEERS, split_axis=0, concat_axis=0, tiled=True)  13.3 us
    pallas_call x2, Pallas kernels, tally(): call(functools.partial(tally_kernel, per=per, which=which), 'early_sums'...  8.22 us
    all_to_all x2, starting transfers between devices, trade(): lax.all_to_all(found.reshape(devices, -1, width), AXES, split_axis=0, con...  8.2 us
    all_to_all x1, starting transfers between devices, body(): lax.all_to_all(requests, AXES, split_axis=0, concat_axis=0, tiled=True)  7.3 us
    pallas_call x1, Pallas kernels, run_step(): call(functools.partial(step_kernel, classes=classes), 'step', (jax.ShapeD...  7.28 us
  transfers between devices with their start and end apart: 5, of which 5 were waited for; matrix products, arithmetic and copies ran while one was open for 0% of the time, Pallas kernels for 16%

profile of v6, /device:TPU:0, one launch (start us, length us, event | category | flops | bytes accessed | tf_op | source)
XLA Modules:
  0.0 140.4 jit_solution(15154398877953522010)
XLA Ops:
  0.6 1.4 all_to_all.18
  2.0 7.3 %all-to-all-start = ((s32[32,1,256]{2,1,0:T(1,128)}), s32[32,1,256]{2,1,0:T(1,128)S(1)}, u32[]{:S(2)}, u32[]{:S(2)}) async-start(s32[32,1,256]{2,1,0:T(1,128)} %all_to_all.18), calls=%async_computation | async-start | bytes 65536 | tf_op jit(solution)/shard_map/all_to_all | solution.py:1038
  9.3 0.0 copy-start.18
  9.4 0.7 copy-done.18
  10.1 0.7 copy-done.19
  10.8 0.7 copy-done.23
  11.5 0.7 copy-done.24
  12.2 0.7 copy-done.25
  12.9 2.6 %reach.1 = (s32[48,128]{1,0:T(8,128)S(1)}, s32[48,128]{1,0:T(8,128)S(1)}, s32[384,16]{1,0:T(8,128)S(1)}, s32[64,8]{1,0:T(8,128)S(1)}, s32[2]{0:T(128)S(1)}) custom-call(s32[5,64]{1,0:T(8,128)S(1)} %bitcast.44, s32[5,64]{1,0:T(8,128)S(1)} %bitcast.45, s32[64]{0:T(128)S(1)} %copy-done.25, s32[10,384]{1,0:T(8,128)S(1)} %bitcast.42, s32[10,384]{1,0:T(8,128)S(1)} %bitcast.43), custom_call_target="tpu_custom_call" | custom-call | bytes 10800000 | tf_op jit(solution)/shard_map/reach/pallas_call | solution.py:257
  15.5 1.0 all-to-all-done
  16.5 0.6 copy-done.28
  17.1 7.7 %pick_rows.3 = bf16[4096,128]{1,0:T(8,128)(2,1)} custom-call(s32[8192]{0:T(1024)} %bitcast.48, f32[16384,128]{1,0:T(8,128)} %source.3), custom_call_target="tpu_custom_call" | custom-call | bytes 28800000 | tf_op jit(solution)/shard_map/pick_rows/pallas_call | solution.py:130
  24.8 0.0 copy-start.3
  24.8 0.0 copy-start.4
  24.8 4.8 %all-to-all-start.1 = ((bf16[32,128,128]{2,1,0:T(8,128)(2,1)}), bf16[32,128,128]{2,1,0:T(8,128)(2,1)S(1)}, u32[]{:S(2)}, u32[]{:S(2)}) async-start(bf16[32,128,128]{2,1,0:T(8,128)(2,1)} %bitcast.46), calls=%async_computation.1 | async-start | bytes 2097152 | tf_op jit(solution)/shard_map/all_to_all | solution.py:1046
  30.4 0.1 pad_add_fusion.info
  30.5 0.1 pad_maximum_fusion.fixes
  30.6 7.6 %pick_rows.2 = bf16[4096,128]{1,0:T(8,128)(2,1)} custom-call(s32[8192]{0:T(1024)} %bitcast.49, f32[16384,128]{1,0:T(8,128)} %source.3), custom_call_target="tpu_custom_call" | custom-call | bytes 28800000 | tf_op jit(solution)/shard_map/pick_rows/pallas_call | solution.py:130
  38.2 3.6 %link_matrix.1.links = bf16[72,384,256]{2,1,0:T(8,128)(2,1)} custom-call(s32[2]{0:T(128)S(1)} %get-tuple-element.48.count, s32[48,128]{1,0:T(8,128)S(1)} %get-tuple-element.49.names, s32[384,16]{1,0:T(8,128)S(1)} %get-tuple-element.50.near.refs_2_), custom_call_target="tpu_custom_call" | custom-call | bytes 18000000 | tf_op jit(solution)/shard_map/link_matrix/pallas_call | solution.py:473
  41.8 0.0 copy-start.1
  41.8 0.0 copy-start.2
  41.8 0.0 copy-start.5
  41.8 0.0 copy-start.20
  41.9 0.0 copy-start.26
  41.9 0.0 copy-start.27
  41.9 3.5 %tally.1.tallies = f8e4m3fn[4608,4096]{1,0:T(32,128)(4,1)} custom-call(s32[2]{0:T(128)S(1)} %get-tuple-element.48.count, s32[6144]{0:T(1024)S(1)} %bitcast.39, s32[15,4224]{1,0:T(8,128)S(1)} %bitcast.33, s32[15,4224]{1,0:T(8,128)S(1)} %bitcast.35), custom_call_target="tpu_custom_call" | custom-call | bytes 50400000 | tf_op jit(solution)/shard_map/tally/pallas_call | solution.py:404
  45.4 11.8 %all-to-all-done.1 = bf16[32,128,128]{2,1,0:T(8,128)(2,1)S(1)} async-done(((bf16[32,128,128]{2,1,0:T(8,128)(2,1)}), bf16[32,128,128]{2,1,0:T(8,128)(2,1)S(1)}, u32[]{:S(2)}, u32[]{:S(2)}) %all-to-all-start.1) | async-done | bytes 1048608 | tf_op jit(solution)/shard_map/all_to_all | solution.py:1046
  57.3 3.4 %all-to-all-start.2 = ((bf16[32,128,128]{2,1,0:T(8,128)(2,1)}), bf16[32,128,128]{2,1,0:T(8,128)(2,1)}, u32[]{:S(2)}, u32[]{:S(2)}) async-start(bf16[32,128,128]{2,1,0:T(8,128)(2,1)} %bitcast.47), calls=%async_computation.2 | async-start | bytes 2097152 | tf_op jit(solution)/shard_map/all_to_all | solution.py:1046
  60.7 4.7 %early_sums.1.partial = f32[13824,256]{1,0:T(8,128)} custom-call(s32[2]{0:T(128)S(1)} %get-tuple-element.48.count, s32[6144]{0:T(1024)S(1)} %bitcast.40, s32[15,4224]{1,0:T(8,128)S(1)} %bitcast.34, s32[15,4224]{1,0:T(8,128)S(1)} %bitcast.36, bf16[4096,128]{1,0:T(8,128)(2,1)S(1)} %bitcast.26), custom_call_target="tpu_custom_call" | custom-call | bytes 50400000 | tf_op jit(solution)/shard_map/early_sums/pallas_call | solution.py:404
  65.3 22.9 %all-to-all-done.2 = bf16[32,128,128]{2,1,0:T(8,128)(2,1)} async-done(((bf16[32,128,128]{2,1,0:T(8,128)(2,1)}), bf16[32,128,128]{2,1,0:T(8,128)(2,1)}, u32[]{:S(2)}, u32[]{:S(2)}) %all-to-all-start.2) | async-done | bytes 1048608 | tf_op jit(solution)/shard_map/all_to_all | solution.py:1046
  88.3 0.0 copy-start.6
  88.3 0.0 copy-start.7
  88.3 0.0 copy-start.8
  88.3 0.0 copy-start.10
  88.3 0.0 copy-start.11
  88.4 0.0 copy-start.14
  88.4 0.0 copy-start.15
  88.4 0.0 copy-start.21
  88.4 0.0 copy-start.22
  88.4 7.3 %step.1 = (bf16[1152,128]{1,0:T(8,128)(2,1)S(1)}, bf16[1152,128]{1,0:T(8,128)(2,1)S(1)}) custom-call(s32[2]{0:T(128)S(1)} %pad_add_fusion.info, s32[2]{0:T(128)S(1)} %get-tuple-element.48.count, s32[6144]{0:T(1024)S(1)} %bitcast.41, f32[13824,256]{1,0:T(8,128)} %early_sums.1.partial, f8e4m3fn[4608,4096]{1,0:T(32,128)(4,1)} %tally.1.tallies, ...), custom_call_target="tpu_custom_call" | custom-call | bytes 50400000 | tf_op jit(solution)/shard_map/step/pallas_call | solution.py:788
  95.7 1.2 collective-permute-start
  97.0 1.2 collective-permute-done.theirs
  98.2 0.6 pair_sum.1
  98.8 21.9 %all_to_all.29.pieces = bf16[16,72,128]{2,1,0:T(8,128)(2,1)S(1)} all-to-all(bf16[16,72,128]{2,1,0:T(8,128)(2,1)S(1)} %bitcast.32), channel_id=1, replica_groups=mesh['chip'=2,'core'=2,'dev'=8] {'chip','dev'}, dimensions={0} | all-to-all | bytes 589824 | tf_op jit(solution)/shard_map/all_to_all | solution.py:1101
  120.7 0.6 spread_sum.1
  121.3 13.3 %all_to_all.30 = bf16[16,72,128]{2,1,0:T(8,128)(2,1)S(1)} all-to-all(bf16[16,72,128]{2,1,0:T(8,128)(2,1)S(1)} %spread_sum.1), channel_id=1, replica_groups=mesh['chip'=2,'core'=2,'dev'=8] {'chip','dev'}, dimensions={0} | all-to-all | bytes 589824 | tf_op jit(solution)/shard_map/all_to_all | solution.py:1103
  134.6 1.6 %collective-permute-done.1.theirs = bf16[1152,128]{1,0:T(8,128)(2,1)S(1)} collective-permute-done((bf16[1152,128]{1,0:T(8,128)(2,1)S(1)}, bf16[1152,128]{1,0:T(8,128)(2,1)S(1)}, u32[]{:S(2)}, u32[]{:S(2)}) %collective-permute-start.1) | collective-permute-done | bytes 294944 | tf_op jit(solution)/shard_map/ppermute | solution.py:1105
  136.3 3.9 %update.1 = (f32[1,1]{1,0:T(1,128)}, f32[2,128,256]{2,1,0:T(8,128)}, bf16[2,128,256]{2,1,0:T(8,128)(2,1)}, f32[2,128,128]{2,1,0:T(8,128)}, f32[2,256,256]{2,1,0:...) custom-call(s32[2]{0:T(128)S(1)} %pad_add_fusion.info, ...), custom_call_target="tpu_custom_call" | custom-call | bytes 14400000 | tf_op jit(solution)/shard_map/update/pallas_call | solution.py:984
  (35 shorter events, 0.1 us)
Async XLA Ops:
  2.0 14.5 %all-to-all-start = ((s32[32,1,256]{2,1,0:T(1,128)}), s32[32,1,256]{2,1,0:T(1,128)S(1)}, u32[]{:S(2)}, u32[]{:S(2)}) async-start(s32[32,1,256]{2,1,0:T(1,128)} %all_to_all.18), calls=%async_computation | async-start | bytes 65536 | tf_op jit(solution)/shard_map/all_to_all | solution.py:1038
  9.3 0.7 copy-start.18
  10.1 0.7 copy-start.19
  10.8 0.7 copy-start.23
  11.5 0.7 copy-start.24
  12.2 0.7 copy-start.25
  16.5 0.6 copy-start.28
  24.8 17.0 %copy-start.3 = (s32[4224,15]{0,1:T(8,128)S(1)}, s32[4224,15]{0,1:T(8,128)}, u32[]{:S(2)}) copy-start(s32[4224,15]{0,1:T(8,128)} %param.31) | copy-start | bytes 760324
  24.8 17.0 %copy-start.4 = (s32[4224,15]{0,1:T(8,128)S(1)}, s32[4224,15]{0,1:T(8,128)}, u32[]{:S(2)}) copy-start(s32[4224,15]{0,1:T(8,128)} %param.34) | copy-start | bytes 760324
  24.8 32.4 %all-to-all-start.1 = ((bf16[32,128,128]{2,1,0:T(8,128)(2,1)}), bf16[32,128,128]{2,1,0:T(8,128)(2,1)S(1)}, u32[]{:S(2)}, u32[]{:S(2)}) async-start(bf16[32,128,128]{2,1,0:T(8,128)(2,1)} %bitcast.46), calls=%async_computation.1 | async-start | bytes 2097152 | tf_op jit(solution)/shard_map/all_to_all | solution.py:1046
  41.8 46.4 %copy-start.1 = (f32[2,256,256]{2,1,0:T(8,128)S(1)}, f32[2,256,256]{2,1,0:T(8,128)}, u32[]{:S(2)}) copy-start(f32[2,256,256]{2,1,0:T(8,128)} %refs_5_.3) | copy-start | bytes 1572868
  41.8 46.4 %copy-start.2 = (f32[2,256,172]{1,0,2:T(2,128)S(1)}, f32[2,256,172]{1,0,2:T(2,128)}, u32[]{:S(2)}) copy-start(f32[2,256,172]{1,0,2:T(2,128)} %param.41) | copy-start | bytes 1056772
  41.8 46.4 %copy-start.5 = (f32[2,128,256]{2,1,0:T(8,128)S(1)}, f32[2,128,256]{2,1,0:T(8,128)}, u32[]{:S(2)}) copy-start(f32[2,128,256]{2,1,0:T(8,128)} %refs_0_.1) | copy-start | bytes 786436
  41.8 46.4 %copy-start.20 = (f32[684]{0:T(1024)S(1)}, f32[684]{0:T(1024)}, u32[]{:S(2)}) copy-start(f32[684]{0:T(1024)} %biases.1) | copy-start | bytes 8212
  41.9 46.4 %copy-start.26 = (s32[64]{0:T(128)S(1)}, s32[64]{0:T(128)}, u32[]{:S(2)}) copy-start(s32[64]{0:T(128)} %refs_5_.2) | copy-start | bytes 772
  41.9 46.4 %copy-start.27 = (s32[64]{0:T(128)S(1)}, s32[64]{0:T(128)}, u32[]{:S(2)}) copy-start(s32[64]{0:T(128)} %refs_4_.2) | copy-start | bytes 772
  57.3 31.0 %copy-start = (bf16[32,128,128]{2,1,0:T(8,128)(2,1)}, bf16[32,128,128]{2,1,0:T(8,128)(2,1)S(1)}, u32[]{:S(2)}) copy-start(bf16[32,128,128]{2,1,0:T(8,128)(2,1)S(1)} %all-to-all-done.1) | copy-start | bytes 3145732
  57.3 30.9 %all-to-all-start.2 = ((bf16[32,128,128]{2,1,0:T(8,128)(2,1)}), bf16[32,128,128]{2,1,0:T(8,128)(2,1)}, u32[]{:S(2)}, u32[]{:S(2)}) async-start(bf16[32,128,128]{2,1,0:T(8,128)(2,1)} %bitcast.47), calls=%async_computation.2 | async-start | bytes 2097152 | tf_op jit(solution)/shard_map/all_to_all | solution.py:1046
  88.3 47.9 %copy-start.6 = (f32[2,256,256]{2,1,0:T(8,128)S(1)}, f32[2,256,256]{2,1,0:T(8,128)}, u32[]{:S(2)}) copy-start(f32[2,256,256]{2,1,0:T(8,128)} %refs_2_.1) | copy-start | bytes 1572868
  88.3 47.9 %copy-start.7 = (f32[2,256,256]{2,1,0:T(8,128)S(1)}, f32[2,256,256]{2,1,0:T(8,128)}, u32[]{:S(2)}) copy-start(f32[2,256,256]{2,1,0:T(8,128)} %refs_4_.3) | copy-start | bytes 1572868
  88.3 47.9 %copy-start.8 = (f32[2,256,256]{2,1,0:T(8,128)S(1)}, f32[2,256,256]{2,1,0:T(8,128)}, u32[]{:S(2)}) copy-start(f32[2,256,256]{2,1,0:T(8,128)} %refs_6_.3) | copy-start | bytes 1572868
  88.3 47.9 %copy-start.9 = (f32[2,256,256]{2,1,0:T(8,128)S(1)}, f32[2,256,256]{2,1,0:T(8,128)}, u32[]{:S(2)}) copy-start(f32[2,256,256]{2,1,0:T(8,128)} %refs_7_.3) | copy-start | bytes 1572868
  88.3 47.9 %copy-start.10 = (f32[2,256,256]{2,1,0:T(8,128)S(1)}, f32[2,256,256]{2,1,0:T(8,128)}, u32[]{:S(2)}) copy-start(f32[2,256,256]{2,1,0:T(8,128)} %refs_8_.1) | copy-start | bytes 1572868
  88.3 47.9 %copy-start.11 = (f32[2,256,256]{2,1,0:T(8,128)S(1)}, f32[2,256,256]{2,1,0:T(8,128)}, u32[]{:S(2)}) copy-start(f32[2,256,256]{2,1,0:T(8,128)} %refs_9_.3) | copy-start | bytes 1572868
  88.3 47.9 %copy-start.12 = (f32[2,256,256]{2,1,0:T(8,128)S(1)}, f32[2,256,256]{2,1,0:T(8,128)}, u32[]{:S(2)}) copy-start(f32[2,256,256]{2,1,0:T(8,128)} %refs_12_.1) | copy-start | bytes 1572868
  88.4 47.9 %copy-start.13 = (f32[2,256,256]{2,1,0:T(8,128)S(1)}, f32[2,256,256]{2,1,0:T(8,128)}, u32[]{:S(2)}) copy-start(f32[2,256,256]{2,1,0:T(8,128)} %refs_14_.1) | copy-start | bytes 1572868
  88.4 47.9 %copy-start.14 = (f32[2,172,172]{2,0,1:T(2,128)S(1)}, f32[2,172,172]{2,0,1:T(2,128)}, u32[]{:S(2)}) copy-start(f32[2,172,172]{2,0,1:T(2,128)} %param.51) | copy-start | bytes 710020
  88.4 47.9 %copy-start.15 = (f32[2,172,172]{2,0,1:T(2,128)S(1)}, f32[2,172,172]{2,0,1:T(2,128)}, u32[]{:S(2)}) copy-start(f32[2,172,172]{2,0,1:T(2,128)} %param.57) | copy-start | bytes 710020
  88.4 47.9 %copy-start.16 = (f32[2,128,128]{2,1,0:T(8,128)S(1)}, f32[2,128,128]{2,1,0:T(8,128)}, u32[]{:S(2)}) copy-start(f32[2,128,128]{2,1,0:T(8,128)} %refs_1_.1) | copy-start | bytes 393220
  88.4 47.9 %copy-start.17 = (f32[2,128,128]{2,1,0:T(8,128)S(1)}, f32[2,128,128]{2,1,0:T(8,128)}, u32[]{:S(2)}) copy-start(f32[2,128,128]{2,1,0:T(8,128)} %refs_3_.1) | copy-start | bytes 393220
  88.4 47.9 %copy-start.21 = (f32[684]{0:T(1024)S(1)}, f32[684]{0:T(1024)}, u32[]{:S(2)}) copy-start(f32[684]{0:T(1024)} %moment_one.1) | copy-start | bytes 8212
  88.4 47.9 %copy-start.22 = (f32[684]{0:T(1024)S(1)}, f32[684]{0:T(1024)}, u32[]{:S(2)}) copy-start(f32[684]{0:T(1024)} %moment_two.1) | copy-start | bytes 8212
  95.7 2.5 %collective-permute-start = (bf16[1152,128]{1,0:T(8,128)(2,1)S(1)}, bf16[1152,128]{1,0:T(8,128)(2,1)S(1)}, u32[]{:S(2)}, u32[]{:S(2)}) collective-permute-start(bf16[1152,128]{1,0:T(8,128)(2,1)S(1)} %get-tuple-element.59), channel_id=1, source_target_pairs={{0,8},{8,0},{1,9},{9,1},{2,10},{10,2},{3,11},{11,3},{4,12},{12,4},... | collective-permute-start | bytes 884744 | tf_op jit(solution)/shard_map/ppermute | solution.py:1099
  134.6 1.6 %collective-permute-start.1 = (bf16[1152,128]{1,0:T(8,128)(2,1)S(1)}, bf16[1152,128]{1,0:T(8,128)(2,1)S(1)}, u32[]{:S(2)}, u32[]{:S(2)}) collective-permute-start(bf16[1152,128]{1,0:T(8,128)(2,1)S(1)} %bitcast.30), channel_id=1, source_target_pairs={{0,8},{8,0},{1,9},{9,1},{2,10},{10,2},{3,11},{11,3},{4,12},{12,4},... | collective-permute-start | bytes 884744 | tf_op jit(solution)/shard_map/ppermute | solution.py:1105
